TPU v7x, 256 devices: a whole 4x4x8 slice. The times are simulated.
256 devices in a mesh: ctx: 16 (over z, core), exp: 16 (over x, y).
Axes of the slice: x: 4, y: 4, z: 8, core: 2. Of those that a mesh axis runs over, the one named last changes fastest.
Arguments:
- queries: bfloat16 [2, 16384, 2560], P(None, ('ctx', 'exp'))
- key_states: bfloat16 [2, 16384, 512], P(None, ('ctx', 'exp'))
- value_state_rows: bfloat16 [2, 16384, 512], P(None, ('ctx', 'exp')), may hold values from -6 to 6
- block_lists: int32 [32], replicated, may hold values from 0 to 31, as said below
- hidden: bfloat16 [8192, 5120], P(('ctx', 'exp')), may hold values from -8 to 8
- router: bfloat16 [5120, 16], replicated, may hold values from -0.078125 to 0.078125
- expert_ids: int32 [8192, 1], P(('ctx', 'exp')), may hold values from 0 to 15; in each aligned block of 32 rows (0 to 31, 32 to 63, ...) at most 4 rows name the same one
- w_gate: bfloat16 [16, 5120, 4096], P('exp', None, 'ctx'), may hold values from -0.078125 to 0.078125
- w_up: bfloat16 [16, 5120, 4096], P('exp', None, 'ctx'), may hold values from -0.078125 to 0.078125
- w_down: bfloat16 [16, 4096, 5120], P('exp', 'ctx'), may hold values from -0.1875 to 0.1875
Outputs:
- attention: bfloat16 [2, 16384, 2560], P(None, ('ctx', 'exp'))
- moe_out: bfloat16 [8192, 5120], P(('ctx', 'exp'))
Inputs may be any that keep to these rules, and one draw needn't show every extreme that they name: block_lists[b] is a block before b, or b itself when block b attends only to its own keys (always for b = 0 and for b = 31). Block p is held by index min(p, 31 - p) of ctx; for each d < 16 with block_lists[d] != d and block_lists[31 - d] != 31 - d, the two listed blocks are held by different indices. `expert_ids`: among the rows of one device no expert is named more than 4 times.
All inputs are finite; a program needn't handle non-finite values.
Results may differ from a plain program's by a relative error of at most 0.023.
Values may be sent and summed in bfloat16 or wider, within the bound.
No kernel may reach another device: no remote copies, remote signals or barrier semaphores. Data moves between devices by JAX's collectives and lax.ppermute only.
A program may use at most 128 MiB of HBM per device.

v0:
```python
import jax
import jax.numpy as jnp
from jax import lax
from jax.sharding import PartitionSpec as P

QUERY_HEADS = 20
KEY_HEADS = 4
HEAD_DIM = 128


NEGATIVE_LARGE = -1e30


def attend_all(queries, key_states, value_state_rows, block_lists):
    ctx_count = lax.axis_size("ctx")
    blocks_total = 2 * ctx_count
    ctx_index = lax.axis_index("ctx")
    exp_index = lax.axis_index("exp")
    row_total_count = queries.shape[1]
    query_group_width = QUERY_HEADS // KEY_HEADS
    key_value_width = KEY_HEADS * HEAD_DIM
    paired = jnp.concatenate([key_states, value_state_rows], axis=2)
    own_blocks = jnp.stack([ctx_index, blocks_total - 1 - ctx_index])
    listed = block_lists[own_blocks]
    usable = listed != own_blocks
    holder = jnp.minimum(listed, blocks_total - 1 - listed)
    everyone = lax.all_gather(paired[None], "ctx", axis=0, tiled=True)
    second_half = (listed >= ctx_count).astype(jnp.int32)
    remote = everyone[holder, second_half]
    stacked = jnp.concatenate([paired, remote], axis=0)
    query_head_rows = queries.reshape(2, row_total_count, KEY_HEADS, query_group_width, HEAD_DIM)
    query_pos = exp_index * row_total_count + jnp.arange(row_total_count)
    scaling = HEAD_DIM ** (-0.5)
    piece_rows = lax.all_gather(stacked, "exp", axis=1, tiled=True)
    running_maximum = jnp.full(
        (2, KEY_HEADS, query_group_width, row_total_count), NEGATIVE_LARGE, jnp.float32
    )
    key_total_count = piece_rows.shape[1]
    concatenated_rows = jnp.concatenate([piece_rows[0:2], piece_rows[2:4]], axis=1)
    key_portion = concatenated_rows[..., :key_value_width].reshape(
        2, 2 * key_total_count, KEY_HEADS, HEAD_DIM
    )
    value_portion = concatenated_rows[..., key_value_width:].reshape(
        2, 2 * key_total_count, KEY_HEADS, HEAD_DIM
    )
    scores = (
        jnp.einsum(
            "prhgd,pkhd->phgrk", query_head_rows, key_portion, preferred_element_type=jnp.float32
        )
        * scaling
    )
    key_pos = jnp.arange(key_total_count)
    causal = jnp.broadcast_to(
        (key_pos[None, :] <= query_pos[:, None])[None], (2, row_total_count, key_total_count)
    )
    listed_ok = jnp.broadcast_to(usable[:, None, None], (2, row_total_count, key_total_count))
    allowed = jnp.concatenate([causal, listed_ok], axis=2)[:, None, None]
    masked = jnp.where(allowed, scores, NEGATIVE_LARGE)
    new_max = jnp.maximum(running_maximum, jnp.max(masked, axis=-1))
    weights = jnp.where(allowed, jnp.exp(masked - new_max[..., None]), 0.0)
    new_sum = jnp.sum(weights, axis=-1)
    update = jnp.einsum(
        "phgrk,pkhd->phgrd",
        weights.astype(jnp.bfloat16),
        value_portion,
        preferred_element_type=jnp.float32,
    )
    mixed_rows = update / new_sum[..., None]
    return (
        jnp.transpose(mixed_rows, (0, 3, 1, 2, 4))
        .reshape(2, row_total_count, QUERY_HEADS * HEAD_DIM)
        .astype(jnp.bfloat16)
    )


def route_experts(hidden, router, expert_ids, w_gate, w_up, w_down):
    expert_table = router.shape[1]
    local_tokens = hidden.shape[0]
    model_width = hidden.shape[1]
    capacity = max(2, 2 * local_tokens // expert_table)
    exp_count = lax.axis_size("exp")
    logits = jnp.dot(hidden, router, preferred_element_type=jnp.float32)
    selected_expert = expert_ids[:, 0]
    onehot = (selected_expert[:, None] == jnp.arange(expert_table)[None, :]).astype(jnp.float32)
    gate_score = jax.nn.sigmoid(jnp.sum(logits * onehot, axis=1))
    scaled_scores = (hidden.astype(jnp.float32) * gate_score[:, None]).astype(jnp.bfloat16)
    slot_rank = (jnp.sum(jnp.cumsum(onehot, axis=0) * onehot, axis=1) - 1.0).astype(jnp.int32)
    dispatch = (
        (selected_expert[None, None, :] == jnp.arange(expert_table)[:, None, None])
        & (slot_rank[None, None, :] == jnp.arange(capacity)[None, :, None])
    ).astype(jnp.bfloat16)
    gate_local = w_gate[0]
    up_local = w_up[0]
    down_local = w_down[0]
    outgoing = jnp.einsum(
        "ect,td->ecd", dispatch, scaled_scores, preferred_element_type=jnp.float32
    ).astype(jnp.bfloat16)
    incoming = lax.all_to_all(outgoing, "exp", split_axis=0, concat_axis=0, tiled=True)
    piece_rows = lax.all_gather(incoming.reshape(-1, model_width), "ctx", axis=0, tiled=True)
    gate_part = jnp.dot(piece_rows, gate_local, preferred_element_type=jnp.float32)
    up_part = jnp.dot(piece_rows, up_local, preferred_element_type=jnp.float32)
    hidden_activation = (jax.nn.silu(gate_part) * up_part).astype(jnp.bfloat16)
    summed_output = lax.psum_scatter(
        jnp.dot(hidden_activation, down_local, preferred_element_type=jnp.float32).astype(
            jnp.bfloat16
        ),
        "ctx",
        scatter_dimension=0,
        tiled=True,
    )
    returned = lax.all_to_all(
        summed_output.reshape(exp_count, capacity, model_width),
        "exp",
        split_axis=0,
        concat_axis=0,
        tiled=True,
    )
    return jnp.einsum("ect,ecd->td", dispatch, returned, preferred_element_type=jnp.float32).astype(
        jnp.bfloat16
    )


def shards(
    queries,
    key_states,
    value_state_rows,
    block_lists,
    hidden,
    router,
    expert_ids,
    w_gate,
    w_up,
    w_down,
):
    attention = attend_all(queries, key_states, value_state_rows, block_lists)
    moe_out = route_experts(hidden, router, expert_ids, w_gate, w_up, w_down)
    return (attention, moe_out)


def solution(mesh):
    placed = (
        P(None, ("ctx", "exp"), None),
        P(None, ("ctx", "exp"), None),
        P(None, ("ctx", "exp"), None),
        P(),
        P(("ctx", "exp"), None),
        P(),
        P(("ctx", "exp"), None),
        P("exp", None, "ctx"),
        P("exp", None, "ctx"),
        P("exp", "ctx", None),
    )
    return jax.shard_map(
        shards,
        mesh=mesh,
        in_specs=placed,
        out_specs=(P(None, ("ctx", "exp"), None), P(("ctx", "exp"), None)),
        check_vma=False,
    )
```

profile of v0, /device:TPU:2, one launch (start us, length us, event | category | flops | bytes accessed | tf_op | source)
XLA Modules:
  0.0 308.0 jit_solution(14980662462300857561)
XLA Ops:
  7.2 1.1 constant_dynamic-update-slice_fusion.1
  11.5 1.3 fusion.24
  13.5 1.4 convolution_convert_fusion.1
  15.4 18.6 %all_to_all.10 = bf16[16,4,5120]{2,1,0:T(4,128)(2,1)S(1)} all-to-all(bf16[16,4,5120]{2,1,0:T(4,128)(2,1)S(1)} %copy.30), channel_id=1, replica_groups=mesh['ctx'=16,'exp'=16] {'exp'}, dimensions={0} | all-to-all | bytes 1310720 | tf_op jit(solution)/shard_map/all_to_all | solution.py:98
  35.2 1.3 gather_fusion
  36.5 19.3 %all-gather.9.cloned.1.call-done = bf16[32,64,1024]{2,1,0:T(8,128)(2,1)} async-done(((bf16[2,64,1024]{2,1,0:T(8,128)(2,1)}), bf16[32,64,1024]{2,1,0:T(8,128)(2,1)}) %all-gather.9.cloned.1.call-update) | async-done | bytes 4194320 | tf_op jit(solution)/shard_map/all_gather | solution.py:27
  55.8 2.8 gather_fusion.1
  58.5 1.8 pad_maximum_fusion.1
  60.4 61.9 %all-gather.7.cloned.1.call-done = bf16[1024,5120]{1,0:T(8,128)(2,1)} async-done(((bf16[64,5120]{1,0:T(8,128)(2,1)}), bf16[1024,5120]{1,0:T(8,128)(2,1)}) %all-gather.7.cloned.1.call-update) | async-done | bytes 10485776 | tf_op jit(solution)/shard_map/all_gather | solution.py:99
  122.3 8.6 %fusion.11 = f32[1024,256]{1,0:T(8,128)} fusion(bf16[1024,5120]{1,0:T(8,128)(2,1)} %all-gather.7.cloned.1.call-done, bf16[1,5120,256]{2,1,0:T(8,128)(2,1)} %param.17), kind=kOutput, calls=%fused_computation.20 | convolution fusion | flops 2684354560 | bytes 14155776 | tf_op jit(solution)/shard_map/dot_general | solution.py:100
  130.9 21.1 %convolution_convert_fusion = bf16[1024,5120]{1,0:T(8,128)(2,1)} fusion(bf16[1,256,5120]{2,1,0:T(8,128)(2,1)S(1)} %copy-done, bf16[1024,5120]{1,0:T(8,128)(2,1)} %all-gather.7.cloned.1.call-done, bf16[1,5120,256]{2,1,0:T(8,128)(2,1)} %param.18, f32[1024,256]{1,0:T(8,128)} %fusion.11), kind=kOutput, calls=%fused_computation.9 | convolution fusion | flops 5375524864 | bytes 27262976 | tf_op jit(solution)/shard_map/dot_general | solution.py:104
  154.2 44.9 %all-gather.5.cloned.1.call-done = bf16[4,1024,1024]{2,1,0:T(8,128)(2,1)} async-done(((bf16[4,64,1024]{2,1,0:T(8,128)(2,1)}), bf16[4,1024,1024]{2,1,0:T(8,128)(2,1)}) %all-gather.5.cloned.1.call-update) | async-done | bytes 8388624 | tf_op jit(solution)/shard_map/all_gather | solution.py:34
  199.1 3.9 %fusion.57 = (bf16[2,1024,1024]{2,1,0:T(8,128)(2,1)S(1)}, bf16[2,1024,1024]{2,1,0:T(8,128)(2,1)S(1)}) fusion(bf16[4,1024,1024]{2,1,0:T(8,128)(2,1)} %all-gather.5.cloned.1.call-done), kind=kLoop, calls=%fused_computation.78 | loop fusion | bytes 16777216 | tf_op jit(solution)/shard_map/slice | solution.py:39
  203.1 3.7 %fusion.7 = (bf16[2,2048,512]{2,1,0:T(8,128)(2,1)}, bf16[2,2048,512]{2,1,0:T(8,128)(2,1)}) fusion(bf16[2,1024,1024]{2,1,0:T(8,128)(2,1)S(1)} %get-tuple-element.4, bf16[2,1024,1024]{2,1,0:T(8,128)(2,1)S(1)} %get-tuple-element.5), kind=kLoop, calls=%fused_computation.15 | loop fusion | flops 16777216 | bytes 16777216 | tf_op jit(solution)/shard_map/concatenate | solution.py:39
  206.8 6.3 %copy.25 = bf16[2,2048,512]{1,2,0:T(8,128)(2,1)} copy(bf16[2,2048,512]{2,1,0:T(8,128)(2,1)} %get-tuple-element.3) | data formatting | bytes 8388608 | tf_op jit(solution)/shard_map/slice | solution.py:43
  213.1 6.3 %copy.22 = bf16[2,2048,512]{1,2,0:T(8,128)(2,1)} copy(bf16[2,2048,512]{2,1,0:T(8,128)(2,1)} %get-tuple-element.2) | data formatting | bytes 8388608 | tf_op jit(solution)/shard_map/slice | solution.py:40
  219.4 13.4 %fusion = (f32[2,4,5,64]{3,2,1,0:T(8,128)S(1)}, f32[2,4,2048,64,5]{2,3,4,1,0:T(8,128)}) fusion(pred[2,64,2048]{2,1,0:T(8,128)(4,1)S(1)} %pad_add_fusion, bf16[2,2048,4,128,1]{1,3,4,2,0:T(8,128)(2,1)} %bitcast.70, bf16[2,64,4,5,128]{4,3,2,1,0:T(8,128)(2,1)S(1)} %reshape.250), kind=kOutput, calls=%fused_computation.4 | convolution fusion | flops 1357903360 | bytes 26093568 | tf_op jit(solution)/shard_map/prhgd,pkhd->phgrk/dot_general | solution.py:47
  232.9 11.6 %fusion.1 = f32[2,4,5,64]{3,2,1,0:T(8,128)} fusion(f32[2,4,2048,64,5]{2,3,4,1,0:T(8,128)} %get-tuple-element.7, f32[2,4,5,64]{3,2,1,0:T(8,128)S(1)} %broadcast_maximum_fusion, pred[2,64,2048]{2,1,0:T(8,128)(4,1)S(1)} %pad_add_fusion), kind=kLoop, calls=%fused_computation.5 | loop fusion | flops 26211840 | bytes 21254144 | tf_op jit(solution)/shard_map/reduce_sum | solution.py:61
  244.5 31.3 %reduce-scatter.2.cloned.1.call-done = bf16[64,5120]{1,0:T(8,128)(2,1)} async-done(((bf16[1024,5120]{1,0:T(8,128)(2,1)}), bf16[64,5120]{1,0:T(8,128)(2,1)}) %reduce-scatter.2.cloned.1.call-update) | async-done | bytes 655376 | tf_op jit(solution)/shard_map/reduce_scatter | solution.py:103
  275.8 2.4 reshape.253
  278.2 7.4 %all-to-all-start.1 = ((bf16[16,4,5120]{2,1,0:T(4,128)(2,1)}), bf16[16,4,5120]{2,1,0:T(4,128)(2,1)S(1)}, u32[]{:S(2)}, u32[]{:S(2)}) async-start(bf16[16,4,5120]{2,1,0:T(4,128)(2,1)} %reshape.253), calls=%async_computation.2 | async-start | bytes 1310720 | tf_op jit(solution)/shard_map/all_to_all | solution.py:111
  285.5 10.9 %divide_convert_fusion = bf16[2,64,4,5,128]{4,1,3,2,0:T(8,128)(2,1)S(1)} fusion(bf16[2,2048,4,128,1]{1,3,4,2,0:T(8,128)(2,1)} %bitcast.71, f32[2,4,2048,64,5]{2,3,4,1,0:T(8,128)} %get-tuple-element.7, f32[2,4,5,64]{3,2,1,0:T(8,128)} %copy-done.4, pred[2,64,2048]{2,1,0:T(8,128)(4,1)S(1)} %pad_add_fusion, f32[2,64,4,5]{1,3,2,0:T(8,128)} %bitcast.72), kind=kOutput, calls=%fused_computation.23 | convolution fusion | flops 1369047040 | bytes 26103808 | tf_op jit(solution)/shard_map/phgrk,pkhd->phgrd/dot_general | solution.py:62
  296.4 1.4 copy.27
  297.9 2.6 convert_element_type.51
  (43 shorter events, 8.9 us)
Async XLA Ops:
  7.2 123.7 %copy-start = (bf16[1,256,5120]{2,1,0:T(8,128)(2,1)S(1)}, bf16[1,256,5120]{2,1,0:T(8,128)(2,1)}, u32[]{:S(2)}) copy-start(bf16[1,256,5120]{2,1,0:T(8,128)(2,1)} %param.19) | copy-start | bytes 7864324
  7.2 48.6 %all-gather.9.cloned.1.call-start = ((), (), s32[]{:S(2)}) async-start(), calls=%async_computation.6 | async-start | bytes 4456448 | tf_op jit(solution)/shard_map/all_gather | solution.py:27
  9.2 0.7 copy-start.2
  9.9 112.4 %all-gather.7.cloned.1.call-start = ((), (), s32[]{:S(2)}) async-start(), calls=%async_computation.4 | async-start | bytes 11141120 | tf_op jit(solution)/shard_map/all_gather | solution.py:99
  35.0 164.1 %all-gather.5.cloned.1.call-start = ((), (), s32[]{:S(2)}) async-start(), calls=%async_computation.3 | async-start | bytes 8912896 | tf_op jit(solution)/shard_map/all_gather | solution.py:34
  60.3 215.5 %reduce-scatter.2.cloned.1.call-start = ((), (), s32[]{:S(2)}) async-start(), calls=%async_computation.5 | async-start | bytes 11141120 | tf_op jit(solution)/shard_map/reduce_scatter | solution.py:103
  152.0 1.1 copy-start.3
  232.9 11.6 %copy-start.4 = (f32[2,4,5,64]{3,2,1,0:T(8,128)}, f32[2,4,5,64]{3,2,1,0:T(8,128)S(1)}, u32[]{:S(2)}) copy-start(f32[2,4,5,64]{3,2,1,0:T(8,128)S(1)} %broadcast_maximum_fusion) | copy-start | bytes 30724
  278.2 22.3 %all-to-all-start.1 = ((bf16[16,4,5120]{2,1,0:T(4,128)(2,1)}), bf16[16,4,5120]{2,1,0:T(4,128)(2,1)S(1)}, u32[]{:S(2)}, u32[]{:S(2)}) async-start(bf16[16,4,5120]{2,1,0:T(4,128)(2,1)} %reshape.253), calls=%async_computation.2 | async-start | bytes 1310720 | tf_op jit(solution)/shard_map/all_to_all | solution.py:111
  285.5 15.9 %copy-start.1 = (bf16[1,256,5120]{2,1,0:T(8,128)(2,1)S(1)}, bf16[1,256,5120]{2,1,0:T(8,128)(2,1)}, u32[]{:S(2)}) copy-start(bf16[1,256,5120]{2,1,0:T(8,128)(2,1)} %param.19) | copy-start | bytes 7864324
Sparse Core Ops, SparseCore 0:
  10.4 45.3 all-gather.8
  58.2 64.0 all-gather.6
  124.8 74.2 all-gather.4
  201.5 74.1 reduce-scatter.1
where the time goes:
time: 309 us; the launch traced here: 308 us
  waiting for transfers between devices  157 us (51%)
  matrix products  57.7 us (19%)
  local copies, waits for them, and re-layouts  33.3 us (11%)
  other arithmetic  19.5 us (6%)
  blocking collectives  18.6 us (6%)
  between operations  13.9 us (4%)
  starting transfers between devices  7.54 us (2%)
    all_gather x1, waiting for transfers between devices, route_experts(): lax.all_gather(incoming.reshape(-1, model_width), 'ctx', axis=0, tiled=True)  61.9 us
    all_gather x1, waiting for transfers between devices, attend_all(): piece_rows = lax.all_gather(stacked, 'exp', axis=1, tiled=True)  44.9 us
    reduce_scatter x1, waiting for transfers between devices, route_experts(): lax.psum_scatter(jnp.dot(hidden_activation, down_local, preferred_element...  31.3 us
    dot_general x1, matrix products, route_experts(): jnp.dot(hidden_activation, down_local, preferred_element_type=jnp.float32)  21.1 us
    all_gather x1, waiting for transfers between devices, attend_all(): everyone = lax.all_gather(paired[None], 'ctx', axis=0, tiled=True)  19.3 us
    all_to_all x1, blocking collectives, route_experts(): lax.all_to_all(outgoing, 'exp', split_axis=0, concat_axis=0, tiled=True)  18.6 us
    dot_general x1, matrix products, attend_all(): jnp.einsum('prhgd,pkhd->phgrk', query_head_rows, key_portion, preferred_e...  13.4 us
    reduce_sum x1, other arithmetic, attend_all(): new_sum = jnp.sum(weights, axis=-1)  11.6 us
  transfers between devices with their start and end apart: 5, of which 4 were waited for; matrix products, arithmetic and copies ran while one was open for 34% of the time, Pallas kernels for 0%

commit v1 on v0

v1 whole, which is shorter than its diff:
```python
import jax
import jax.numpy as jnp
from jax import lax
from jax.experimental import pallas as pl
from jax.experimental.pallas import tpu as pltpu
from jax.sharding import PartitionSpec as P

HEAD_DIM = 128
NEGATIVE_LARGE = -1e30
SIDE = 4
RINGS = [[2 * z + c for z in range(8)] for c in range(2)]
CORE_SWAP = [(i, i ^ 1) for i in range(16)]


def shift_x(d):
    return [(4 * a + b, 4 * ((a + d) % 4) + b) for a in range(4) for b in range(4)]


def shift_y(d):
    return [(4 * a + b, 4 * a + (b + d) % 4) for a in range(4) for b in range(4)]


def ordinary(vmem=48):
    return pltpu.CompilerParams(
        dimension_semantics=("arbitrary",), vmem_limit_bytes=vmem * 1024 * 1024
    )


def pick_kernel(table, source, *outs):
    x = table[4]
    for d in range(SIDE):
        h = lax.rem(x + d, SIDE)
        outs[d][0] = source[0, :, pl.ds(pl.multiple_of(h * 256, 256), 256)]


def pick_heads(everyone, table):
    rows, width = everyone.shape[1], everyone.shape[2]
    part = jax.ShapeDtypeStruct((4, rows, 256), everyone.dtype)
    return pl.pallas_call(
        pick_kernel,
        grid_spec=pltpu.PrefetchScalarGridSpec(
            num_scalar_prefetch=1,
            grid=(4,),
            in_specs=[pl.BlockSpec((1, rows, width), lambda i, t: (t[i], 0, 0))],
            out_specs=[pl.BlockSpec((1, rows, 256), lambda i, t: (i, 0, 0))] * SIDE,
        ),
        out_shape=[part] * SIDE,
        compiler_params=ordinary(16),
        cost_estimate=pl.CostEstimate(flops=0, bytes_accessed=2 << 20, transcendentals=0),
        name="pick_heads",
    )(table, everyone)


def split_kernel(where, source, *outs):
    x = where[0]
    width = outs[0].shape[2]
    for d in range(SIDE):
        h = lax.rem(x + d, SIDE)
        outs[d][...] = source[:, :, pl.ds(pl.multiple_of(h * width, 128), width)]


def split_queries(queries, where):
    part = jax.ShapeDtypeStruct(queries.shape[:2] + (queries.shape[2] // SIDE,), queries.dtype)
    return pl.pallas_call(
        split_kernel,
        grid_spec=pltpu.PrefetchScalarGridSpec(
            num_scalar_prefetch=1,
            grid=(1,),
            in_specs=[pl.BlockSpec(queries.shape, lambda i, t: (0, 0, 0))],
            out_specs=[pl.BlockSpec(part.shape, lambda i, t: (0, 0, 0))] * SIDE,
        ),
        out_shape=[part] * SIDE,
        compiler_params=ordinary(16),
        cost_estimate=pl.CostEstimate(flops=0, bytes_accessed=1310720, transcendentals=0),
        name="split_queries",
    )(where, queries)


def stack_kernel(where, *refs):
    x = where[0]
    out = refs[SIDE]
    for d in range(SIDE):
        out[lax.rem(x + SIDE - d, SIDE)] = refs[d][...]


def stack_sources(parts, where):
    shape = parts[0].shape
    zeros = (0,) * len(shape)
    return pl.pallas_call(
        stack_kernel,
        grid_spec=pltpu.PrefetchScalarGridSpec(
            num_scalar_prefetch=1,
            grid=(1,),
            in_specs=[pl.BlockSpec(shape, lambda i, t: zeros)] * SIDE,
            out_specs=pl.BlockSpec((SIDE,) + shape, lambda i, t: (0,) + zeros),
        ),
        out_shape=jax.ShapeDtypeStruct((SIDE,) + shape, parts[0].dtype),
        compiler_params=ordinary(16),
        cost_estimate=pl.CostEstimate(flops=0, bytes_accessed=1 << 20, transcendentals=0),
        name="stack_sources",
    )(where, *parts)


def join_kernel(where, *refs):
    x = where[0]
    out = refs[SIDE]
    width = refs[0].shape[2]
    for d in range(SIDE):
        h = lax.rem(x + d, SIDE)
        out[:, :, pl.ds(pl.multiple_of(h * width, 128), width)] = refs[d][...]


def join_heads(parts, where):
    shape = parts[0].shape
    full = shape[:2] + (shape[2] * SIDE,)
    return pl.pallas_call(
        join_kernel,
        grid_spec=pltpu.PrefetchScalarGridSpec(
            num_scalar_prefetch=1,
            grid=(1,),
            in_specs=[pl.BlockSpec(shape, lambda i, t: (0, 0, 0))] * SIDE,
            out_specs=pl.BlockSpec(full, lambda i, t: (0, 0, 0)),
        ),
        out_shape=jax.ShapeDtypeStruct(full, parts[0].dtype),
        compiler_params=ordinary(16),
        cost_estimate=pl.CostEstimate(flops=0, bytes_accessed=1310720, transcendentals=0),
        name="join_heads",
    )(where, *parts)


NT = (((1,), (1,)), ((), ()))


def attend_kernel(where, q0, q1, q2, q3, r0, r1, r2, r3a, r3b, o0, o1, o2, o3, kown, vown, klist, vlist, qall, oall):
    p = pl.program_id(0)
    x, y, usable = where[0], where[1], where[2 + p]
    pieces = (r0, r1, r2)
    for xs in range(SIDE):
        last = r3a if xs < 2 else r3b
        for turn in range(SIDE):
            piece = pieces[turn][xs] if turn < 3 else last[xs % 2]
            at = pl.ds(xs * 256 + turn * 64, 64)
            kown[at, :] = piece[0, 0, :, :HEAD_DIM]
            vown[at, :] = piece[0, 0, :, HEAD_DIM:]
            klist[at, :] = piece[1, 0, :, :HEAD_DIM]
            vlist[at, :] = piece[1, 0, :, HEAD_DIM:]
    scaling = HEAD_DIM ** (-0.5)
    group = q0.shape[2] // HEAD_DIM
    rows = 64 * group
    qs, outs = (q0, q1, q2, q3), (o0, o1, o2, o3)
    query_row = lax.rem(lax.broadcasted_iota(jnp.int32, (rows, 256), 0), 64)
    key_index = lax.broadcasted_iota(jnp.int32, (rows, 256), 1)
    turn = key_index // 64
    behind = jnp.where(turn == 0, 0, jnp.where(turn == 1, 3, jnp.where(turn == 2, 1, 2)))
    key_pos = lax.rem(y + behind, SIDE) * 64 + lax.rem(key_index, 64)
    diagonal = key_pos <= y * 64 + query_row
    for d in range(SIDE):
        qall[lax.rem(x + SIDE - d, SIDE)] = qs[d][0]
    for case in range(SIDE):
        query = jnp.concatenate(
            [qall[case, :, g * HEAD_DIM : (g + 1) * HEAD_DIM] for g in range(group)], axis=0
        )
        before = case * 256
        own = lax.dot_general(
            query, kown[pl.ds(before, 256), :], NT, preferred_element_type=jnp.float32
        )
        own = jnp.where(diagonal, own * scaling, NEGATIVE_LARGE)
        far = lax.dot_general(query, klist[...], NT, preferred_element_type=jnp.float32)
        far = jnp.where(usable > 0, far * scaling, NEGATIVE_LARGE)
        top = jnp.maximum(jnp.max(own, axis=1, keepdims=True), jnp.max(far, axis=1, keepdims=True))
        if case:
            near = lax.dot_general(
                query, kown[pl.ds(0, before), :], NT, preferred_element_type=jnp.float32
            )
            near = near * scaling
            top = jnp.maximum(top, jnp.max(near, axis=1, keepdims=True))
        own = jnp.exp(own - top)
        far = jnp.exp(far - top)
        total = jnp.sum(own, axis=1, keepdims=True) + jnp.sum(far, axis=1, keepdims=True)
        mixed = jnp.dot(
            own.astype(jnp.bfloat16), vown[pl.ds(before, 256), :], preferred_element_type=jnp.float32
        ) + jnp.dot(far.astype(jnp.bfloat16), vlist[...], preferred_element_type=jnp.float32)
        if case:
            near = jnp.exp(near - top)
            total = total + jnp.sum(near, axis=1, keepdims=True)
            mixed = mixed + jnp.dot(
                near.astype(jnp.bfloat16),
                vown[pl.ds(0, before), :],
                preferred_element_type=jnp.float32,
            )
        mixed = (mixed / total).astype(jnp.bfloat16)
        for g in range(group):
            oall[case, :, g * HEAD_DIM : (g + 1) * HEAD_DIM] = mixed[g * 64 : (g + 1) * 64]
    for d in range(SIDE):
        outs[d][0] = oall[lax.rem(x + SIDE - d, SIDE)]


def attend(where, qs, rs):
    qspec = pl.BlockSpec((1,) + qs[0].shape[1:], lambda i, t: (i, 0, 0))

    def rspec(r):
        return pl.BlockSpec((r.shape[0], 2, 1) + r.shape[3:], lambda i, t: (0, 0, i, 0, 0))

    return pl.pallas_call(
        attend_kernel,
        grid_spec=pltpu.PrefetchScalarGridSpec(
            num_scalar_prefetch=1,
            grid=(2,),
            in_specs=[qspec] * SIDE + [rspec(r) for r in rs],
            out_specs=[qspec] * SIDE,
            scratch_shapes=[pltpu.VMEM((1024, HEAD_DIM), jnp.bfloat16)] * 4
            + [pltpu.VMEM((SIDE,) + qs[0].shape[1:], jnp.bfloat16)] * 2,
        ),
        out_shape=[jax.ShapeDtypeStruct(q.shape, q.dtype) for q in qs],
        compiler_params=ordinary(40),
        cost_estimate=pl.CostEstimate(
            flops=2200000000, bytes_accessed=4 << 20, transcendentals=4300000
        ),
        name="attend",
    )(where, *qs, *rs)


def attend_all(queries, key_states, value_state_rows, block_lists):
    ctx_count = lax.axis_size("ctx")
    blocks_total = 2 * ctx_count
    ctx_index = lax.axis_index("ctx")
    exp_index = lax.axis_index("exp")
    x, y = exp_index // SIDE, exp_index % SIDE
    where = jnp.stack([x, y]).astype(jnp.int32)
    heads = key_states.shape[2] // HEAD_DIM
    columns = []
    for h in range(heads):
        columns.append(key_states[:, :, h * HEAD_DIM : (h + 1) * HEAD_DIM])
        columns.append(value_state_rows[:, :, h * HEAD_DIM : (h + 1) * HEAD_DIM])
    paired = jnp.concatenate(columns, axis=2)
    everyone = lax.all_gather(paired, "ctx", axis=0, tiled=True)
    own_blocks = jnp.stack([ctx_index, blocks_total - 1 - ctx_index])
    listed = block_lists[own_blocks]
    usable = (listed != own_blocks).astype(jnp.int32)
    wanted = jnp.concatenate([own_blocks, listed])
    holder = jnp.minimum(wanted, blocks_total - 1 - wanted)
    row = 2 * holder + (wanted >= ctx_count).astype(jnp.int32)
    table = jnp.concatenate([row, x[None]]).astype(jnp.int32)

    mine = split_queries(queries, where)
    qs = [mine[0]] + [lax.ppermute(mine[d], "exp", shift_x(d)) for d in range(1, SIDE)]
    picked = pick_heads(everyone, table)
    received = [picked[0]] + [lax.ppermute(picked[d], "exp", shift_x(d)) for d in range(1, SIDE)]
    r0 = stack_sources(received, where)
    r1 = lax.ppermute(r0, "exp", shift_y(1))
    r2 = lax.ppermute(r0, "exp", shift_y(-1))
    r3a = lax.ppermute(r1[:2], "exp", shift_y(1))
    r3b = lax.ppermute(r2[2:], "exp", shift_y(-1))
    rs = [r.reshape((r.shape[0], 2, 2) + r.shape[2:]) for r in (r0, r1, r2, r3a, r3b)]
    outs = attend(jnp.concatenate([where, usable]), qs, rs)
    back = [outs[0]] + [lax.ppermute(outs[d], "exp", shift_x(-d)) for d in range(1, SIDE)]
    return join_heads(back, where)


def ffn_kernel(x_ref, g0, u0, d0, g1, u1, d1, o_ref, acc):
    i = pl.program_id(0)
    half = pl.num_programs(0) // 2

    def run(g, u, d):
        gate = jnp.dot(x_ref[...], g[...], preferred_element_type=jnp.float32)
        up = jnp.dot(x_ref[...], u[...], preferred_element_type=jnp.float32)
        act = (gate / (1.0 + jnp.exp(-gate)) * up).astype(jnp.bfloat16)
        return jnp.dot(act, d[...], preferred_element_type=jnp.float32)

    @pl.when(i == 0)
    def _():
        acc[...] = run(g0, u0, d0)

    @pl.when((i > 0) & (i < half))
    def _():
        acc[...] += run(g0, u0, d0)

    @pl.when((i >= half) & (i < 2 * half - 1))
    def _():
        acc[...] += run(g1, u1, d1)

    @pl.when(i == 2 * half - 1)
    def _():
        o_ref[...] = (acc[...] + run(g1, u1, d1)).astype(jnp.bfloat16)


def expert_rows(rows, weights):
    tokens, width = rows.shape
    hidden = weights[0].shape[1]
    block = 128
    steps = hidden // block
    first = lambda i: jnp.minimum(i, steps - 1)
    second = lambda i: jnp.maximum(i - steps, 0)
    specs = []
    for at in (first, second):
        specs.append(pl.BlockSpec((width, block), lambda i, at=at: (0, at(i))))
        specs.append(pl.BlockSpec((width, block), lambda i, at=at: (0, at(i))))
        specs.append(pl.BlockSpec((block, width), lambda i, at=at: (at(i), 0)))
    return pl.pallas_call(
        ffn_kernel,
        grid=(2 * steps,),
        in_specs=[pl.BlockSpec((tokens, width), lambda i: (0, 0), pipeline_mode=pl.Buffered(1))] + specs,
        out_specs=pl.BlockSpec((tokens, width), lambda i: (0, 0), pipeline_mode=pl.Buffered(1)),
        out_shape=jax.ShapeDtypeStruct((tokens, width), jnp.bfloat16),
        scratch_shapes=[pltpu.VMEM((tokens, width), jnp.float32)],
        compiler_params=ordinary(56),
        cost_estimate=pl.CostEstimate(
            flops=12 * tokens * width * hidden,
            bytes_accessed=12 * width * hidden + 4 * tokens * width,
            transcendentals=2 * tokens * hidden,
        ),
        name="expert_rows",
    )(rows, *weights)


def route_experts(hidden, router, expert_ids, w_gate, w_up, w_down):
    expert_table = router.shape[1]
    local_tokens = hidden.shape[0]
    model_width = hidden.shape[1]
    capacity = max(2, 2 * local_tokens // expert_table)
    exp_count = lax.axis_size("exp")
    own = (w_gate[0], w_up[0], w_down[0])
    other = tuple(lax.ppermute(w, "ctx", CORE_SWAP) for w in own)
    logits = jnp.dot(hidden, router, preferred_element_type=jnp.float32)
    selected_expert = expert_ids[:, 0]
    onehot = (selected_expert[:, None] == jnp.arange(expert_table)[None, :]).astype(jnp.float32)
    gate_score = jax.nn.sigmoid(jnp.sum(logits * onehot, axis=1))
    scaled_scores = (hidden.astype(jnp.float32) * gate_score[:, None]).astype(jnp.bfloat16)
    slot_rank = (jnp.sum(jnp.cumsum(onehot, axis=0) * onehot, axis=1) - 1.0).astype(jnp.int32)
    dispatch = (
        (selected_expert[None, None, :] == jnp.arange(expert_table)[:, None, None])
        & (slot_rank[None, None, :] == jnp.arange(capacity)[None, :, None])
    ).astype(jnp.bfloat16)
    outgoing = jnp.einsum(
        "ect,td->ecd", dispatch, scaled_scores, preferred_element_type=jnp.float32
    ).astype(jnp.bfloat16)
    incoming = lax.all_to_all(outgoing, "exp", split_axis=0, concat_axis=0, tiled=True)
    rows = lax.all_gather(
        incoming.reshape(-1, model_width), "ctx", axis=0, tiled=True, axis_index_groups=RINGS
    )
    partial = expert_rows(rows, own + other)
    summed_output = lax.psum_scatter(
        partial, "ctx", scatter_dimension=0, tiled=True, axis_index_groups=RINGS
    )
    returned = lax.all_to_all(
        summed_output.reshape(exp_count, capacity, model_width),
        "exp",
        split_axis=0,
        concat_axis=0,
        tiled=True,
    )
    return jnp.einsum("ect,ecd->td", dispatch, returned, preferred_element_type=jnp.float32).astype(
        jnp.bfloat16
    )


def shards(
    queries,
    key_states,
    value_state_rows,
    block_lists,
    hidden,
    router,
    expert_ids,
    w_gate,
    w_up,
    w_down,
):
    attention = attend_all(queries, key_states, value_state_rows, block_lists)
    moe_out = route_experts(hidden, router, expert_ids, w_gate, w_up, w_down)
    return (attention, moe_out)


def solution(mesh):
    placed = (
        P(None, ("ctx", "exp"), None),
        P(None, ("ctx", "exp"), None),
        P(None, ("ctx", "exp"), None),
        P(),
        P(("ctx", "exp"), None),
        P(),
        P(("ctx", "exp"), None),
        P("exp", None, "ctx"),
        P("exp", None, "ctx"),
        P("exp", "ctx", None),
    )
    return jax.shard_map(
        shards,
        mesh=mesh,
        in_specs=placed,
        out_specs=(P(None, ("ctx", "exp"), None), P(("ctx", "exp"), None)),
        check_vma=False,
    )
```

time: 309 us -> 250 us (0.81)
  matrix products: 57.7 us -> 4.72 us
  Pallas kernels: 0 us -> 37.3 us
  waiting for transfers between devices: 157 us -> 132 us
  local copies, waits for them, and re-layouts: 33.3 us -> 9.62 us
  starting transfers between devices: 7.54 us -> 28.7 us
  other arithmetic: 19.5 us -> 2.6 us
    all_gather x3 -> x2, waiting for transfers between devices: 126 us -> 68.3 us  [the longest x1 51.5 us: route_experts(): lax.all_gather(incoming.reshape(-1, model_width), 'ctx', axis=0, tiled=Tr...]
    dot_general x4 -> x0, matrix products: 54 us -> none  [the longest x1 21.1 us: route_experts(): jnp.dot(hidden_activation, down_local, preferred_element_type=jnp.float32)]
    pallas_call x0 -> x6, Pallas kernels: none -> 37.3 us  [the longest x1 24.7 us: expert_rows(): pl.pallas_call(ffn_kernel, grid=(2 * steps,), in_specs=[pl.BlockSpec((tok...]
    ppermute x0 -> x16, waiting for transfers between devices: none -> 29.6 us  [the longest x3 12.1 us: route_experts(): other = tuple((lax.ppermute(w, 'ctx', CORE_SWAP) for w in own))]
    ppermute x0 -> x16, starting transfers between devices: none -> 21.3 us  [the longest x3 4.79 us: attend_all(): lax.ppermute(picked[d], 'exp', shift_x(d))]
    slice x3 -> x2, local copies, waits for them, and re-layouts: 16.5 us -> 1.44 us  [the longest x1 0.72 us: attend_all(): r3a = lax.ppermute(r1[:2], 'exp', shift_y(1))]
    reduce_sum x1 -> x0, other arithmetic: 11.6 us -> none  [attend_all(): new_sum = jnp.sum(weights, axis=-1)]
    concatenate x4 -> x2, other arithmetic: 5.56 us -> 0.16 us  [the longest x1 0.08 us: attend_all(): outs = attend(jnp.concatenate([where, usable]), qs, rs)]
  transfers between devices with their start and end apart: 5 -> 20, of which waited for: 4 -> 13; matrix products, arithmetic and copies ran while one was open for 34% -> 2% of each run, Pallas kernels for 0% -> 15%
where the time goes in v1:
time: 250 us; the launch traced here: 247 us
  waiting for transfers between devices  132 us (53%)
  Pallas kernels  37.3 us (15%)
  starting transfers between devices  28.7 us (11%)
  blocking collectives  18.6 us (7%)
  between operations  14 us (6%)
  local copies, waits for them, and re-layouts  9.62 us (4%)
  matrix products  4.72 us (2%)
  other arithmetic  2.6 us (1%)
    all_gather x1, waiting for transfers between devices, route_experts(): lax.all_gather(incoming.reshape(-1, model_width), 'ctx', axis=0, tiled=Tr...  51.5 us
    reduce_scatter x1, waiting for transfers between devices, route_experts(): lax.psum_scatter(partial, 'ctx', scatter_dimension=0, tiled=True, axis_in...  33.6 us
    pallas_call x1, Pallas kernels, expert_rows(): pl.pallas_call(ffn_kernel, grid=(2 * steps,), in_specs=[pl.BlockSpec((tok...  24.7 us
    all_to_all x1, blocking collectives, route_experts(): lax.all_to_all(outgoing, 'exp', split_axis=0, concat_axis=0, tiled=True)  18.6 us
    all_gather x1, waiting for transfers between devices, attend_all(): everyone = lax.all_gather(paired, 'ctx', axis=0, tiled=True)  16.8 us
    ppermute x3, waiting for transfers between devices, route_experts(): other = tuple((lax.ppermute(w, 'ctx', CORE_SWAP) for w in own))  12.1 us
    pallas_call x1, Pallas kernels, attend(): pl.pallas_call(attend_kernel, grid_spec=pltpu.PrefetchScalarGridSpec(num_...  9.24 us
    all_to_all x1, starting transfers between devices, route_experts(): lax.all_to_all(summed_output.reshape(exp_count, capacity, model_width), '...  7.27 us
  transfers between devices with their start and end apart: 20, of which 13 were waited for; matrix products, arithmetic and copies ran while one was open for 2% of the time, Pallas kernels for 15%

profile of v1, /device:TPU:2, one launch (start us, length us, event | category | flops | bytes accessed | tf_op | source)
XLA Modules:
  0.0 247.1 jit_solution(16237240065654259744)
XLA Ops:
  12.6 18.6 %all_to_all.10 = bf16[16,4,5120]{2,1,0:T(4,128)(2,1)S(1)} all-to-all(bf16[16,4,5120]{2,1,0:T(4,128)(2,1)S(1)} %copy.18), channel_id=1, replica_groups=mesh['ctx'=16,'exp'=16] {'exp'}, dimensions={0} | all-to-all | bytes 1310720 | tf_op jit(solution)/shard_map/all_to_all | solution.py:337
  34.0 7.2 %collective-permute-done.13.g1 = bf16[5120,256]{1,0:T(8,128)(2,1)S(1)} collective-permute-done((bf16[5120,256]{1,0:T(8,128)(2,1)}, bf16[5120,256]{1,0:T(8,128)(2,1)S(1)}, u32[]{:S(2)}, u32[]{:S(2)}) %collective-permute-start.13) | collective-permute-done | bytes 2621472 | tf_op jit(solution)/shard_map/ppermute | solution.py:323
  42.4 3.7 %collective-permute-done.15.d1 = bf16[256,5120]{1,0:T(8,128)(2,1)} collective-permute-done((bf16[256,5120]{1,0:T(8,128)(2,1)}, bf16[256,5120]{1,0:T(8,128)(2,1)}, u32[]{:S(2)}, u32[]{:S(2)}) %collective-permute-start.15) | collective-permute-done | bytes 2621472 | tf_op jit(solution)/shard_map/ppermute | solution.py:323
  46.1 51.5 %all-gather.5.cloned.1.call-done.x_ref = bf16[512,5120]{1,0:T(8,128)(2,1)} async-done(((bf16[64,5120]{1,0:T(8,128)(2,1)}), bf16[512,5120]{1,0:T(8,128)(2,1)}) %all-gather.5.cloned.1.call-update) | async-done | bytes 5242896 | tf_op jit(solution)/shard_map/all_gather | solution.py:338
  97.6 24.7 %expert_rows.1 = bf16[512,5120]{1,0:T(8,128)(2,1)} custom-call(bf16[512,5120]{1,0:T(8,128)(2,1)} %all-gather.5.cloned.1.call-done.x_ref, bf16[5120,256]{1,0:T(8,128)(2,1)} %bitcast.36, bf16[5120,256]{1,0:T(8,128)(2,1)} %bitcast.38, bf16[256,5120]{1,0:T(8,128)(2,1)} %bitcast.40, bf16[5120,256]{1,0:T(8,128)(2,1)} %copy-done.7, ...), custom_call_target="tpu_custom_call" | custom-call | flops 8053063680 | bytes 26214400 | tf_op jit(solution)/shard_map/expert_rows/pallas_call | solution.py:299
  123.8 16.8 %all-gather.3.cloned.1.call-done.source = bf16[32,64,1024]{2,1,0:T(8,128)(2,1)} async-done(((bf16[2,64,1024]{2,1,0:T(8,128)(2,1)}), bf16[32,64,1024]{2,1,0:T(8,128)(2,1)}) %all-gather.3.cloned.1.call-update) | async-done | bytes 4194320 | tf_op jit(solution)/shard_map/all_gather | solution.py:236
  140.6 2.2 copy-done.1
  143.5 1.5 collective-permute-start.3
  146.2 2.1 collective-permute-start.5
  149.6 3.4 %collective-permute-done.4.refs_2_ = bf16[4,64,256]{2,1,0:T(8,128)(2,1)S(1)} collective-permute-done((bf16[4,64,256]{2,1,0:T(8,128)(2,1)S(1)}, bf16[4,64,256]{2,1,0:T(8,128)(2,1)S(1)}, u32[]{:S(2)}, u32[]{:S(2)}) %collective-permute-start.4) | collective-permute-done | bytes 131104 | tf_op jit(solution)/shard_map/ppermute | solution.py:248
  154.8 2.9 %collective-permute-start.7 = (bf16[4,4,64,256]{3,2,1,0:T(8,128)(2,1)S(1)}, bf16[4,4,64,256]{3,2,1,0:T(8,128)(2,1)S(1)}, u32[]{:S(2)}, u32[]{:S(2)}) collective-permute-start(bf16[4,4,64,256]{3,2,1,0:T(8,128)(2,1)S(1)} %stack_sources.1), channel_id=1, source_target_pairs={{0,3},{1,0},{2,1},{3,2},{4,7},{5,4},{6,5},{7,6},{8,11},{9,8},{10,9... | collective-permute-start | bytes 1572872 | tf_op jit(solution)/shard_map/ppermute | solution.py:251
  160.9 1.9 collective-permute-start.2
  162.8 5.6 %collective-permute-done.7 = bf16[4,4,64,256]{3,2,1,0:T(8,128)(2,1)S(1)} collective-permute-done((bf16[4,4,64,256]{3,2,1,0:T(8,128)(2,1)S(1)}, bf16[4,4,64,256]{3,2,1,0:T(8,128)(2,1)S(1)}, u32[]{:S(2)}, u32[]{:S(2)}) %collective-permute-start.7) | collective-permute-done | bytes 524320 | tf_op jit(solution)/shard_map/ppermute | solution.py:251
  169.1 3.7 %collective-permute-start.9 = (bf16[2,4,64,256]{3,2,1,0:T(8,128)(2,1)}, bf16[2,4,64,256]{3,2,1,0:T(8,128)(2,1)S(1)}, u32[]{:S(2)}, u32[]{:S(2)}) collective-permute-start(bf16[2,4,64,256]{3,2,1,0:T(8,128)(2,1)} %slice.43), channel_id=1, source_target_pairs={{0,3},{1,0},{2,1},{3,2},{4,7},{5,4},{6,5},{7,6},{8,11},{9,8},{10,9... | collective-permute-start | bytes 786440 | tf_op jit(solution)/shard_map/ppermute | solution.py:253
  173.5 33.6 %reduce-scatter.2.cloned.1.call-done = bf16[64,5120]{1,0:T(8,128)(2,1)} async-done(((bf16[512,5120]{1,0:T(8,128)(2,1)}), bf16[64,5120]{1,0:T(8,128)(2,1)}) %reduce-scatter.2.cloned.1.call-update) | async-done | bytes 655376 | tf_op jit(solution)/shard_map/reduce_scatter | solution.py:342
  207.1 2.3 reshape.174
  209.5 7.3 %all-to-all-start.1 = ((bf16[16,4,5120]{2,1,0:T(4,128)(2,1)}), bf16[16,4,5120]{2,1,0:T(4,128)(2,1)}, u32[]{:S(2)}, u32[]{:S(2)}) async-start(bf16[16,4,5120]{2,1,0:T(4,128)(2,1)} %reshape.174), calls=%async_computation.2 | async-start | bytes 1310720 | tf_op jit(solution)/shard_map/all_to_all | solution.py:345
  216.9 9.2 %attend.1 = (bf16[2,64,640]{2,1,0:T(8,128)(2,1)S(1)}, bf16[2,64,640]{2,1,0:T(8,128)(2,1)S(1)}, bf16[2,64,640]{2,1,0:T(8,128)(2,1)S(1)}, bf16[2,64,640]{2,1,0:T(8,128)(2,1)S(1)}) custom-call(s32[4]{0:T(128)S(1)} %pad_add_fusion.1.where, bf16[2,64,640]{2,1,0:T(8,128)(2,1)S(1)} %get-tuple-element.14.q0, bf16[2,64,640]{2,1,0:T(8,128)(2,1)S(1)} %collective-permute-done.q1, ...), custom_call_target="tpu_custom_call" | custom-call | flops 2200000000 | bytes 4194304 | tf_op jit(solution)/shard_map/attend/pallas_call | solution.py:204
  226.4 2.8 %collective-permute-start.11 = (bf16[2,64,640]{2,1,0:T(8,128)(2,1)S(1)}, bf16[2,64,640]{2,1,0:T(8,128)(2,1)S(1)}, u32[]{:S(2)}, u32[]{:S(2)}) collective-permute-start(bf16[2,64,640]{2,1,0:T(8,128)(2,1)S(1)} %get-tuple-element.24), channel_id=1, source_target_pairs={{0,8},{1,9},{2,10},{3,11},{4,12},{5,13},{6,14},{7,15},{8,0},{9,1},... | collective-permute-start | bytes 491528 | tf_op jit(solution)/shard_map/ppermute | solution.py:256
  229.2 1.8 collective-permute-start.12
  231.0 1.5 collective-permute-done.10.refs_1_
  232.5 3.6 %collective-permute-done.11.refs_2_ = bf16[2,64,640]{2,1,0:T(8,128)(2,1)S(1)} collective-permute-done((bf16[2,64,640]{2,1,0:T(8,128)(2,1)S(1)}, bf16[2,64,640]{2,1,0:T(8,128)(2,1)S(1)}, u32[]{:S(2)}, u32[]{:S(2)}) %collective-permute-start.11) | collective-permute-done | bytes 163872 | tf_op jit(solution)/shard_map/ppermute | solution.py:256
  237.0 1.4 join_heads.1
  238.4 2.1 fusion
  (75 shorter events, 21.5 us)
Async XLA Ops:
  7.2 90.4 %all-gather.5.cloned.1.call-start = ((), (), s32[]{:S(2)}) async-start(), calls=%async_computation.4 | async-start | bytes 5898240 | tf_op jit(solution)/shard_map/all_gather | solution.py:338
  10.7 21.6 %copy-start.5 = (bf16[2,64,512]{2,1,0:T(8,128)(2,1)S(1)}, bf16[2,64,512]{2,1,0:T(8,128)(2,1)}, u32[]{:S(2)}) copy-start(bf16[2,64,512]{2,1,0:T(8,128)(2,1)} %param.11) | copy-start | bytes 393220
  10.7 21.6 %copy-start.6 = (bf16[2,64,512]{2,1,0:T(8,128)(2,1)S(1)}, bf16[2,64,512]{2,1,0:T(8,128)(2,1)}, u32[]{:S(2)}) copy-start(bf16[2,64,512]{2,1,0:T(8,128)(2,1)} %param.12) | copy-start | bytes 393220
  32.3 108.3 %all-gather.3.cloned.1.call-start = ((), (), s32[]{:S(2)}) async-start(), calls=%async_computation.3 | async-start | bytes 4456448 | tf_op jit(solution)/shard_map/all_gather | solution.py:236
  33.2 173.9 %reduce-scatter.2.cloned.1.call-start = ((), (), s32[]{:S(2)}) async-start(), calls=%async_computation.5 | async-start | bytes 5898240 | tf_op jit(solution)/shard_map/reduce_scatter | solution.py:342
  33.3 7.9 %collective-permute-start.13 = (bf16[5120,256]{1,0:T(8,128)(2,1)}, bf16[5120,256]{1,0:T(8,128)(2,1)S(1)}, u32[]{:S(2)}, u32[]{:S(2)}) collective-permute-start(bf16[5120,256]{1,0:T(8,128)(2,1)} %bitcast.35), channel_id=1, source_target_pairs={{0,16},{16,0},{32,48},{48,32},{64,80},{80,64},{96,112},{112,96},{1... | collective-permute-start | bytes 7864328 | tf_op jit(solution)/shard_map/ppermute | solution.py:323
  33.4 9.0 %collective-permute-start.14 = (bf16[5120,256]{1,0:T(8,128)(2,1)}, bf16[5120,256]{1,0:T(8,128)(2,1)}, u32[]{:S(2)}, u32[]{:S(2)}) collective-permute-start(bf16[5120,256]{1,0:T(8,128)(2,1)} %bitcast.37), channel_id=1, source_target_pairs={{0,16},{16,0},{32,48},{48,32},{64,80},{80,64},{96,112},{112,96},{1... | collective-permute-start | bytes 7864328 | tf_op jit(solution)/shard_map/ppermute | solution.py:323
  33.9 12.2 %collective-permute-start.15 = (bf16[256,5120]{1,0:T(8,128)(2,1)}, bf16[256,5120]{1,0:T(8,128)(2,1)}, u32[]{:S(2)}, u32[]{:S(2)}) collective-permute-start(bf16[256,5120]{1,0:T(8,128)(2,1)} %bitcast.39), channel_id=1, source_target_pairs={{0,16},{16,0},{32,48},{48,32},{64,80},{80,64},{96,112},{112,96},{1... | collective-permute-start | bytes 7864328 | tf_op jit(solution)/shard_map/ppermute | solution.py:323
  41.2 56.4 %copy-start.7 = (bf16[5120,256]{1,0:T(8,128)(2,1)}, bf16[5120,256]{1,0:T(8,128)(2,1)S(1)}, u32[]{:S(2)}) copy-start(bf16[5120,256]{1,0:T(8,128)(2,1)S(1)} %collective-permute-done.13.g1) | copy-start | bytes 7864324
  142.8 14.9 %copy-start.2 = (bf16[2,64,2560]{2,1,0:T(8,128)(2,1)S(1)}, bf16[2,64,2560]{2,1,0:T(8,128)(2,1)}, u32[]{:S(2)}) copy-start(bf16[2,64,2560]{2,1,0:T(8,128)(2,1)} %source.1) | copy-start | bytes 1966084
  143.5 6.1 %collective-permute-start.3 = (bf16[4,64,256]{2,1,0:T(8,128)(2,1)S(1)}, bf16[4,64,256]{2,1,0:T(8,128)(2,1)S(1)}, u32[]{:S(2)}, u32[]{:S(2)}) collective-permute-start(bf16[4,64,256]{2,1,0:T(8,128)(2,1)S(1)} %get-tuple-element.19), channel_id=1, source_target_pairs={{0,4},{1,5},{2,6},{3,7},{4,8},{5,9},{6,10},{7,11},{8,12},{9,13},{1... | collective-permute-start | bytes 393224 | tf_op jit(solution)/shard_map/ppermute | solution.py:248
  145.1 7.9 %collective-permute-start.4 = (bf16[4,64,256]{2,1,0:T(8,128)(2,1)S(1)}, bf16[4,64,256]{2,1,0:T(8,128)(2,1)S(1)}, u32[]{:S(2)}, u32[]{:S(2)}) collective-permute-start(bf16[4,64,256]{2,1,0:T(8,128)(2,1)S(1)} %get-tuple-element.20), channel_id=1, source_target_pairs={{0,8},{1,9},{2,10},{3,11},{4,12},{5,13},{6,14},{7,15},{8,0},{9,1},... | collective-permute-start | bytes 393224 | tf_op jit(solution)/shard_map/ppermute | solution.py:248
  146.2 8.0 %collective-permute-start.5 = (bf16[4,64,256]{2,1,0:T(8,128)(2,1)S(1)}, bf16[4,64,256]{2,1,0:T(8,128)(2,1)S(1)}, u32[]{:S(2)}, u32[]{:S(2)}) collective-permute-start(bf16[4,64,256]{2,1,0:T(8,128)(2,1)S(1)} %get-tuple-element.21), channel_id=1, source_target_pairs={{0,12},{1,13},{2,14},{3,15},{4,0},{5,1},{6,2},{7,3},{8,4},{9,5},{1... | collective-permute-start | bytes 393224 | tf_op jit(solution)/shard_map/ppermute | solution.py:248
  154.8 13.6 %collective-permute-start.7 = (bf16[4,4,64,256]{3,2,1,0:T(8,128)(2,1)S(1)}, bf16[4,4,64,256]{3,2,1,0:T(8,128)(2,1)S(1)}, u32[]{:S(2)}, u32[]{:S(2)}) collective-permute-start(bf16[4,4,64,256]{3,2,1,0:T(8,128)(2,1)S(1)} %stack_sources.1), channel_id=1, source_target_pairs={{0,3},{1,0},{2,1},{3,2},{4,7},{5,4},{6,5},{7,6},{8,11},{9,8},{10,9... | collective-permute-start | bytes 1572872 | tf_op jit(solution)/shard_map/ppermute | solution.py:251
  157.7 15.1 %collective-permute-start.6 = (bf16[4,4,64,256]{3,2,1,0:T(8,128)(2,1)S(1)}, bf16[4,4,64,256]{3,2,1,0:T(8,128)(2,1)S(1)}, u32[]{:S(2)}, u32[]{:S(2)}) collective-permute-start(bf16[4,4,64,256]{3,2,1,0:T(8,128)(2,1)S(1)} %stack_sources.1), channel_id=1, source_target_pairs={{0,1},{1,2},{2,3},{3,0},{4,5},{5,6},{6,7},{7,4},{8,9},{9,10},{10,1... | collective-permute-start | bytes 1572872 | tf_op jit(solution)/shard_map/ppermute | solution.py:250
  158.3 58.6 %collective-permute-start = (bf16[2,64,640]{2,1,0:T(8,128)(2,1)S(1)}, bf16[2,64,640]{2,1,0:T(8,128)(2,1)S(1)}, u32[]{:S(2)}, u32[]{:S(2)}) collective-permute-start(bf16[2,64,640]{2,1,0:T(8,128)(2,1)S(1)} %get-tuple-element.15), channel_id=1, source_target_pairs={{0,4},{1,5},{2,6},{3,7},{4,8},{5,9},{6,10},{7,11},{8,12},{9,13},{1... | collective-permute-start | bytes 491528 | tf_op jit(solution)/shard_map/ppermute | solution.py:246
  159.6 57.4 %collective-permute-start.1 = (bf16[2,64,640]{2,1,0:T(8,128)(2,1)S(1)}, bf16[2,64,640]{2,1,0:T(8,128)(2,1)S(1)}, u32[]{:S(2)}, u32[]{:S(2)}) collective-permute-start(bf16[2,64,640]{2,1,0:T(8,128)(2,1)S(1)} %get-tuple-element.16), channel_id=1, source_target_pairs={{0,8},{1,9},{2,10},{3,11},{4,12},{5,13},{6,14},{7,15},{8,0},{9,1},... | collective-permute-start | bytes 491528 | tf_op jit(solution)/shard_map/ppermute | solution.py:246
  160.9 56.0 %collective-permute-start.2 = (bf16[2,64,640]{2,1,0:T(8,128)(2,1)S(1)}, bf16[2,64,640]{2,1,0:T(8,128)(2,1)S(1)}, u32[]{:S(2)}, u32[]{:S(2)}) collective-permute-start(bf16[2,64,640]{2,1,0:T(8,128)(2,1)S(1)} %get-tuple-element.17), channel_id=1, source_target_pairs={{0,12},{1,13},{2,14},{3,15},{4,0},{5,1},{6,2},{7,3},{8,4},{9,5},{1... | collective-permute-start | bytes 491528 | tf_op jit(solution)/shard_map/ppermute | solution.py:246
  169.1 47.8 %collective-permute-start.9 = (bf16[2,4,64,256]{3,2,1,0:T(8,128)(2,1)}, bf16[2,4,64,256]{3,2,1,0:T(8,128)(2,1)S(1)}, u32[]{:S(2)}, u32[]{:S(2)}) collective-permute-start(bf16[2,4,64,256]{3,2,1,0:T(8,128)(2,1)} %slice.43), channel_id=1, source_target_pairs={{0,3},{1,0},{2,1},{3,2},{4,7},{5,4},{6,5},{7,6},{8,11},{9,8},{10,9... | collective-permute-start | bytes 786440 | tf_op jit(solution)/shard_map/ppermute | solution.py:253
  173.5 43.4 %collective-permute-start.8 = (bf16[2,4,64,256]{3,2,1,0:T(8,128)(2,1)}, bf16[2,4,64,256]{3,2,1,0:T(8,128)(2,1)S(1)}, u32[]{:S(2)}, u32[]{:S(2)}) collective-permute-start(bf16[2,4,64,256]{3,2,1,0:T(8,128)(2,1)} %slice.42), channel_id=1, source_target_pairs={{0,1},{1,2},{2,3},{3,0},{4,5},{5,6},{6,7},{7,4},{8,9},{9,10},{10,1... | collective-permute-start | bytes 786440 | tf_op jit(solution)/shard_map/ppermute | solution.py:252
  209.5 29.0 %all-to-all-start.1 = ((bf16[16,4,5120]{2,1,0:T(4,128)(2,1)}), bf16[16,4,5120]{2,1,0:T(4,128)(2,1)}, u32[]{:S(2)}, u32[]{:S(2)}) async-start(bf16[16,4,5120]{2,1,0:T(4,128)(2,1)} %reshape.174), calls=%async_computation.2 | async-start | bytes 1310720 | tf_op jit(solution)/shard_map/all_to_all | solution.py:345
  226.2 6.3 %collective-permute-start.10 = (bf16[2,64,640]{2,1,0:T(8,128)(2,1)S(1)}, bf16[2,64,640]{2,1,0:T(8,128)(2,1)S(1)}, u32[]{:S(2)}, u32[]{:S(2)}) collective-permute-start(bf16[2,64,640]{2,1,0:T(8,128)(2,1)S(1)} %get-tuple-element.23), channel_id=1, source_target_pairs={{0,12},{1,13},{2,14},{3,15},{4,0},{5,1},{6,2},{7,3},{8,4},{9,5},{1... | collective-permute-start | bytes 491528 | tf_op jit(solution)/shard_map/ppermute | solution.py:256
  226.4 9.7 %collective-permute-start.11 = (bf16[2,64,640]{2,1,0:T(8,128)(2,1)S(1)}, bf16[2,64,640]{2,1,0:T(8,128)(2,1)S(1)}, u32[]{:S(2)}, u32[]{:S(2)}) collective-permute-start(bf16[2,64,640]{2,1,0:T(8,128)(2,1)S(1)} %get-tuple-element.24), channel_id=1, source_target_pairs={{0,8},{1,9},{2,10},{3,11},{4,12},{5,13},{6,14},{7,15},{8,0},{9,1},... | collective-permute-start | bytes 491528 | tf_op jit(solution)/shard_map/ppermute | solution.py:256
  229.2 7.8 %collective-permute-start.12 = (bf16[2,64,640]{2,1,0:T(8,128)(2,1)S(1)}, bf16[2,64,640]{2,1,0:T(8,128)(2,1)S(1)}, u32[]{:S(2)}, u32[]{:S(2)}) collective-permute-start(bf16[2,64,640]{2,1,0:T(8,128)(2,1)S(1)} %get-tuple-element.25), channel_id=1, source_target_pairs={{0,4},{1,5},{2,6},{3,7},{4,8},{5,9},{6,10},{7,11},{8,12},{9,13},{1... | collective-permute-start | bytes 491528 | tf_op jit(solution)/shard_map/ppermute | solution.py:256
  (4 other events, 5.0 us)
Sparse Core Ops, SparseCore 0:
  32.4 65.1 all-gather.4
  100.0 40.5 all-gather.2
  143.2 63.9 reduce-scatter.1

commit v2 on v1

--- a/solution.py
+++ b/solution.py
@@ -1,3 +1,5 @@
+import functools
+
 import jax
 import jax.numpy as jnp
 from jax import lax
@@ -220,20 +222,22 @@
     )(where, *qs, *rs)
 
 
-def attend_all(queries, key_states, value_state_rows, block_lists):
-    ctx_count = lax.axis_size("ctx")
-    blocks_total = 2 * ctx_count
-    ctx_index = lax.axis_index("ctx")
-    exp_index = lax.axis_index("exp")
-    x, y = exp_index // SIDE, exp_index % SIDE
-    where = jnp.stack([x, y]).astype(jnp.int32)
+def pair_rows(key_states, value_state_rows):
     heads = key_states.shape[2] // HEAD_DIM
     columns = []
     for h in range(heads):
         columns.append(key_states[:, :, h * HEAD_DIM : (h + 1) * HEAD_DIM])
         columns.append(value_state_rows[:, :, h * HEAD_DIM : (h + 1) * HEAD_DIM])
-    paired = jnp.concatenate(columns, axis=2)
-    everyone = lax.all_gather(paired, "ctx", axis=0, tiled=True)
+    return jnp.concatenate(columns, axis=2)
+
+
+def attend_all(queries, everyone, block_lists):
+    ctx_count = lax.axis_size("ctx")
+    blocks_total = 2 * ctx_count
+    ctx_index = lax.axis_index("ctx")
+    exp_index = lax.axis_index("exp")
+    x, y = lax.div(exp_index, SIDE), lax.rem(exp_index, SIDE)
+    where = jnp.stack([x, y]).astype(jnp.int32)
     own_blocks = jnp.stack([ctx_index, blocks_total - 1 - ctx_index])
     listed = block_lists[own_blocks]
     usable = (listed != own_blocks).astype(jnp.int32)
@@ -257,63 +261,129 @@
     return join_heads(back, where)
 
 
-def ffn_kernel(x_ref, g0, u0, d0, g1, u1, d1, o_ref, acc):
-    i = pl.program_id(0)
-    half = pl.num_programs(0) // 2
-
-    def run(g, u, d):
-        gate = jnp.dot(x_ref[...], g[...], preferred_element_type=jnp.float32)
-        up = jnp.dot(x_ref[...], u[...], preferred_element_type=jnp.float32)
-        act = (gate / (1.0 + jnp.exp(-gate)) * up).astype(jnp.bfloat16)
-        return jnp.dot(act, d[...], preferred_element_type=jnp.float32)
-
-    @pl.when(i == 0)
-    def _():
-        acc[...] = run(g0, u0, d0)
-
-    @pl.when((i > 0) & (i < half))
-    def _():
-        acc[...] += run(g0, u0, d0)
-
-    @pl.when((i >= half) & (i < 2 * half - 1))
-    def _():
-        acc[...] += run(g1, u1, d1)
-
-    @pl.when(i == 2 * half - 1)
-    def _():
-        o_ref[...] = (acc[...] + run(g1, u1, d1)).astype(jnp.bfloat16)
-
-
-def expert_rows(rows, weights):
-    tokens, width = rows.shape
+def ffn_kernel(counts, width, hidden, *refs):
+    n, m = counts
+    xs, ws, outs = refs[:n], refs[n : n + 6], refs[n + 6 : n + 6 + m]
+    x_all, gates, downs, sums, sems = refs[n + 6 + m :]
+    targets = [gates.at[0], gates.at[1], gates.at[2], gates.at[3]]
+    targets += [downs.at[pl.ds(0, hidden), :], downs.at[pl.ds(hidden, hidden), :]]
+    order = (0, 1, 3, 4, 2, 5)
+    copies = [pltpu.make_async_copy(ws[w], targets[k], sems.at[k]) for k, w in enumerate(order)]
+    for copy in copies:
+        copy.start()
+    at = 0
+    for x in xs:
+        x_all[pl.ds(at, x.shape[0]), :] = x[...]
+        at += x.shape[0]
+    acts = []
+    depth = 1024
+
+    def project(which):
+        sums[...] = jnp.zeros_like(sums)
+
+        @pl.loop(0, width // depth)
+        def _(k):
+            span = pl.ds(pl.multiple_of(k * depth, depth), depth)
+            sums[...] += jnp.dot(
+                x_all[:, span], gates[which, span, :], preferred_element_type=jnp.float32
+            )
+
+        return sums[...]
+
+    for half in range(2):
+        copies[2 * half].wait()
+        gate = project(2 * half)
+        gate = gate / (1.0 + jnp.exp(-gate))
+        copies[2 * half + 1].wait()
+        acts.append((gate * project(2 * half + 1)).astype(jnp.bfloat16))
+    act = jnp.concatenate(acts, axis=1)
+    copies[4].wait()
+    copies[5].wait()
+    block = 512
+
+    @pl.loop(0, width // block)
+    def _(k):
+        columns = pl.ds(pl.multiple_of(k * block, block), block)
+        part = jnp.dot(act, downs[:, columns], preferred_element_type=jnp.float32)
+        part = part.astype(jnp.bfloat16)
+        at = 0
+        for out in outs:
+            out[:, columns] = part[at : at + out.shape[0]]
+            at += out.shape[0]
+
+
+def expert_rows(xs, weights, out_rows):
+    width = xs[0].shape[1]
     hidden = weights[0].shape[1]
-    block = 128
-    steps = hidden // block
-    first = lambda i: jnp.minimum(i, steps - 1)
-    second = lambda i: jnp.maximum(i - steps, 0)
-    specs = []
-    for at in (first, second):
-        specs.append(pl.BlockSpec((width, block), lambda i, at=at: (0, at(i))))
-        specs.append(pl.BlockSpec((width, block), lambda i, at=at: (0, at(i))))
-        specs.append(pl.BlockSpec((block, width), lambda i, at=at: (at(i), 0)))
-    return pl.pallas_call(
-        ffn_kernel,
-        grid=(2 * steps,),
-        in_specs=[pl.BlockSpec((tokens, width), lambda i: (0, 0), pipeline_mode=pl.Buffered(1))] + specs,
-        out_specs=pl.BlockSpec((tokens, width), lambda i: (0, 0), pipeline_mode=pl.Buffered(1)),
-        out_shape=jax.ShapeDtypeStruct((tokens, width), jnp.bfloat16),
-        scratch_shapes=[pltpu.VMEM((tokens, width), jnp.float32)],
-        compiler_params=ordinary(56),
+    tokens = sum(x.shape[0] for x in xs)
+    whole = pl.BlockSpec(memory_space=pltpu.VMEM)
+    return pl.pallas_call(
+        functools.partial(ffn_kernel, (len(xs), len(out_rows)), width, hidden),
+        in_specs=[whole] * len(xs) + [pl.BlockSpec(memory_space=pl.ANY)] * 6,
+        out_specs=[whole] * len(out_rows),
+        out_shape=[jax.ShapeDtypeStruct((r, width), jnp.bfloat16) for r in out_rows],
+        scratch_shapes=[
+            pltpu.VMEM((tokens, width), jnp.bfloat16),
+            pltpu.VMEM((4, width, hidden), jnp.bfloat16),
+            pltpu.VMEM((2 * hidden, width), jnp.bfloat16),
+            pltpu.VMEM((tokens, hidden), jnp.float32),
+            pltpu.SemaphoreType.DMA((6,)),
+        ],
+        compiler_params=pltpu.CompilerParams(vmem_limit_bytes=40 * 1024 * 1024),
         cost_estimate=pl.CostEstimate(
             flops=12 * tokens * width * hidden,
             bytes_accessed=12 * width * hidden + 4 * tokens * width,
             transcendentals=2 * tokens * hidden,
         ),
         name="expert_rows",
-    )(rows, *weights)
-
-
-def route_experts(hidden, router, expert_ids, w_gate, w_up, w_down):
+    )(*xs, *weights)
+
+
+def ring(d):
+    return [(2 * z + c, 2 * ((z + d) % 8) + c) for z in range(8) for c in range(2)]
+
+
+def up_z(v):
+    return lax.ppermute(v, "ctx", ring(1))
+
+
+def down_z(v):
+    return lax.ppermute(v, "ctx", ring(-1))
+
+
+def add(a, b):
+    return (a.astype(jnp.float32) + b.astype(jnp.float32)).astype(jnp.bfloat16)
+
+
+def ring_experts(block, first, gathered, weights):
+    rows = block.shape[0]
+    half = rows // 2
+    below, above = [block, first[0]], [block, first[1]]
+    for k in range(2):
+        below.append(up_z(below[-1]))
+        above.append(down_z(above[-1]))
+    far_low, far_high = up_z(below[3][:half]), down_z(above[3][half:])
+    near = expert_rows(
+        [block, below[1], above[1], below[2], above[2]], weights, [rows] * 5
+    )
+    near, far_low, far_high = lax.optimization_barrier((near, far_low, far_high))
+    own, p_b1, p_a1, p_b2, p_a2 = near
+    p_low, p_high, p_b3, p_a3, p_gathered = expert_rows(
+        [far_low, far_high, below[3], above[3], gathered],
+        weights,
+        [half, half, rows, rows, gathered.shape[0]],
+    )
+    rise, fall = up_z(p_low), down_z(p_high)
+    rise = jnp.concatenate([add(rise, p_a3[:half]), p_a3[half:]], axis=0)
+    fall = jnp.concatenate([p_b3[:half], add(fall, p_b3[half:])], axis=0)
+    rise, fall = up_z(rise), down_z(fall)
+    rise, fall = up_z(add(rise, p_a2)), down_z(add(fall, p_b2))
+    rise, fall = up_z(add(rise, p_a1)), down_z(add(fall, p_b1))
+    total = rise.astype(jnp.float32) + fall.astype(jnp.float32) + own.astype(jnp.float32)
+    return total.astype(jnp.bfloat16), p_gathered
+
+
+def route_experts(hidden, router, expert_ids, w_gate, w_up, w_down, everyone):
     expert_table = router.shape[1]
     local_tokens = hidden.shape[0]
     model_width = hidden.shape[1]
@@ -321,6 +391,7 @@
     exp_count = lax.axis_size("exp")
     own = (w_gate[0], w_up[0], w_down[0])
     other = tuple(lax.ppermute(w, "ctx", CORE_SWAP) for w in own)
+    weights = own + other
     logits = jnp.dot(hidden, router, preferred_element_type=jnp.float32)
     selected_expert = expert_ids[:, 0]
     onehot = (selected_expert[:, None] == jnp.arange(expert_table)[None, :]).astype(jnp.float32)
@@ -335,13 +406,17 @@
         "ect,td->ecd", dispatch, scaled_scores, preferred_element_type=jnp.float32
     ).astype(jnp.bfloat16)
     incoming = lax.all_to_all(outgoing, "exp", split_axis=0, concat_axis=0, tiled=True)
-    rows = lax.all_gather(
-        incoming.reshape(-1, model_width), "ctx", axis=0, tiled=True, axis_index_groups=RINGS
-    )
-    partial = expert_rows(rows, own + other)
-    summed_output = lax.psum_scatter(
+    incoming = incoming.reshape(-1, model_width)
+    split = incoming.shape[0] * 3 // 4
+    kept = incoming[:split]
+    first = (up_z(kept), down_z(kept))
+    gathered_part, first, everyone = lax.optimization_barrier((incoming[split:], first, everyone))
+    rows = lax.all_gather(gathered_part, "ctx", axis=0, tiled=True, axis_index_groups=RINGS)
+    ringed, partial = ring_experts(kept, first, rows, weights)
+    scattered = lax.psum_scatter(
         partial, "ctx", scatter_dimension=0, tiled=True, axis_index_groups=RINGS
     )
+    summed_output = jnp.concatenate([ringed, scattered], axis=0)
     returned = lax.all_to_all(
         summed_output.reshape(exp_count, capacity, model_width),
         "exp",
@@ -349,9 +424,10 @@
         concat_axis=0,
         tiled=True,
     )
-    return jnp.einsum("ect,ecd->td", dispatch, returned, preferred_element_type=jnp.float32).astype(
-        jnp.bfloat16
-    )
+    moe_out = jnp.einsum(
+        "ect,ecd->td", dispatch, returned, preferred_element_type=jnp.float32
+    ).astype(jnp.bfloat16)
+    return moe_out, everyone
 
 
 def shards(
@@ -366,8 +442,12 @@
     w_up,
     w_down,
 ):
-    attention = attend_all(queries, key_states, value_state_rows, block_lists)
-    moe_out = route_experts(hidden, router, expert_ids, w_gate, w_up, w_down)
+    paired = pair_rows(key_states, value_state_rows)
+    everyone = lax.all_gather(paired, "ctx", axis=0, tiled=True)
+    moe_out, everyone = route_experts(
+        hidden, router, expert_ids, w_gate, w_up, w_down, everyone
+    )
+    attention = attend_all(queries, everyone, block_lists)
     return (attention, moe_out)
 
 

time: 250 us -> 265 us (1.060)
  starting transfers between devices: 28.7 us -> 62.6 us
  waiting for transfers between devices: 132 us -> 99 us
  local copies, waits for them, and re-layouts: 9.62 us -> 37.3 us
  blocking collectives: 18.6 us -> 0 us
  other arithmetic: 2.6 us -> 7.13 us
    ppermute x0 -> x16, waiting for transfers between devices: none -> 80.7 us  [the longest x8 51.6 us: up_z(): return lax.ppermute(v, 'ctx', ring(1))]
    all_gather x2, waiting for transfers between devices: 68.3 us -> 0.04 us  [the longest x1 0.04 us: shards(): everyone = lax.all_gather(paired, 'ctx', axis=0, tiled=True)]
    reduce_scatter x1, waiting for transfers between devices: 33.6 us -> 0.01 us  [route_experts(): lax.psum_scatter(partial, 'ctx', scatter_dimension=0, tiled=True, axis_in...]
    ppermute x0 -> x16, starting transfers between devices: none -> 26.1 us  [the longest x8 19.7 us: down_z(): return lax.ppermute(v, 'ctx', ring(-1))]
    unnamed x23 -> x61, local copies, waits for them, and re-layouts: 3.53 us -> 23.8 us
    all_to_all x1 -> x0, blocking collectives: 18.6 us -> none  [route_experts(): lax.all_to_all(outgoing, 'exp', split_axis=0, concat_axis=0, tiled=True)]
    ppermute x3, waiting for transfers between devices: 12.1 us -> 0.01 us  [route_experts(): other = tuple((lax.ppermute(w, 'ctx', CORE_SWAP) for w in own))]
    all_to_all x0 -> x1, waiting for transfers between devices: none -> 9.96 us  [route_experts(): lax.all_to_all(outgoing, 'exp', split_axis=0, concat_axis=0, tiled=True)]
  transfers between devices with their start and end apart: 20 -> 37, of which waited for: 13 -> 17; matrix products, arithmetic and copies ran while one was open for 2% -> 9% of each run, Pallas kernels for 15% -> 9%
where the time goes in v2:
time: 265 us; the launch traced here: 261 us
  waiting for transfers between devices  99 us (37%)
  starting transfers between devices  62.6 us (24%)
  local copies, waits for them, and re-layouts  37.3 us (14%)
  Pallas kernels  36.6 us (14%)
  between operations  14.2 us (5%)
  other arithmetic  7.13 us (3%)
  matrix products  4.67 us (2%)
    ppermute x8, waiting for transfers between devices, up_z(): return lax.ppermute(v, 'ctx', ring(1))  51.6 us
    ppermute x8, waiting for transfers between devices, down_z(): return lax.ppermute(v, 'ctx', ring(-1))  29.1 us
    pallas_call x2, Pallas kernels, expert_rows(): pl.pallas_call(functools.partial(ffn_kernel, (len(xs), len(out_rows)), wi...  24 us
    unnamed x61, local copies, waits for them, and re-layouts  23.8 us
    ppermute x8, starting transfers between devices, down_z(): return lax.ppermute(v, 'ctx', ring(-1))  19.7 us
    all_to_all x1, waiting for transfers between devices, route_experts(): lax.all_to_all(outgoing, 'exp', split_axis=0, concat_axis=0, tiled=True)  9.96 us
    pallas_call x1, Pallas kernels, attend(): pl.pallas_call(attend_kernel, grid_spec=pltpu.PrefetchScalarGridSpec(num_...  9.24 us
    all_to_all x1, starting transfers between devices, route_experts(): lax.all_to_all(outgoing, 'exp', split_axis=0, concat_axis=0, tiled=True)  7.48 us
  transfers between devices with their start and end apart: 37, of which 17 were waited for; matrix products, arithmetic and copies ran while one was open for 9% of the time, Pallas kernels for 9%

profile of v2, /device:TPU:2, one launch (start us, length us, event | category | flops | bytes accessed | tf_op | source)
XLA Modules:
  0.0 261.5 jit_solution(7732564348547385547)
XLA Ops:
  20.5 7.5 %all-to-all-start = ((bf16[16,4,5120]{2,1,0:T(4,128)(2,1)}), bf16[16,4,5120]{2,1,0:T(4,128)(2,1)}, u32[]{:S(2)}, u32[]{:S(2)}) async-start(bf16[16,4,5120]{2,1,0:T(4,128)(2,1)} %copy.20), calls=%async_computation | async-start | bytes 1310720 | tf_op jit(solution)/shard_map/all_to_all | solution.py:408
  28.7 10.0 %all-to-all-done = bf16[16,4,5120]{2,1,0:T(4,128)(2,1)} async-done(((bf16[16,4,5120]{2,1,0:T(4,128)(2,1)}), bf16[16,4,5120]{2,1,0:T(4,128)(2,1)}, u32[]{:S(2)}, u32[]{:S(2)}) %all-to-all-start) | async-done | bytes 655392 | tf_op jit(solution)/shard_map/all_to_all | solution.py:408
  41.8 5.9 %collective-permute-start.4 = (bf16[48,5120]{1,0:T(8,128)(2,1)S(1)}, bf16[48,5120]{1,0:T(8,128)(2,1)}, u32[]{:S(2)}, u32[]{:S(2)}) collective-permute-start(bf16[48,5120]{1,0:T(8,128)(2,1)S(1)} %slice.63.refs_0_), channel_id=1, source_target_pairs={{0,224},{16,240},{32,0},{48,16},{64,32},{80,48},{96,64},{112,80},{... | collective-permute-start | bytes 1474568 | tf_op jit(solution)/shard_map/ppermute | solution.py:351
  49.4 14.8 %collective-permute-done.4.refs_2_ = bf16[48,5120]{1,0:T(8,128)(2,1)} collective-permute-done((bf16[48,5120]{1,0:T(8,128)(2,1)S(1)}, bf16[48,5120]{1,0:T(8,128)(2,1)}, u32[]{:S(2)}, u32[]{:S(2)}) %collective-permute-start.4) | collective-permute-done | bytes 491552 | tf_op jit(solution)/shard_map/ppermute | solution.py:351
  69.0 12.6 %collective-permute-done.15.refs_3_ = bf16[48,5120]{1,0:T(8,128)(2,1)} collective-permute-done((bf16[48,5120]{1,0:T(8,128)(2,1)}, bf16[48,5120]{1,0:T(8,128)(2,1)}, u32[]{:S(2)}, u32[]{:S(2)}) %collective-permute-start.15) | collective-permute-done | bytes 491552 | tf_op jit(solution)/shard_map/ppermute | solution.py:347
  82.1 3.2 %collective-permute-start.22 = (bf16[48,5120]{1,0:T(8,128)(2,1)}, bf16[48,5120]{1,0:T(8,128)(2,1)}, u32[]{:S(2)}, u32[]{:S(2)}) collective-permute-start(bf16[48,5120]{1,0:T(8,128)(2,1)} %collective-permute-done.16.refs_4_), channel_id=1, source_target_pairs={{0,224},{16,240},{32,0},{48,16},{64,32},{80,48},{96,64},{112,80},{... | collective-permute-start | bytes 1474568 | tf_op jit(solution)/shard_map/ppermute | solution.py:351
  86.1 18.0 %collective-permute-done.20.refs_2_ = bf16[48,5120]{1,0:T(8,128)(2,1)} collective-permute-done((bf16[48,5120]{1,0:T(8,128)(2,1)}, bf16[48,5120]{1,0:T(8,128)(2,1)}, u32[]{:S(2)}, u32[]{:S(2)}) %collective-permute-start.20) | collective-permute-done | bytes 491552 | tf_op jit(solution)/shard_map/ppermute | solution.py:347
  106.1 3.5 %collective-permute-start.23 = (bf16[24,5120]{1,0:T(8,128)(2,1)S(1)}, bf16[24,5120]{1,0:T(8,128)(2,1)S(1)}, u32[]{:S(2)}, u32[]{:S(2)}) collective-permute-start(bf16[24,5120]{1,0:T(8,128)(2,1)S(1)} %slice.87), channel_id=1, source_target_pairs={{0,224},{16,240},{32,0},{48,16},{64,32},{80,48},{96,64},{112,80},{... | collective-permute-start | bytes 737288 | tf_op jit(solution)/shard_map/ppermute | solution.py:351
  113.1 11.3 %expert_rows.2 = (bf16[48,5120]{1,0:T(8,128)(2,1)S(1)}, bf16[48,5120]{1,0:T(8,128)(2,1)S(1)}, bf16[48,5120]{1,0:T(8,128)(2,1)S(1)}, bf16[48,5120]{1,0:T(8,128)(2,1)S(1)}, bf16[48,5120]{1,0:T(8,128)(2,1)S(1)}) custom-call(bf16[48,5120]{1,0:T(8,128)(2,1)S(1)} %slice.63.refs_0_, bf16[48,5120]{1,0:T(8,128)(2,1)} %collective-permute-done.3.refs_1_, ...), custom_call_target="tpu_custom_call" | custom-call | flops 3774873600 | bytes 20643840 | tf_op jit(solution)/shard_map/expert_rows/pallas_call | solution.py:320
  134.8 12.7 %expert_rows.3 = (bf16[24,5120]{1,0:T(8,128)(2,1)S(1)}, bf16[24,5120]{1,0:T(8,128)(2,1)}, bf16[48,5120]{1,0:T(8,128)(2,1)S(1)}, bf16[48,5120]{1,0:T(8,128)(2,1)S(1)}, bf16[128,5120]{1,0:T(8,128)(2,1)}) custom-call(bf16[24,5120]{1,0:T(8,128)(2,1)S(1)} %collective-permute-done.21.refs_0_, bf16[24,5120]{1,0:T(8,128)(2,1)S(1)} %copy-done.22, ...), custom_call_target="tpu_custom_call" | custom-call | flops 4278190080 | bytes 21299200 | tf_op jit(solution)/shard_map/expert_rows/pallas_call | solution.py:320
  154.3 2.5 collective-permute-start.7
  157.7 2.6 collective-permute-done.6.refs_2_
  161.2 3.5 %collective-permute-start.9 = (bf16[4,4,64,256]{3,2,1,0:T(8,128)(2,1)S(1)}, bf16[4,4,64,256]{3,2,1,0:T(8,128)(2,1)S(1)}, u32[]{:S(2)}, u32[]{:S(2)}) collective-permute-start(bf16[4,4,64,256]{3,2,1,0:T(8,128)(2,1)S(1)} %stack_sources.1), channel_id=1, source_target_pairs={{0,3},{1,0},{2,1},{3,2},{4,7},{5,4},{6,5},{7,6},{8,11},{9,8},{10,9... | collective-permute-start | bytes 1572872 | tf_op jit(solution)/shard_map/ppermute | solution.py:255
  169.3 4.1 %collective-permute-done.24 = bf16[24,5120]{1,0:T(8,128)(2,1)S(1)} collective-permute-done((bf16[24,5120]{1,0:T(8,128)(2,1)S(1)}, bf16[24,5120]{1,0:T(8,128)(2,1)S(1)}, u32[]{:S(2)}, u32[]{:S(2)}) %collective-permute-start.24) | collective-permute-done | bytes 245792 | tf_op jit(solution)/shard_map/ppermute | solution.py:347
  175.4 7.1 %collective-permute-done.29 = bf16[48,5120]{1,0:T(8,128)(2,1)S(1)} collective-permute-done((bf16[48,5120]{1,0:T(8,128)(2,1)S(1)}, bf16[48,5120]{1,0:T(8,128)(2,1)S(1)}, u32[]{:S(2)}, u32[]{:S(2)}) %collective-permute-start.29) | collective-permute-done | bytes 491552 | tf_op jit(solution)/shard_map/ppermute | solution.py:351
  184.2 9.7 %collective-permute-done.25 = bf16[48,5120]{1,0:T(8,128)(2,1)S(1)} collective-permute-done((bf16[48,5120]{1,0:T(8,128)(2,1)S(1)}, bf16[48,5120]{1,0:T(8,128)(2,1)S(1)}, u32[]{:S(2)}, u32[]{:S(2)}) %collective-permute-start.25) | collective-permute-done | bytes 491552 | tf_op jit(solution)/shard_map/ppermute | solution.py:347
  194.7 7.2 %collective-permute-done.30 = bf16[48,5120]{1,0:T(8,128)(2,1)S(1)} collective-permute-done((bf16[48,5120]{1,0:T(8,128)(2,1)S(1)}, bf16[48,5120]{1,0:T(8,128)(2,1)S(1)}, u32[]{:S(2)}, u32[]{:S(2)}) %collective-permute-start.30) | collective-permute-done | bytes 491552 | tf_op jit(solution)/shard_map/ppermute | solution.py:351
  203.8 5.5 %collective-permute-done.26 = bf16[48,5120]{1,0:T(8,128)(2,1)S(1)} collective-permute-done((bf16[48,5120]{1,0:T(8,128)(2,1)S(1)}, bf16[48,5120]{1,0:T(8,128)(2,1)S(1)}, u32[]{:S(2)}, u32[]{:S(2)}) %collective-permute-start.26) | collective-permute-done | bytes 491552 | tf_op jit(solution)/shard_map/ppermute | solution.py:347
  215.4 3.7 %collective-permute-start.11 = (bf16[2,4,64,256]{3,2,1,0:T(8,128)(2,1)}, bf16[2,4,64,256]{3,2,1,0:T(8,128)(2,1)S(1)}, u32[]{:S(2)}, u32[]{:S(2)}) collective-permute-start(bf16[2,4,64,256]{3,2,1,0:T(8,128)(2,1)} %slice.85), channel_id=1, source_target_pairs={{0,3},{1,0},{2,1},{3,2},{4,7},{5,4},{6,5},{7,6},{8,11},{9,8},{10,9... | collective-permute-start | bytes 786440 | tf_op jit(solution)/shard_map/ppermute | solution.py:257
  224.7 2.4 reshape.173
  227.0 5.7 %all-to-all-start.1 = ((bf16[16,4,5120]{2,1,0:T(4,128)(2,1)}), bf16[16,4,5120]{2,1,0:T(4,128)(2,1)}, u32[]{:S(2)}, u32[]{:S(2)}) async-start(bf16[16,4,5120]{2,1,0:T(4,128)(2,1)} %reshape.173), calls=%async_computation.2 | async-start | bytes 1310720 | tf_op jit(solution)/shard_map/all_to_all | solution.py:420
  232.9 9.2 %attend.1 = (bf16[2,64,640]{2,1,0:T(8,128)(2,1)S(1)}, bf16[2,64,640]{2,1,0:T(8,128)(2,1)S(1)}, bf16[2,64,640]{2,1,0:T(8,128)(2,1)S(1)}, bf16[2,64,640]{2,1,0:T(8,128)(2,1)S(1)}) custom-call(s32[4]{0:T(128)S(1)} %pad_add_fusion.1.where, bf16[2,64,640]{2,1,0:T(8,128)(2,1)S(1)} %get-tuple-element.35.q0, bf16[2,64,640]{2,1,0:T(8,128)(2,1)S(1)} %collective-permute-done.q1, ...), custom_call_target="tpu_custom_call" | custom-call | flops 2200000000 | bytes 4194304 | tf_op jit(solution)/shard_map/attend/pallas_call | solution.py:206
  242.4 2.8 %collective-permute-start.13 = (bf16[2,64,640]{2,1,0:T(8,128)(2,1)S(1)}, bf16[2,64,640]{2,1,0:T(8,128)(2,1)S(1)}, u32[]{:S(2)}, u32[]{:S(2)}) collective-permute-start(bf16[2,64,640]{2,1,0:T(8,128)(2,1)S(1)} %get-tuple-element.46), channel_id=1, source_target_pairs={{0,8},{1,9},{2,10},{3,11},{4,12},{5,13},{6,14},{7,15},{8,0},{9,1},... | collective-permute-start | bytes 491528 | tf_op jit(solution)/shard_map/ppermute | solution.py:260
  247.5 2.7 %collective-permute-done.13.refs_2_ = bf16[2,64,640]{2,1,0:T(8,128)(2,1)S(1)} collective-permute-done((bf16[2,64,640]{2,1,0:T(8,128)(2,1)S(1)}, bf16[2,64,640]{2,1,0:T(8,128)(2,1)S(1)}, u32[]{:S(2)}, u32[]{:S(2)}) %collective-permute-start.13) | collective-permute-done | bytes 163872 | tf_op jit(solution)/shard_map/ppermute | solution.py:260
  (164 shorter events, 79.2 us)
Async XLA Ops:
  7.2 58.4 %all-gather.3.cloned.1.call-start = ((), (), s32[]{:S(2)}) async-start(), calls=%async_computation.3 | async-start | bytes 4456448 | tf_op jit(solution)/shard_map/all_gather | solution.py:446
  20.5 18.2 %all-to-all-start = ((bf16[16,4,5120]{2,1,0:T(4,128)(2,1)}), bf16[16,4,5120]{2,1,0:T(4,128)(2,1)}, u32[]{:S(2)}, u32[]{:S(2)}) async-start(bf16[16,4,5120]{2,1,0:T(4,128)(2,1)} %copy.20), calls=%async_computation | async-start | bytes 1310720 | tf_op jit(solution)/shard_map/all_to_all | solution.py:408
  27.9 101.1 %all-gather.5.cloned.1.call-start = ((), (), s32[]{:S(2)}) async-start(), calls=%async_computation.4 | async-start | bytes 1474560 | tf_op jit(solution)/shard_map/all_gather | solution.py:414
  28.0 81.6 %collective-permute-start.17 = (bf16[5120,256]{1,0:T(8,128)(2,1)S(1)}, bf16[5120,256]{1,0:T(8,128)(2,1)}, u32[]{:S(2)}, u32[]{:S(2)}) collective-permute-start(bf16[5120,256]{1,0:T(8,128)(2,1)S(1)} %bitcast.26), channel_id=1, source_target_pairs={{0,16},{16,0},{32,48},{48,32},{64,80},{80,64},{96,112},{112,96},{1... | collective-permute-start | bytes 7864328 | tf_op jit(solution)/shard_map/ppermute | solution.py:393
  28.1 81.5 %collective-permute-start.18 = (bf16[5120,256]{1,0:T(8,128)(2,1)}, bf16[5120,256]{1,0:T(8,128)(2,1)}, u32[]{:S(2)}, u32[]{:S(2)}) collective-permute-start(bf16[5120,256]{1,0:T(8,128)(2,1)} %bitcast.29), channel_id=1, source_target_pairs={{0,16},{16,0},{32,48},{48,32},{64,80},{80,64},{96,112},{112,96},{1... | collective-permute-start | bytes 7864328 | tf_op jit(solution)/shard_map/ppermute | solution.py:393
  28.6 81.0 %collective-permute-start.19 = (bf16[256,5120]{1,0:T(8,128)(2,1)}, bf16[256,5120]{1,0:T(8,128)(2,1)}, u32[]{:S(2)}, u32[]{:S(2)}) collective-permute-start(bf16[256,5120]{1,0:T(8,128)(2,1)} %bitcast.32), channel_id=1, source_target_pairs={{0,16},{16,0},{32,48},{48,32},{64,80},{80,64},{96,112},{112,96},{1... | collective-permute-start | bytes 7864328 | tf_op jit(solution)/shard_map/ppermute | solution.py:393
  41.8 22.5 %collective-permute-start.4 = (bf16[48,5120]{1,0:T(8,128)(2,1)S(1)}, bf16[48,5120]{1,0:T(8,128)(2,1)}, u32[]{:S(2)}, u32[]{:S(2)}) collective-permute-start(bf16[48,5120]{1,0:T(8,128)(2,1)S(1)} %slice.63.refs_0_), channel_id=1, source_target_pairs={{0,224},{16,240},{32,0},{48,16},{64,32},{80,48},{96,64},{112,80},{... | collective-permute-start | bytes 1474568 | tf_op jit(solution)/shard_map/ppermute | solution.py:351
  47.7 17.9 %collective-permute-start.3 = (bf16[48,5120]{1,0:T(8,128)(2,1)S(1)}, bf16[48,5120]{1,0:T(8,128)(2,1)}, u32[]{:S(2)}, u32[]{:S(2)}) collective-permute-start(bf16[48,5120]{1,0:T(8,128)(2,1)S(1)} %slice.63.refs_0_), channel_id=1, source_target_pairs={{0,32},{16,48},{32,64},{48,80},{64,96},{80,112},{96,128},{112,144}... | collective-permute-start | bytes 1474568 | tf_op jit(solution)/shard_map/ppermute | solution.py:347
  65.6 157.0 %reduce-scatter.2.cloned.1.call-start = ((), (), s32[]{:S(2)}) async-start(), calls=%async_computation.5 | async-start | bytes 1474560 | tf_op jit(solution)/shard_map/reduce_scatter | solution.py:416
  65.7 15.9 %collective-permute-start.15 = (bf16[48,5120]{1,0:T(8,128)(2,1)}, bf16[48,5120]{1,0:T(8,128)(2,1)}, u32[]{:S(2)}, u32[]{:S(2)}) collective-permute-start(bf16[48,5120]{1,0:T(8,128)(2,1)} %collective-permute-done.3.refs_1_), channel_id=1, source_target_pairs={{0,32},{16,48},{32,64},{48,80},{64,96},{80,112},{96,128},{112,144}... | collective-permute-start | bytes 1474568 | tf_op jit(solution)/shard_map/ppermute | solution.py:347
  81.6 22.5 %collective-permute-start.20 = (bf16[48,5120]{1,0:T(8,128)(2,1)}, bf16[48,5120]{1,0:T(8,128)(2,1)}, u32[]{:S(2)}, u32[]{:S(2)}) collective-permute-start(bf16[48,5120]{1,0:T(8,128)(2,1)} %collective-permute-done.15.refs_3_), channel_id=1, source_target_pairs={{0,32},{16,48},{32,64},{48,80},{64,96},{80,112},{96,128},{112,144}... | collective-permute-start | bytes 1474568 | tf_op jit(solution)/shard_map/ppermute | solution.py:347
  82.1 23.0 %collective-permute-start.22 = (bf16[48,5120]{1,0:T(8,128)(2,1)}, bf16[48,5120]{1,0:T(8,128)(2,1)}, u32[]{:S(2)}, u32[]{:S(2)}) collective-permute-start(bf16[48,5120]{1,0:T(8,128)(2,1)} %collective-permute-done.16.refs_4_), channel_id=1, source_target_pairs={{0,224},{16,240},{32,0},{48,16},{64,32},{80,48},{96,64},{112,80},{... | collective-permute-start | bytes 1474568 | tf_op jit(solution)/shard_map/ppermute | solution.py:351
  105.1 23.3 %collective-permute-start.21 = (bf16[24,5120]{1,0:T(8,128)(2,1)S(1)}, bf16[24,5120]{1,0:T(8,128)(2,1)S(1)}, u32[]{:S(2)}, u32[]{:S(2)}) collective-permute-start(bf16[24,5120]{1,0:T(8,128)(2,1)S(1)} %slice.86), channel_id=1, source_target_pairs={{0,32},{16,48},{32,64},{48,80},{64,96},{80,112},{96,128},{112,144}... | collective-permute-start | bytes 737288 | tf_op jit(solution)/shard_map/ppermute | solution.py:347
  106.1 22.2 %collective-permute-start.23 = (bf16[24,5120]{1,0:T(8,128)(2,1)S(1)}, bf16[24,5120]{1,0:T(8,128)(2,1)S(1)}, u32[]{:S(2)}, u32[]{:S(2)}) collective-permute-start(bf16[24,5120]{1,0:T(8,128)(2,1)S(1)} %slice.87), channel_id=1, source_target_pairs={{0,224},{16,240},{32,0},{48,16},{64,32},{80,48},{96,64},{112,80},{... | collective-permute-start | bytes 737288 | tf_op jit(solution)/shard_map/ppermute | solution.py:351
  149.0 17.8 %collective-permute-start.28 = (bf16[24,5120]{1,0:T(8,128)(2,1)}, bf16[24,5120]{1,0:T(8,128)(2,1)}, u32[]{:S(2)}, u32[]{:S(2)}) collective-permute-start(bf16[24,5120]{1,0:T(8,128)(2,1)} %get-tuple-element.63), channel_id=1, source_target_pairs={{0,224},{16,240},{32,0},{48,16},{64,32},{80,48},{96,64},{112,80},{... | collective-permute-start | bytes 737288 | tf_op jit(solution)/shard_map/ppermute | solution.py:351
  161.2 49.0 %collective-permute-start.9 = (bf16[4,4,64,256]{3,2,1,0:T(8,128)(2,1)S(1)}, bf16[4,4,64,256]{3,2,1,0:T(8,128)(2,1)S(1)}, u32[]{:S(2)}, u32[]{:S(2)}) collective-permute-start(bf16[4,4,64,256]{3,2,1,0:T(8,128)(2,1)S(1)} %stack_sources.1), channel_id=1, source_target_pairs={{0,3},{1,0},{2,1},{3,2},{4,7},{5,4},{6,5},{7,6},{8,11},{9,8},{10,9... | collective-permute-start | bytes 1572872 | tf_op jit(solution)/shard_map/ppermute | solution.py:255
  164.7 47.9 %collective-permute-start.8 = (bf16[4,4,64,256]{3,2,1,0:T(8,128)(2,1)S(1)}, bf16[4,4,64,256]{3,2,1,0:T(8,128)(2,1)S(1)}, u32[]{:S(2)}, u32[]{:S(2)}) collective-permute-start(bf16[4,4,64,256]{3,2,1,0:T(8,128)(2,1)S(1)} %stack_sources.1), channel_id=1, source_target_pairs={{0,1},{1,2},{2,3},{3,0},{4,5},{5,6},{6,7},{7,4},{8,9},{9,10},{10,1... | collective-permute-start | bytes 1572872 | tf_op jit(solution)/shard_map/ppermute | solution.py:254
  173.4 20.4 %collective-permute-start.25 = (bf16[48,5120]{1,0:T(8,128)(2,1)S(1)}, bf16[48,5120]{1,0:T(8,128)(2,1)S(1)}, u32[]{:S(2)}, u32[]{:S(2)}) collective-permute-start(bf16[48,5120]{1,0:T(8,128)(2,1)S(1)} %pad_maximum_fusion.1), channel_id=1, source_target_pairs={{0,32},{16,48},{32,64},{48,80},{64,96},{80,112},{96,128},{112,144}... | collective-permute-start | bytes 1474568 | tf_op jit(solution)/shard_map/ppermute | solution.py:347
  182.6 19.3 %collective-permute-start.30 = (bf16[48,5120]{1,0:T(8,128)(2,1)S(1)}, bf16[48,5120]{1,0:T(8,128)(2,1)S(1)}, u32[]{:S(2)}, u32[]{:S(2)}) collective-permute-start(bf16[48,5120]{1,0:T(8,128)(2,1)S(1)} %add_convert_fusion.2), channel_id=1, source_target_pairs={{0,224},{16,240},{32,0},{48,16},{64,32},{80,48},{96,64},{112,80},{... | collective-permute-start | bytes 1474568 | tf_op jit(solution)/shard_map/ppermute | solution.py:351
  210.2 22.7 %collective-permute-start = (bf16[2,64,640]{2,1,0:T(8,128)(2,1)S(1)}, bf16[2,64,640]{2,1,0:T(8,128)(2,1)S(1)}, u32[]{:S(2)}, u32[]{:S(2)}) collective-permute-start(bf16[2,64,640]{2,1,0:T(8,128)(2,1)S(1)} %get-tuple-element.36), channel_id=1, source_target_pairs={{0,4},{1,5},{2,6},{3,7},{4,8},{5,9},{6,10},{7,11},{8,12},{9,13},{1... | collective-permute-start | bytes 491528 | tf_op jit(solution)/shard_map/ppermute | solution.py:250
  210.3 22.6 %collective-permute-start.1 = (bf16[2,64,640]{2,1,0:T(8,128)(2,1)S(1)}, bf16[2,64,640]{2,1,0:T(8,128)(2,1)S(1)}, u32[]{:S(2)}, u32[]{:S(2)}) collective-permute-start(bf16[2,64,640]{2,1,0:T(8,128)(2,1)S(1)} %get-tuple-element.37), channel_id=1, source_target_pairs={{0,8},{1,9},{2,10},{3,11},{4,12},{5,13},{6,14},{7,15},{8,0},{9,1},... | collective-permute-start | bytes 491528 | tf_op jit(solution)/shard_map/ppermute | solution.py:250
  212.6 20.2 %collective-permute-start.2 = (bf16[2,64,640]{2,1,0:T(8,128)(2,1)S(1)}, bf16[2,64,640]{2,1,0:T(8,128)(2,1)S(1)}, u32[]{:S(2)}, u32[]{:S(2)}) collective-permute-start(bf16[2,64,640]{2,1,0:T(8,128)(2,1)S(1)} %get-tuple-element.38), channel_id=1, source_target_pairs={{0,12},{1,13},{2,14},{3,15},{4,0},{5,1},{6,2},{7,3},{8,4},{9,5},{1... | collective-permute-start | bytes 491528 | tf_op jit(solution)/shard_map/ppermute | solution.py:250
  215.4 17.5 %collective-permute-start.11 = (bf16[2,4,64,256]{3,2,1,0:T(8,128)(2,1)}, bf16[2,4,64,256]{3,2,1,0:T(8,128)(2,1)S(1)}, u32[]{:S(2)}, u32[]{:S(2)}) collective-permute-start(bf16[2,4,64,256]{3,2,1,0:T(8,128)(2,1)} %slice.85), channel_id=1, source_target_pairs={{0,3},{1,0},{2,1},{3,2},{4,7},{5,4},{6,5},{7,6},{8,11},{9,8},{10,9... | collective-permute-start | bytes 786440 | tf_op jit(solution)/shard_map/ppermute | solution.py:257
  227.0 25.8 %all-to-all-start.1 = ((bf16[16,4,5120]{2,1,0:T(4,128)(2,1)}), bf16[16,4,5120]{2,1,0:T(4,128)(2,1)}, u32[]{:S(2)}, u32[]{:S(2)}) async-start(bf16[16,4,5120]{2,1,0:T(4,128)(2,1)} %reshape.173), calls=%async_computation.2 | async-start | bytes 1310720 | tf_op jit(solution)/shard_map/all_to_all | solution.py:420
  (40 other events, 449.3 us)
Sparse Core Ops, SparseCore 0:
  14.4 51.1 all-gather.2
  67.4 39.7 all-gather.4
  164.8 41.4 reduce-scatter.1

commit v3 on v1

--- a/solution.py
+++ b/solution.py
@@ -1,3 +1,5 @@
+import functools
+
 import jax
 import jax.numpy as jnp
 from jax import lax
@@ -26,29 +28,90 @@
     )
 
 
-def pick_kernel(table, source, *outs):
-    x = table[4]
+WHOLE = pl.BlockSpec(memory_space=pltpu.VMEM)
+TABLE = pl.BlockSpec(memory_space=pltpu.SMEM)
+
+
+def small(kernel, outs, name, moved, scratch=()):
+    return functools.partial(
+        pl.pallas_call,
+        kernel,
+        out_shape=outs,
+        scratch_shapes=scratch,
+        compiler_params=pltpu.CompilerParams(vmem_limit_bytes=16 * 1024 * 1024),
+        cost_estimate=pl.CostEstimate(flops=0, bytes_accessed=moved, transcendentals=0),
+        name=name,
+    )
+
+
+def pair_kernel(keys, values, out):
+    for h in range(SIDE):
+        out[:, :, h * 256 : h * 256 + 128] = keys[:, :, h * 128 : h * 128 + 128]
+        out[:, :, h * 256 + 128 : h * 256 + 256] = values[:, :, h * 128 : h * 128 + 128]
+
+
+def pair_rows(keys, values):
+    shape = keys.shape[:2] + (2 * keys.shape[2],)
+    call = small(pair_kernel, jax.ShapeDtypeStruct(shape, keys.dtype), "pair_rows", 1 << 19)
+    return call(in_specs=[WHOLE] * 2, out_specs=WHOLE)(keys, values)
+
+
+def ring(d):
+    return [(2 * z + c, 2 * ((z + d) % 8) + c) for z in range(8) for c in range(2)]
+
+
+def up_z(v):
+    return lax.ppermute(v, "ctx", ring(1))
+
+
+def down_z(v):
+    return lax.ppermute(v, "ctx", ring(-1))
+
+
+def choose_kernel(table, *refs):
+    own, b1, b2, b3, far_low, far_high, a3, a2, a1, mine, theirs, held = refs
+    for k, block in ((0, own), (1, b1), (2, b2), (3, b3), (5, a3), (6, a2), (7, a1)):
+        held[2 * k] = block[0]
+        held[2 * k + 1] = block[1]
+    held[8] = far_low[0]
+    held[9] = far_high[0]
+    for i in range(2):
+        mine[i] = held[table[i]]
+        theirs[i] = held[table[2 + i]]
+
+
+def choose_blocks(paired, table):
+    below, above = [paired], [paired]
+    for _ in range(3):
+        below.append(up_z(below[-1]))
+        above.append(down_z(above[-1]))
+    far_low, far_high = up_z(below[3][:1]), down_z(above[3][1:])
+    out = jax.ShapeDtypeStruct(paired.shape, paired.dtype)
+    held = pltpu.VMEM((16,) + paired.shape[1:], paired.dtype)
+    call = small(choose_kernel, [out, out], "choose_blocks", 3 << 20, [held])
+    return call(in_specs=[TABLE] + [WHOLE] * 9, out_specs=[WHOLE] * 2)(
+        table, paired, *below[1:], far_low, far_high, above[3], above[2], above[1]
+    )
+
+
+def pick_kernel(table, own, mine, swapped, *outs):
+    x = table[0]
     for d in range(SIDE):
         h = lax.rem(x + d, SIDE)
-        outs[d][0] = source[0, :, pl.ds(pl.multiple_of(h * 256, 256), 256)]
-
-
-def pick_heads(everyone, table):
-    rows, width = everyone.shape[1], everyone.shape[2]
-    part = jax.ShapeDtypeStruct((4, rows, 256), everyone.dtype)
-    return pl.pallas_call(
-        pick_kernel,
-        grid_spec=pltpu.PrefetchScalarGridSpec(
-            num_scalar_prefetch=1,
-            grid=(4,),
-            in_specs=[pl.BlockSpec((1, rows, width), lambda i, t: (t[i], 0, 0))],
-            out_specs=[pl.BlockSpec((1, rows, 256), lambda i, t: (i, 0, 0))] * SIDE,
-        ),
-        out_shape=[part] * SIDE,
-        compiler_params=ordinary(16),
-        cost_estimate=pl.CostEstimate(flops=0, bytes_accessed=2 << 20, transcendentals=0),
-        name="pick_heads",
-    )(table, everyone)
+        columns = pl.ds(pl.multiple_of(h * 256, 256), 256)
+        outs[d][0:2] = own[:, :, columns]
+        for i in range(2):
+            here = table[1 + i] > 0
+            outs[d][2 + i] = jnp.where(here, mine[i, :, columns], swapped[i, :, columns])
+
+
+def pick_heads(own, mine, swapped, table):
+    rows = own.shape[1]
+    part = jax.ShapeDtypeStruct((4, rows, 256), own.dtype)
+    call = small(pick_kernel, [part] * SIDE, "pick_heads", 2 << 20)
+    return call(in_specs=[TABLE] + [WHOLE] * 3, out_specs=[WHOLE] * SIDE)(
+        table, own, mine, swapped
+    )
 
 
 def split_kernel(where, source, *outs):
@@ -220,31 +283,33 @@
     )(where, *qs, *rs)
 
 
-def attend_all(queries, key_states, value_state_rows, block_lists):
+def exchange_rows(queries, key_states, value_state_rows, block_lists):
     ctx_count = lax.axis_size("ctx")
     blocks_total = 2 * ctx_count
     ctx_index = lax.axis_index("ctx")
     exp_index = lax.axis_index("exp")
-    x, y = exp_index // SIDE, exp_index % SIDE
+    x, y = lax.div(exp_index, SIDE), lax.rem(exp_index, SIDE)
+    z, core = lax.div(ctx_index, 2), lax.rem(ctx_index, 2)
     where = jnp.stack([x, y]).astype(jnp.int32)
-    heads = key_states.shape[2] // HEAD_DIM
-    columns = []
-    for h in range(heads):
-        columns.append(key_states[:, :, h * HEAD_DIM : (h + 1) * HEAD_DIM])
-        columns.append(value_state_rows[:, :, h * HEAD_DIM : (h + 1) * HEAD_DIM])
-    paired = jnp.concatenate(columns, axis=2)
-    everyone = lax.all_gather(paired, "ctx", axis=0, tiled=True)
-    own_blocks = jnp.stack([ctx_index, blocks_total - 1 - ctx_index])
+    other = ctx_index + 1 - 2 * core
+    own_blocks = jnp.stack(
+        [ctx_index, blocks_total - 1 - ctx_index, other, blocks_total - 1 - other]
+    )
     listed = block_lists[own_blocks]
     usable = (listed != own_blocks).astype(jnp.int32)
-    wanted = jnp.concatenate([own_blocks, listed])
-    holder = jnp.minimum(wanted, blocks_total - 1 - wanted)
-    row = 2 * holder + (wanted >= ctx_count).astype(jnp.int32)
-    table = jnp.concatenate([row, x[None]]).astype(jnp.int32)
-
-    mine = split_queries(queries, where)
-    qs = [mine[0]] + [lax.ppermute(mine[d], "exp", shift_x(d)) for d in range(1, SIDE)]
-    picked = pick_heads(everyone, table)
+    holder = jnp.minimum(listed, blocks_total - 1 - listed)
+    distance = lax.rem(z + 8 - lax.div(holder, 2), 8)
+    chosen = (2 * distance + (listed >= ctx_count).astype(jnp.int32)).astype(jnp.int32)
+    local = (lax.rem(holder, 2) == core).astype(jnp.int32)
+
+    paired = pair_rows(key_states, value_state_rows)
+    mine, theirs = choose_blocks(paired, chosen)
+    swapped = lax.ppermute(theirs, "ctx", CORE_SWAP)
+    picked = pick_heads(
+        paired, mine, swapped, jnp.concatenate([x[None], local[:2]]).astype(jnp.int32)
+    )
+    split = split_queries(queries, where)
+    qs = [split[0]] + [lax.ppermute(split[d], "exp", shift_x(d)) for d in range(1, SIDE)]
     received = [picked[0]] + [lax.ppermute(picked[d], "exp", shift_x(d)) for d in range(1, SIDE)]
     r0 = stack_sources(received, where)
     r1 = lax.ppermute(r0, "exp", shift_y(1))
@@ -252,68 +317,142 @@
     r3a = lax.ppermute(r1[:2], "exp", shift_y(1))
     r3b = lax.ppermute(r2[2:], "exp", shift_y(-1))
     rs = [r.reshape((r.shape[0], 2, 2) + r.shape[2:]) for r in (r0, r1, r2, r3a, r3b)]
-    outs = attend(jnp.concatenate([where, usable]), qs, rs)
+    return where, jnp.concatenate([where, usable[:2]]), qs, rs
+
+
+def attend_all(where, state, qs, rs):
+    outs = attend(state, qs, rs)
     back = [outs[0]] + [lax.ppermute(outs[d], "exp", shift_x(-d)) for d in range(1, SIDE)]
     return join_heads(back, where)
 
 
-def ffn_kernel(x_ref, g0, u0, d0, g1, u1, d1, o_ref, acc):
-    i = pl.program_id(0)
-    half = pl.num_programs(0) // 2
-
-    def run(g, u, d):
-        gate = jnp.dot(x_ref[...], g[...], preferred_element_type=jnp.float32)
-        up = jnp.dot(x_ref[...], u[...], preferred_element_type=jnp.float32)
-        act = (gate / (1.0 + jnp.exp(-gate)) * up).astype(jnp.bfloat16)
-        return jnp.dot(act, d[...], preferred_element_type=jnp.float32)
-
-    @pl.when(i == 0)
-    def _():
-        acc[...] = run(g0, u0, d0)
-
-    @pl.when((i > 0) & (i < half))
-    def _():
-        acc[...] += run(g0, u0, d0)
-
-    @pl.when((i >= half) & (i < 2 * half - 1))
-    def _():
-        acc[...] += run(g1, u1, d1)
-
-    @pl.when(i == 2 * half - 1)
-    def _():
-        o_ref[...] = (acc[...] + run(g1, u1, d1)).astype(jnp.bfloat16)
-
-
-def expert_rows(rows, weights):
-    tokens, width = rows.shape
+def ffn_kernel(counts, refs):
+    xs, ws, outs = refs[:counts], refs[counts : counts + 6], refs[counts + 6 : 2 * counts + 6]
+    rows, gates, downs, results, act, w_sem, x_sem, o_sem = refs[2 * counts + 6 :]
+    width, hidden = gates.shape[1], gates.shape[2]
+    step = rows.shape[1]
+    parts = []
+    for x, out in zip(xs, outs):
+        for at in range(0, x.shape[0], step):
+            parts.append((x, out, at, min(step, x.shape[0] - at)))
+    loads = [
+        pltpu.make_async_copy(
+            x.at[pl.ds(at, n), :], rows.at[k, pl.ds(0, n), :], x_sem.at[k]
+        )
+        for k, (x, _, at, n) in enumerate(parts)
+    ]
+    stores = [
+        pltpu.make_async_copy(
+            results.at[k, pl.ds(0, n), :], out.at[pl.ds(at, n), :], o_sem.at[k]
+        )
+        for k, (_, out, at, n) in enumerate(parts)
+    ]
+    targets = [gates.at[0], gates.at[1], gates.at[2], gates.at[3]]
+    targets += [downs.at[pl.ds(0, hidden), :], downs.at[pl.ds(hidden, hidden), :]]
+    order = (0, 1, 3, 4, 2, 5)
+    weights = [pltpu.make_async_copy(ws[w], targets[k], w_sem.at[k]) for k, w in enumerate(order)]
+    loads[0].start()
+    for copy in weights:
+        copy.start()
+    for copy in loads[1:]:
+        copy.start()
+    block = 1024
+    for k, (x, out, at, n) in enumerate(parts):
+        loads[k].wait()
+        for half in range(2):
+            if k == 0:
+                weights[2 * half].wait()
+            gate = jnp.dot(rows[k, :n], gates[2 * half], preferred_element_type=jnp.float32)
+            if k == 0:
+                weights[2 * half + 1].wait()
+            up = jnp.dot(rows[k, :n], gates[2 * half + 1], preferred_element_type=jnp.float32)
+            act[:n, half * hidden : (half + 1) * hidden] = (
+                gate / (1.0 + jnp.exp(-gate)) * up
+            ).astype(jnp.bfloat16)
+        if k == 0:
+            weights[4].wait()
+            weights[5].wait()
+
+        @pl.loop(0, width // block)
+        def _(c, k=k, n=n):
+            columns = pl.ds(pl.multiple_of(c * block, block), block)
+            part = jnp.dot(act[:n], downs[:, columns], preferred_element_type=jnp.float32)
+            results[k, :n, columns] = part.astype(jnp.bfloat16)
+
+        stores[k].start()
+    for copy in stores:
+        copy.wait()
+
+
+def expert_rows(xs, weights, step=256):
+    width = xs[0].shape[1]
     hidden = weights[0].shape[1]
-    block = 128
-    steps = hidden // block
-    first = lambda i: jnp.minimum(i, steps - 1)
-    second = lambda i: jnp.maximum(i - steps, 0)
-    specs = []
-    for at in (first, second):
-        specs.append(pl.BlockSpec((width, block), lambda i, at=at: (0, at(i))))
-        specs.append(pl.BlockSpec((width, block), lambda i, at=at: (0, at(i))))
-        specs.append(pl.BlockSpec((block, width), lambda i, at=at: (at(i), 0)))
+    tokens = sum(x.shape[0] for x in xs)
+    step = min(step, max(x.shape[0] for x in xs))
+    parts = sum(-(-x.shape[0] // step) for x in xs)
+    far = pl.BlockSpec(memory_space=pltpu.HBM)
     return pl.pallas_call(
-        ffn_kernel,
-        grid=(2 * steps,),
-        in_specs=[pl.BlockSpec((tokens, width), lambda i: (0, 0), pipeline_mode=pl.Buffered(1))] + specs,
-        out_specs=pl.BlockSpec((tokens, width), lambda i: (0, 0), pipeline_mode=pl.Buffered(1)),
-        out_shape=jax.ShapeDtypeStruct((tokens, width), jnp.bfloat16),
-        scratch_shapes=[pltpu.VMEM((tokens, width), jnp.float32)],
-        compiler_params=ordinary(56),
+        lambda *refs: ffn_kernel(len(xs), refs),
+        in_specs=[far] * (len(xs) + 6),
+        out_specs=[far] * len(xs),
+        out_shape=[jax.ShapeDtypeStruct(x.shape, jnp.bfloat16) for x in xs],
+        scratch_shapes=[
+            pltpu.VMEM((parts, step, width), jnp.bfloat16),
+            pltpu.VMEM((4, width, hidden), jnp.bfloat16),
+            pltpu.VMEM((2 * hidden, width), jnp.bfloat16),
+            pltpu.VMEM((parts, step, width), jnp.bfloat16),
+            pltpu.VMEM((step, 2 * hidden), jnp.bfloat16),
+            pltpu.SemaphoreType.DMA((6,)),
+            pltpu.SemaphoreType.DMA((parts,)),
+            pltpu.SemaphoreType.DMA((parts,)),
+        ],
+        compiler_params=pltpu.CompilerParams(vmem_limit_bytes=60 * 1024 * 1024),
         cost_estimate=pl.CostEstimate(
             flops=12 * tokens * width * hidden,
             bytes_accessed=12 * width * hidden + 4 * tokens * width,
             transcendentals=2 * tokens * hidden,
         ),
         name="expert_rows",
-    )(rows, *weights)
-
-
-def route_experts(hidden, router, expert_ids, w_gate, w_up, w_down):
+    )(*xs, *weights)
+
+
+def slot_kernel(hidden, router, ids, slots, out, places):
+    experts = router.shape[1]
+    tokens, capacity = hidden.shape[0], slots // experts
+    logits = jnp.dot(hidden[...], router[...], preferred_element_type=jnp.float32)
+    column = lax.broadcasted_iota(jnp.int32, (tokens, experts), 1)
+    onehot = jnp.where(ids[...] == column, 1.0, 0.0)
+    gate_score = 1.0 / (1.0 + jnp.exp(-jnp.sum(logits * onehot, axis=1, keepdims=True)))
+    row = lax.broadcasted_iota(jnp.int32, (tokens, tokens), 0)
+    earlier = lax.broadcasted_iota(jnp.int32, (tokens, tokens), 1)
+    upto = jnp.where(earlier <= row, 1.0, 0.0).astype(jnp.bfloat16)
+    counts = jnp.dot(upto, onehot.astype(jnp.bfloat16), preferred_element_type=jnp.float32)
+    rank = jnp.sum(counts * onehot, axis=1, keepdims=True) - 1.0
+    slot = ids[...] * capacity + rank.astype(jnp.int32)
+    target = lax.broadcasted_iota(jnp.int32, (tokens, slots), 1)
+    place = jnp.where(slot == target, 1.0, 0.0).astype(jnp.bfloat16)
+    places[...] = place
+    scaled = (hidden[...].astype(jnp.float32) * gate_score).astype(jnp.bfloat16)
+    out[...] = lax.dot_general(
+        place, scaled, (((0,), (0,)), ((), ())), preferred_element_type=jnp.float32
+    ).astype(jnp.bfloat16)
+
+
+def fill_slots(hidden, router, expert_ids, slots):
+    tokens, width = hidden.shape
+    outs = [
+        jax.ShapeDtypeStruct((slots, width), jnp.bfloat16),
+        jax.ShapeDtypeStruct((tokens, slots), jnp.bfloat16),
+    ]
+
+    def kernel(a, b, c, out, places):
+        slot_kernel(a, b, c, slots, out, places)
+
+    call = small(kernel, outs, "fill_slots", 1 << 20)
+    return call(in_specs=[WHOLE] * 3, out_specs=[WHOLE] * 2)(hidden, router, expert_ids)
+
+
+def route_experts(hidden, router, expert_ids, w_gate, w_up, w_down, exchanged, attend_rows):
     expert_table = router.shape[1]
     local_tokens = hidden.shape[0]
     model_width = hidden.shape[1]
@@ -321,27 +460,24 @@
     exp_count = lax.axis_size("exp")
     own = (w_gate[0], w_up[0], w_down[0])
     other = tuple(lax.ppermute(w, "ctx", CORE_SWAP) for w in own)
-    logits = jnp.dot(hidden, router, preferred_element_type=jnp.float32)
-    selected_expert = expert_ids[:, 0]
-    onehot = (selected_expert[:, None] == jnp.arange(expert_table)[None, :]).astype(jnp.float32)
-    gate_score = jax.nn.sigmoid(jnp.sum(logits * onehot, axis=1))
-    scaled_scores = (hidden.astype(jnp.float32) * gate_score[:, None]).astype(jnp.bfloat16)
-    slot_rank = (jnp.sum(jnp.cumsum(onehot, axis=0) * onehot, axis=1) - 1.0).astype(jnp.int32)
-    dispatch = (
-        (selected_expert[None, None, :] == jnp.arange(expert_table)[:, None, None])
-        & (slot_rank[None, None, :] == jnp.arange(capacity)[None, :, None])
-    ).astype(jnp.bfloat16)
-    outgoing = jnp.einsum(
-        "ect,td->ecd", dispatch, scaled_scores, preferred_element_type=jnp.float32
-    ).astype(jnp.bfloat16)
-    incoming = lax.all_to_all(outgoing, "exp", split_axis=0, concat_axis=0, tiled=True)
+    outgoing, places = fill_slots(hidden, router, expert_ids, expert_table * capacity)
+    incoming = lax.all_to_all(
+        outgoing.reshape(exp_count, capacity, model_width),
+        "exp",
+        split_axis=0,
+        concat_axis=0,
+        tiled=True,
+    )
     rows = lax.all_gather(
         incoming.reshape(-1, model_width), "ctx", axis=0, tiled=True, axis_index_groups=RINGS
     )
-    partial = expert_rows(rows, own + other)
+    rows, exchanged = lax.optimization_barrier((rows, exchanged))
+    (partial,) = expert_rows([rows], own + other)
     summed_output = lax.psum_scatter(
         partial, "ctx", scatter_dimension=0, tiled=True, axis_index_groups=RINGS
     )
+    attention = attend_rows(*exchanged)
+    summed_output, attention = lax.optimization_barrier((summed_output, attention))
     returned = lax.all_to_all(
         summed_output.reshape(exp_count, capacity, model_width),
         "exp",
@@ -349,9 +485,10 @@
         concat_axis=0,
         tiled=True,
     )
-    return jnp.einsum("ect,ecd->td", dispatch, returned, preferred_element_type=jnp.float32).astype(
-        jnp.bfloat16
-    )
+    moe_out = jnp.dot(
+        places, returned.reshape(-1, model_width), preferred_element_type=jnp.float32
+    ).astype(jnp.bfloat16)
+    return attention, moe_out
 
 
 def shards(
@@ -366,8 +503,17 @@
     w_up,
     w_down,
 ):
-    attention = attend_all(queries, key_states, value_state_rows, block_lists)
-    moe_out = route_experts(hidden, router, expert_ids, w_gate, w_up, w_down)
+    where, state, qs, rs = exchange_rows(queries, key_states, value_state_rows, block_lists)
+    attention, moe_out = route_experts(
+        hidden,
+        router,
+        expert_ids,
+        w_gate,
+        w_up,
+        w_down,
+        (qs, rs),
+        lambda qs, rs: attend_all(where, state, qs, rs),
+    )
     return (attention, moe_out)
 
 

time: 250 us -> 242 us (0.968)
  waiting for transfers between devices: 132 us -> 105 us
  blocking collectives: 18.6 us -> 37.1 us
  starting transfers between devices: 28.7 us -> 41.8 us
  matrix products: 4.72 us -> 0.96 us
  Pallas kernels: 37.3 us -> 34.1 us
  local copies, waits for them, and re-layouts: 9.62 us -> 6.9 us
    all_gather x1, waiting for transfers between devices: 51.5 us -> 0.01 us  [route_experts(): lax.all_gather(incoming.reshape(-1, model_width), 'ctx', axis=0, tiled=Tr...]
    ppermute x10 -> x19, waiting for transfers between devices: 11.4 us -> 59.2 us  [the longest x4 29.7 us: down_z(): return lax.ppermute(v, 'ctx', ring(-1))]
    ppermute x10 -> x19, starting transfers between devices: 15.9 us -> 35 us  [the longest x4 17.1 us: down_z(): return lax.ppermute(v, 'ctx', ring(-1))]
    all_to_all x1 -> x2, blocking collectives: 18.6 us -> 37.1 us  [the longest x1 18.6 us: route_experts(): lax.all_to_all(outgoing.reshape(exp_count, capacity, model_width), 'exp',...]
    all_gather x1 -> x0, waiting for transfers between devices: 16.8 us -> none  [attend_all(): everyone = lax.all_gather(paired, 'ctx', axis=0, tiled=True)]
    ppermute x3, waiting for transfers between devices: 12.1 us -> 0.01 us  [route_experts(): other = tuple((lax.ppermute(w, 'ctx', CORE_SWAP) for w in own))]
    reduce_scatter x1, waiting for transfers between devices: 33.6 us -> 42.5 us  [route_experts(): lax.psum_scatter(partial, 'ctx', scatter_dimension=0, tiled=True, axis_in...]
    all_to_all x1 -> x0, starting transfers between devices: 7.27 us -> none  [route_experts(): lax.all_to_all(summed_output.reshape(exp_count, capacity, model_width), '...]
  transfers between devices with their start and end apart: 20 -> 27, of which waited for: 13 -> 17; matrix products, arithmetic and copies ran while one was open for 2% -> 0% of each run, Pallas kernels for 15% -> 6%
where the time goes in v3:
time: 242 us; the launch traced here: 241 us
  waiting for transfers between devices  105 us (43%)
  starting transfers between devices  41.8 us (17%)
  blocking collectives  37.1 us (15%)
  Pallas kernels  34.1 us (14%)
  between operations  14.3 us (6%)
  local copies, waits for them, and re-layouts  6.9 us (3%)
    reduce_scatter x1, waiting for transfers between devices, route_experts(): lax.psum_scatter(partial, 'ctx', scatter_dimension=0, tiled=True, axis_in...  42.5 us
    ppermute x4, waiting for transfers between devices, down_z(): return lax.ppermute(v, 'ctx', ring(-1))  29.7 us
    pallas_call x1, Pallas kernels, expert_rows(): pl.pallas_call(lambda *refs: ffn_kernel(len(xs), refs), in_specs=[far] *...  20 us
    all_to_all x1, blocking collectives, route_experts(): lax.all_to_all(outgoing.reshape(exp_count, capacity, model_width), 'exp',...  18.6 us
    all_to_all x1, blocking collectives, route_experts(): lax.all_to_all(summed_output.reshape(exp_count, capacity, model_width), '...  18.5 us
    ppermute x4, starting transfers between devices, down_z(): return lax.ppermute(v, 'ctx', ring(-1))  17.1 us
    ppermute x1, waiting for transfers between devices, exchange_rows(): r2 = lax.ppermute(r0, 'exp', shift_y(-1))  9.55 us
    pallas_call x1, Pallas kernels, attend(): pl.pallas_call(attend_kernel, grid_spec=pltpu.PrefetchScalarGridSpec(num_...  9.23 us
  transfers between devices with their start and end apart: 27, of which 17 were waited for; matrix products, arithmetic and copies ran while one was open for 0% of the time, Pallas kernels for 6%

profile of v3, /device:TPU:2, one launch (start us, length us, event | category | flops | bytes accessed | tf_op | source)
XLA Modules:
  0.0 240.9 jit_solution(12186996043530446911)
XLA Ops:
  11.5 18.6 %all_to_all.10 = bf16[16,4,5120]{2,1,0:T(4,128)(2,1)S(1)} all-to-all(bf16[16,4,5120]{2,1,0:T(4,128)(2,1)S(1)} %reshape.192), channel_id=1, replica_groups=mesh['ctx'=16,'exp'=16] {'exp'}, dimensions={0} | all-to-all | bytes 1310720 | tf_op jit(solution)/shard_map/all_to_all | solution.py:464
  31.3 5.9 %collective-permute-start.7 = (bf16[2,64,1024]{2,1,0:T(8,128)(2,1)S(1)}, bf16[2,64,1024]{2,1,0:T(8,128)(2,1)S(1)}, u32[]{:S(2)}, u32[]{:S(2)}) collective-permute-start(bf16[2,64,1024]{2,1,0:T(8,128)(2,1)S(1)} %pair_rows.1.refs_0_.own), channel_id=1, source_target_pairs={{0,224},{16,240},{32,0},{48,16},{64,32},{80,48},{96,64},{112,80},{... | collective-permute-start | bytes 786440 | tf_op jit(solution)/shard_map/ppermute | solution.py:68
  37.8 3.6 %collective-permute-done.7.refs_8_ = bf16[2,64,1024]{2,1,0:T(8,128)(2,1)S(1)} collective-permute-done((bf16[2,64,1024]{2,1,0:T(8,128)(2,1)S(1)}, bf16[2,64,1024]{2,1,0:T(8,128)(2,1)S(1)}, u32[]{:S(2)}, u32[]{:S(2)}) %collective-permute-start.7) | collective-permute-done | bytes 262176 | tf_op jit(solution)/shard_map/ppermute | solution.py:68
  41.3 3.7 %collective-permute-start.8 = (bf16[2,64,1024]{2,1,0:T(8,128)(2,1)S(1)}, bf16[2,64,1024]{2,1,0:T(8,128)(2,1)S(1)}, u32[]{:S(2)}, u32[]{:S(2)}) collective-permute-start(bf16[2,64,1024]{2,1,0:T(8,128)(2,1)S(1)} %collective-permute-done.7.refs_8_), channel_id=1, source_target_pairs={{0,224},{16,240},{32,0},{48,16},{64,32},{80,48},{96,64},{112,80},{... | collective-permute-start | bytes 786440 | tf_op jit(solution)/shard_map/ppermute | solution.py:68
  45.1 10.9 %collective-permute-done.8.refs_7_ = bf16[2,64,1024]{2,1,0:T(8,128)(2,1)S(1)} collective-permute-done((bf16[2,64,1024]{2,1,0:T(8,128)(2,1)S(1)}, bf16[2,64,1024]{2,1,0:T(8,128)(2,1)S(1)}, u32[]{:S(2)}, u32[]{:S(2)}) %collective-permute-start.8) | collective-permute-done | bytes 262176 | tf_op jit(solution)/shard_map/ppermute | solution.py:68
  56.0 3.7 %collective-permute-start.9 = (bf16[2,64,1024]{2,1,0:T(8,128)(2,1)S(1)}, bf16[2,64,1024]{2,1,0:T(8,128)(2,1)S(1)}, u32[]{:S(2)}, u32[]{:S(2)}) collective-permute-start(bf16[2,64,1024]{2,1,0:T(8,128)(2,1)S(1)} %collective-permute-done.8.refs_7_), channel_id=1, source_target_pairs={{0,224},{16,240},{32,0},{48,16},{64,32},{80,48},{96,64},{112,80},{... | collective-permute-start | bytes 786440 | tf_op jit(solution)/shard_map/ppermute | solution.py:68
  60.4 10.2 %collective-permute-done.9.refs_6_ = bf16[2,64,1024]{2,1,0:T(8,128)(2,1)S(1)} collective-permute-done((bf16[2,64,1024]{2,1,0:T(8,128)(2,1)S(1)}, bf16[2,64,1024]{2,1,0:T(8,128)(2,1)S(1)}, u32[]{:S(2)}, u32[]{:S(2)}) %collective-permute-start.9) | collective-permute-done | bytes 262176 | tf_op jit(solution)/shard_map/ppermute | solution.py:68
  70.6 3.8 %collective-permute-start.10 = (bf16[1,64,1024]{2,1,0:T(8,128)(2,1)S(1)}, bf16[1,64,1024]{2,1,0:T(8,128)(2,1)S(1)}, u32[]{:S(2)}, u32[]{:S(2)}) collective-permute-start(bf16[1,64,1024]{2,1,0:T(8,128)(2,1)S(1)} %slice.35), channel_id=1, source_target_pairs={{0,224},{16,240},{32,0},{48,16},{64,32},{80,48},{96,64},{112,80},{... | collective-permute-start | bytes 393224 | tf_op jit(solution)/shard_map/ppermute | solution.py:68
  74.5 5.1 %collective-permute-done.10.refs_5_ = bf16[1,64,1024]{2,1,0:T(8,128)(2,1)S(1)} collective-permute-done((bf16[1,64,1024]{2,1,0:T(8,128)(2,1)S(1)}, bf16[1,64,1024]{2,1,0:T(8,128)(2,1)S(1)}, u32[]{:S(2)}, u32[]{:S(2)}) %collective-permute-start.10) | collective-permute-done | bytes 131104 | tf_op jit(solution)/shard_map/ppermute | solution.py:68
  79.6 3.8 %collective-permute-done.6.refs_4_ = bf16[1,64,1024]{2,1,0:T(8,128)(2,1)S(1)} collective-permute-done((bf16[1,64,1024]{2,1,0:T(8,128)(2,1)S(1)}, bf16[1,64,1024]{2,1,0:T(8,128)(2,1)S(1)}, u32[]{:S(2)}, u32[]{:S(2)}) %collective-permute-start.6) | collective-permute-done | bytes 131104 | tf_op jit(solution)/shard_map/ppermute | solution.py:64
  87.4 2.9 %collective-permute-start.13 = (bf16[4,64,256]{2,1,0:T(8,128)(2,1)S(1)}, bf16[4,64,256]{2,1,0:T(8,128)(2,1)S(1)}, u32[]{:S(2)}, u32[]{:S(2)}) collective-permute-start(bf16[4,64,256]{2,1,0:T(8,128)(2,1)S(1)} %get-tuple-element.39), channel_id=1, source_target_pairs={{0,8},{1,9},{2,10},{3,11},{4,12},{5,13},{6,14},{7,15},{8,0},{9,1},... | collective-permute-start | bytes 393224 | tf_op jit(solution)/shard_map/ppermute | solution.py:313
  94.1 3.7 %collective-permute-start.14 = (bf16[4,64,256]{2,1,0:T(8,128)(2,1)S(1)}, bf16[4,64,256]{2,1,0:T(8,128)(2,1)S(1)}, u32[]{:S(2)}, u32[]{:S(2)}) collective-permute-start(bf16[4,64,256]{2,1,0:T(8,128)(2,1)S(1)} %get-tuple-element.40), channel_id=1, source_target_pairs={{0,12},{1,13},{2,14},{3,15},{4,0},{5,1},{6,2},{7,3},{8,4},{9,5},{1... | collective-permute-start | bytes 393224 | tf_op jit(solution)/shard_map/ppermute | solution.py:313
  97.9 2.5 %collective-permute-done.14.refs_3_ = bf16[4,64,256]{2,1,0:T(8,128)(2,1)S(1)} collective-permute-done((bf16[4,64,256]{2,1,0:T(8,128)(2,1)S(1)}, bf16[4,64,256]{2,1,0:T(8,128)(2,1)S(1)}, u32[]{:S(2)}, u32[]{:S(2)}) %collective-permute-start.14) | collective-permute-done | bytes 131104 | tf_op jit(solution)/shard_map/ppermute | solution.py:313
  103.1 9.6 %collective-permute-done.16 = bf16[4,4,64,256]{3,2,1,0:T(8,128)(2,1)S(1)} collective-permute-done((bf16[4,4,64,256]{3,2,1,0:T(8,128)(2,1)S(1)}, bf16[4,4,64,256]{3,2,1,0:T(8,128)(2,1)S(1)}, u32[]{:S(2)}, u32[]{:S(2)}) %collective-permute-start.16) | collective-permute-done | bytes 524320 | tf_op jit(solution)/shard_map/ppermute | solution.py:316
  112.7 4.1 %collective-permute-start.1 = (bf16[2,64,640]{2,1,0:T(8,128)(2,1)S(1)}, bf16[2,64,640]{2,1,0:T(8,128)(2,1)S(1)}, u32[]{:S(2)}, u32[]{:S(2)}) collective-permute-start(bf16[2,64,640]{2,1,0:T(8,128)(2,1)S(1)} %get-tuple-element.33), channel_id=1, source_target_pairs={{0,8},{1,9},{2,10},{3,11},{4,12},{5,13},{6,14},{7,15},{8,0},{9,1},... | collective-permute-start | bytes 491528 | tf_op jit(solution)/shard_map/ppermute | solution.py:312
  117.1 3.0 %collective-permute-done.1.q2 = bf16[2,64,640]{2,1,0:T(8,128)(2,1)S(1)} collective-permute-done((bf16[2,64,640]{2,1,0:T(8,128)(2,1)S(1)}, bf16[2,64,640]{2,1,0:T(8,128)(2,1)S(1)}, u32[]{:S(2)}, u32[]{:S(2)}) %collective-permute-start.1) | collective-permute-done | bytes 163872 | tf_op jit(solution)/shard_map/ppermute | solution.py:312
  123.4 3.1 %collective-permute-done.18 = bf16[2,4,64,256]{3,2,1,0:T(8,128)(2,1)S(1)} collective-permute-done((bf16[2,4,64,256]{3,2,1,0:T(8,128)(2,1)S(1)}, bf16[2,4,64,256]{3,2,1,0:T(8,128)(2,1)S(1)}, u32[]{:S(2)}, u32[]{:S(2)}) %collective-permute-start.18) | collective-permute-done | bytes 262176 | tf_op jit(solution)/shard_map/ppermute | solution.py:318
  126.5 3.2 %collective-permute-done.17 = bf16[2,4,64,256]{3,2,1,0:T(8,128)(2,1)S(1)} collective-permute-done((bf16[2,4,64,256]{3,2,1,0:T(8,128)(2,1)S(1)}, bf16[2,4,64,256]{3,2,1,0:T(8,128)(2,1)S(1)}, u32[]{:S(2)}, u32[]{:S(2)}) %collective-permute-start.17) | collective-permute-done | bytes 262176 | tf_op jit(solution)/shard_map/ppermute | solution.py:317
  129.7 20.0 %expert_rows.1 = bf16[512,5120]{1,0:T(8,128)(2,1)} custom-call(bf16[512,5120]{1,0:T(8,128)(2,1)} %all-gather.2.cloned.1.call-done.refs_0_, bf16[5120,256]{1,0:T(8,128)(2,1)} %bitcast.28, bf16[5120,256]{1,0:T(8,128)(2,1)} %bitcast.30, bf16[256,5120]{1,0:T(8,128)(2,1)} %bitcast.32, bf16[5120,256]{1,0:T(8,128)(2,1)} %collective-permute-done.19.refs_4_, ...), custom_call_target="tpu_custom_call" | custom-call | flops 8053063680 | bytes 26214400 | tf_op jit(solution)/shard_map/expert_rows/pallas_call | solution.py:394
  149.8 9.2 %attend.1 = (bf16[2,64,640]{2,1,0:T(8,128)(2,1)S(1)}, bf16[2,64,640]{2,1,0:T(8,128)(2,1)S(1)}, bf16[2,64,640]{2,1,0:T(8,128)(2,1)S(1)}, bf16[2,64,640]{2,1,0:T(8,128)(2,1)S(1)}) custom-call(s32[4]{0:T(128)S(1)} %pad_add_fusion.2.where, bf16[2,64,640]{2,1,0:T(8,128)(2,1)S(1)} %get-tuple-element.42.q0, bf16[2,64,640]{2,1,0:T(8,128)(2,1)S(1)} %collective-permute-done.q1, ...), custom_call_target="tpu_custom_call" | custom-call | flops 2200000000 | bytes 4194304 | tf_op jit(solution)/shard_map/attend/pallas_call | solution.py:267
  162.8 2.5 %collective-permute-start.24 = (bf16[2,64,640]{2,1,0:T(8,128)(2,1)S(1)}, bf16[2,64,640]{2,1,0:T(8,128)(2,1)S(1)}, u32[]{:S(2)}, u32[]{:S(2)}) collective-permute-start(bf16[2,64,640]{2,1,0:T(8,128)(2,1)S(1)} %get-tuple-element.54), channel_id=1, source_target_pairs={{0,4},{1,5},{2,6},{3,7},{4,8},{5,9},{6,10},{7,11},{8,12},{9,13},{1... | collective-permute-start | bytes 491528 | tf_op jit(solution)/shard_map/ppermute | solution.py:325
  165.3 2.7 %collective-permute-done.23.refs_2_ = bf16[2,64,640]{2,1,0:T(8,128)(2,1)S(1)} collective-permute-done((bf16[2,64,640]{2,1,0:T(8,128)(2,1)S(1)}, bf16[2,64,640]{2,1,0:T(8,128)(2,1)S(1)}, u32[]{:S(2)}, u32[]{:S(2)}) %collective-permute-start.23) | collective-permute-done | bytes 163872 | tf_op jit(solution)/shard_map/ppermute | solution.py:325
  170.3 42.5 %reduce-scatter.2.cloned.1.call-done = bf16[64,5120]{1,0:T(8,128)(2,1)} async-done(((bf16[512,5120]{1,0:T(8,128)(2,1)}), bf16[64,5120]{1,0:T(8,128)(2,1)}) %reduce-scatter.2.cloned.1.call-update) | async-done | bytes 655376 | tf_op jit(solution)/shard_map/reduce_scatter | solution.py:476
  214.4 18.5 %all_to_all.11 = bf16[16,4,5120]{2,1,0:T(4,128)(2,1)S(1)} all-to-all(bf16[16,4,5120]{2,1,0:T(4,128)(2,1)S(1)} %reshape.199), channel_id=1, replica_groups=mesh['ctx'=16,'exp'=16] {'exp'}, dimensions={0} | all-to-all | bytes 1310720 | tf_op jit(solution)/shard_map/all_to_all | solution.py:481
  (74 shorter events, 29.9 us)
Async XLA Ops:
  7.2 122.5 %all-gather.2.cloned.1.call-start = ((), (), s32[]{:S(2)}) async-start(), calls=%async_computation.3 | async-start | bytes 5898240 | tf_op jit(solution)/shard_map/all_gather | solution.py:471
  31.2 181.7 %reduce-scatter.2.cloned.1.call-start = ((), (), s32[]{:S(2)}) async-start(), calls=%async_computation.4 | async-start | bytes 5898240 | tf_op jit(solution)/shard_map/reduce_scatter | solution.py:476
  31.3 10.0 %collective-permute-start.7 = (bf16[2,64,1024]{2,1,0:T(8,128)(2,1)S(1)}, bf16[2,64,1024]{2,1,0:T(8,128)(2,1)S(1)}, u32[]{:S(2)}, u32[]{:S(2)}) collective-permute-start(bf16[2,64,1024]{2,1,0:T(8,128)(2,1)S(1)} %pair_rows.1.refs_0_.own), channel_id=1, source_target_pairs={{0,224},{16,240},{32,0},{48,16},{64,32},{80,48},{96,64},{112,80},{... | collective-permute-start | bytes 786440 | tf_op jit(solution)/shard_map/ppermute | solution.py:68
  37.2 7.8 %collective-permute-start.3 = (bf16[2,64,1024]{2,1,0:T(8,128)(2,1)S(1)}, bf16[2,64,1024]{2,1,0:T(8,128)(2,1)S(1)}, u32[]{:S(2)}, u32[]{:S(2)}) collective-permute-start(bf16[2,64,1024]{2,1,0:T(8,128)(2,1)S(1)} %pair_rows.1.refs_0_.own), channel_id=1, source_target_pairs={{0,32},{16,48},{32,64},{48,80},{64,96},{80,112},{96,128},{112,144}... | collective-permute-start | bytes 786440 | tf_op jit(solution)/shard_map/ppermute | solution.py:64
  37.2 92.5 %collective-permute-start.19 = (bf16[5120,256]{1,0:T(8,128)(2,1)}, bf16[5120,256]{1,0:T(8,128)(2,1)}, u32[]{:S(2)}, u32[]{:S(2)}) collective-permute-start(bf16[5120,256]{1,0:T(8,128)(2,1)} %bitcast.27), channel_id=1, source_target_pairs={{0,16},{16,0},{32,48},{48,32},{64,80},{80,64},{96,112},{112,96},{1... | collective-permute-start | bytes 7864328 | tf_op jit(solution)/shard_map/ppermute | solution.py:462
  37.2 92.5 %collective-permute-start.20 = (bf16[5120,256]{1,0:T(8,128)(2,1)}, bf16[5120,256]{1,0:T(8,128)(2,1)}, u32[]{:S(2)}, u32[]{:S(2)}) collective-permute-start(bf16[5120,256]{1,0:T(8,128)(2,1)} %bitcast.29), channel_id=1, source_target_pairs={{0,16},{16,0},{32,48},{48,32},{64,80},{80,64},{96,112},{112,96},{1... | collective-permute-start | bytes 7864328 | tf_op jit(solution)/shard_map/ppermute | solution.py:462
  37.7 92.0 %collective-permute-start.21 = (bf16[256,5120]{1,0:T(8,128)(2,1)}, bf16[256,5120]{1,0:T(8,128)(2,1)}, u32[]{:S(2)}, u32[]{:S(2)}) collective-permute-start(bf16[256,5120]{1,0:T(8,128)(2,1)} %bitcast.31), channel_id=1, source_target_pairs={{0,16},{16,0},{32,48},{48,32},{64,80},{80,64},{96,112},{112,96},{1... | collective-permute-start | bytes 7864328 | tf_op jit(solution)/shard_map/ppermute | solution.py:462
  41.3 14.6 %collective-permute-start.8 = (bf16[2,64,1024]{2,1,0:T(8,128)(2,1)S(1)}, bf16[2,64,1024]{2,1,0:T(8,128)(2,1)S(1)}, u32[]{:S(2)}, u32[]{:S(2)}) collective-permute-start(bf16[2,64,1024]{2,1,0:T(8,128)(2,1)S(1)} %collective-permute-done.7.refs_8_), channel_id=1, source_target_pairs={{0,224},{16,240},{32,0},{48,16},{64,32},{80,48},{96,64},{112,80},{... | collective-permute-start | bytes 786440 | tf_op jit(solution)/shard_map/ppermute | solution.py:68
  45.0 14.6 %collective-permute-start.4 = (bf16[2,64,1024]{2,1,0:T(8,128)(2,1)S(1)}, bf16[2,64,1024]{2,1,0:T(8,128)(2,1)S(1)}, u32[]{:S(2)}, u32[]{:S(2)}) collective-permute-start(bf16[2,64,1024]{2,1,0:T(8,128)(2,1)S(1)} %collective-permute-done.3.refs_1_), channel_id=1, source_target_pairs={{0,32},{16,48},{32,64},{48,80},{64,96},{80,112},{96,128},{112,144}... | collective-permute-start | bytes 786440 | tf_op jit(solution)/shard_map/ppermute | solution.py:64
  56.0 14.6 %collective-permute-start.9 = (bf16[2,64,1024]{2,1,0:T(8,128)(2,1)S(1)}, bf16[2,64,1024]{2,1,0:T(8,128)(2,1)S(1)}, u32[]{:S(2)}, u32[]{:S(2)}) collective-permute-start(bf16[2,64,1024]{2,1,0:T(8,128)(2,1)S(1)} %collective-permute-done.8.refs_7_), channel_id=1, source_target_pairs={{0,224},{16,240},{32,0},{48,16},{64,32},{80,48},{96,64},{112,80},{... | collective-permute-start | bytes 786440 | tf_op jit(solution)/shard_map/ppermute | solution.py:68
  59.6 14.7 %collective-permute-start.5 = (bf16[2,64,1024]{2,1,0:T(8,128)(2,1)S(1)}, bf16[2,64,1024]{2,1,0:T(8,128)(2,1)S(1)}, u32[]{:S(2)}, u32[]{:S(2)}) collective-permute-start(bf16[2,64,1024]{2,1,0:T(8,128)(2,1)S(1)} %collective-permute-done.4.refs_2_), channel_id=1, source_target_pairs={{0,32},{16,48},{32,64},{48,80},{64,96},{80,112},{96,128},{112,144}... | collective-permute-start | bytes 786440 | tf_op jit(solution)/shard_map/ppermute | solution.py:64
  70.6 9.0 %collective-permute-start.10 = (bf16[1,64,1024]{2,1,0:T(8,128)(2,1)S(1)}, bf16[1,64,1024]{2,1,0:T(8,128)(2,1)S(1)}, u32[]{:S(2)}, u32[]{:S(2)}) collective-permute-start(bf16[1,64,1024]{2,1,0:T(8,128)(2,1)S(1)} %slice.35), channel_id=1, source_target_pairs={{0,224},{16,240},{32,0},{48,16},{64,32},{80,48},{96,64},{112,80},{... | collective-permute-start | bytes 393224 | tf_op jit(solution)/shard_map/ppermute | solution.py:68
  74.4 9.0 %collective-permute-start.6 = (bf16[1,64,1024]{2,1,0:T(8,128)(2,1)S(1)}, bf16[1,64,1024]{2,1,0:T(8,128)(2,1)S(1)}, u32[]{:S(2)}, u32[]{:S(2)}) collective-permute-start(bf16[1,64,1024]{2,1,0:T(8,128)(2,1)S(1)} %slice.34), channel_id=1, source_target_pairs={{0,32},{16,48},{32,64},{48,80},{64,96},{80,112},{96,128},{112,144}... | collective-permute-start | bytes 393224 | tf_op jit(solution)/shard_map/ppermute | solution.py:64
  86.4 6.4 %collective-permute-start.12 = (bf16[4,64,256]{2,1,0:T(8,128)(2,1)S(1)}, bf16[4,64,256]{2,1,0:T(8,128)(2,1)S(1)}, u32[]{:S(2)}, u32[]{:S(2)}) collective-permute-start(bf16[4,64,256]{2,1,0:T(8,128)(2,1)S(1)} %get-tuple-element.38), channel_id=1, source_target_pairs={{0,4},{1,5},{2,6},{3,7},{4,8},{5,9},{6,10},{7,11},{8,12},{9,13},{1... | collective-permute-start | bytes 393224 | tf_op jit(solution)/shard_map/ppermute | solution.py:313
  87.4 6.8 %collective-permute-start.13 = (bf16[4,64,256]{2,1,0:T(8,128)(2,1)S(1)}, bf16[4,64,256]{2,1,0:T(8,128)(2,1)S(1)}, u32[]{:S(2)}, u32[]{:S(2)}) collective-permute-start(bf16[4,64,256]{2,1,0:T(8,128)(2,1)S(1)} %get-tuple-element.39), channel_id=1, source_target_pairs={{0,8},{1,9},{2,10},{3,11},{4,12},{5,13},{6,14},{7,15},{8,0},{9,1},... | collective-permute-start | bytes 393224 | tf_op jit(solution)/shard_map/ppermute | solution.py:313
  92.8 9.3 %collective-permute-start = (bf16[2,64,640]{2,1,0:T(8,128)(2,1)S(1)}, bf16[2,64,640]{2,1,0:T(8,128)(2,1)S(1)}, u32[]{:S(2)}, u32[]{:S(2)}) collective-permute-start(bf16[2,64,640]{2,1,0:T(8,128)(2,1)S(1)} %get-tuple-element.32), channel_id=1, source_target_pairs={{0,4},{1,5},{2,6},{3,7},{4,8},{5,9},{6,10},{7,11},{8,12},{9,13},{1... | collective-permute-start | bytes 491528 | tf_op jit(solution)/shard_map/ppermute | solution.py:312
  94.1 6.3 %collective-permute-start.14 = (bf16[4,64,256]{2,1,0:T(8,128)(2,1)S(1)}, bf16[4,64,256]{2,1,0:T(8,128)(2,1)S(1)}, u32[]{:S(2)}, u32[]{:S(2)}) collective-permute-start(bf16[4,64,256]{2,1,0:T(8,128)(2,1)S(1)} %get-tuple-element.40), channel_id=1, source_target_pairs={{0,12},{1,13},{2,14},{3,15},{4,0},{5,1},{6,2},{7,3},{8,4},{9,5},{1... | collective-permute-start | bytes 393224 | tf_op jit(solution)/shard_map/ppermute | solution.py:313
  101.0 11.7 %collective-permute-start.16 = (bf16[4,4,64,256]{3,2,1,0:T(8,128)(2,1)S(1)}, bf16[4,4,64,256]{3,2,1,0:T(8,128)(2,1)S(1)}, u32[]{:S(2)}, u32[]{:S(2)}) collective-permute-start(bf16[4,4,64,256]{3,2,1,0:T(8,128)(2,1)S(1)} %stack_sources.1), channel_id=1, source_target_pairs={{0,3},{1,0},{2,1},{3,2},{4,7},{5,4},{6,5},{7,6},{8,11},{9,8},{10,9... | collective-permute-start | bytes 1572872 | tf_op jit(solution)/shard_map/ppermute | solution.py:316
  102.1 14.7 %collective-permute-start.15 = (bf16[4,4,64,256]{3,2,1,0:T(8,128)(2,1)S(1)}, bf16[4,4,64,256]{3,2,1,0:T(8,128)(2,1)S(1)}, u32[]{:S(2)}, u32[]{:S(2)}) collective-permute-start(bf16[4,4,64,256]{3,2,1,0:T(8,128)(2,1)S(1)} %stack_sources.1), channel_id=1, source_target_pairs={{0,1},{1,2},{2,3},{3,0},{4,5},{5,6},{6,7},{7,4},{8,9},{9,10},{10,1... | collective-permute-start | bytes 1572872 | tf_op jit(solution)/shard_map/ppermute | solution.py:315
  112.7 7.4 %collective-permute-start.1 = (bf16[2,64,640]{2,1,0:T(8,128)(2,1)S(1)}, bf16[2,64,640]{2,1,0:T(8,128)(2,1)S(1)}, u32[]{:S(2)}, u32[]{:S(2)}) collective-permute-start(bf16[2,64,640]{2,1,0:T(8,128)(2,1)S(1)} %get-tuple-element.33), channel_id=1, source_target_pairs={{0,8},{1,9},{2,10},{3,11},{4,12},{5,13},{6,14},{7,15},{8,0},{9,1},... | collective-permute-start | bytes 491528 | tf_op jit(solution)/shard_map/ppermute | solution.py:312
  120.1 6.4 %collective-permute-start.18 = (bf16[2,4,64,256]{3,2,1,0:T(8,128)(2,1)S(1)}, bf16[2,4,64,256]{3,2,1,0:T(8,128)(2,1)S(1)}, u32[]{:S(2)}, u32[]{:S(2)}) collective-permute-start(bf16[2,4,64,256]{3,2,1,0:T(8,128)(2,1)S(1)} %slice.37), channel_id=1, source_target_pairs={{0,3},{1,0},{2,1},{3,2},{4,7},{5,4},{6,5},{7,6},{8,11},{9,8},{10,9... | collective-permute-start | bytes 786440 | tf_op jit(solution)/shard_map/ppermute | solution.py:318
  122.1 7.6 %collective-permute-start.17 = (bf16[2,4,64,256]{3,2,1,0:T(8,128)(2,1)S(1)}, bf16[2,4,64,256]{3,2,1,0:T(8,128)(2,1)S(1)}, u32[]{:S(2)}, u32[]{:S(2)}) collective-permute-start(bf16[2,4,64,256]{3,2,1,0:T(8,128)(2,1)S(1)} %slice.36), channel_id=1, source_target_pairs={{0,1},{1,2},{2,3},{3,0},{4,5},{5,6},{6,7},{7,4},{8,9},{9,10},{10,1... | collective-permute-start | bytes 786440 | tf_op jit(solution)/shard_map/ppermute | solution.py:317
  159.0 6.3 %collective-permute-start.22 = (bf16[2,64,640]{2,1,0:T(8,128)(2,1)S(1)}, bf16[2,64,640]{2,1,0:T(8,128)(2,1)S(1)}, u32[]{:S(2)}, u32[]{:S(2)}) collective-permute-start(bf16[2,64,640]{2,1,0:T(8,128)(2,1)S(1)} %get-tuple-element.52), channel_id=1, source_target_pairs={{0,12},{1,13},{2,14},{3,15},{4,0},{5,1},{6,2},{7,3},{8,4},{9,5},{1... | collective-permute-start | bytes 491528 | tf_op jit(solution)/shard_map/ppermute | solution.py:325
  161.2 6.8 %collective-permute-start.23 = (bf16[2,64,640]{2,1,0:T(8,128)(2,1)S(1)}, bf16[2,64,640]{2,1,0:T(8,128)(2,1)S(1)}, u32[]{:S(2)}, u32[]{:S(2)}) collective-permute-start(bf16[2,64,640]{2,1,0:T(8,128)(2,1)S(1)} %get-tuple-element.53), channel_id=1, source_target_pairs={{0,8},{1,9},{2,10},{3,11},{4,12},{5,13},{6,14},{7,15},{8,0},{9,1},... | collective-permute-start | bytes 491528 | tf_op jit(solution)/shard_map/ppermute | solution.py:325
  (8 other events, 165.7 us)
Sparse Core Ops, SparseCore 0:
  31.3 78.4 all-gather.1
  149.8 62.9 reduce-scatter.1

commit v4 on v3

--- a/solution.py
+++ b/solution.py
@@ -80,11 +80,16 @@
         theirs[i] = held[table[2 + i]]
 
 
-def choose_blocks(paired, table):
+def pass_blocks(paired):
     below, above = [paired], [paired]
     for _ in range(3):
         below.append(up_z(below[-1]))
         above.append(down_z(above[-1]))
+    return below, above
+
+
+def choose_blocks(below, above, table):
+    paired = below[0]
     far_low, far_high = up_z(below[3][:1]), down_z(above[3][1:])
     out = jax.ShapeDtypeStruct(paired.shape, paired.dtype)
     held = pltpu.VMEM((16,) + paired.shape[1:], paired.dtype)
@@ -283,7 +288,7 @@
     )(where, *qs, *rs)
 
 
-def exchange_rows(queries, key_states, value_state_rows, block_lists):
+def exchange_rows(queries, below, above, block_lists):
     ctx_count = lax.axis_size("ctx")
     blocks_total = 2 * ctx_count
     ctx_index = lax.axis_index("ctx")
@@ -302,8 +307,8 @@
     chosen = (2 * distance + (listed >= ctx_count).astype(jnp.int32)).astype(jnp.int32)
     local = (lax.rem(holder, 2) == core).astype(jnp.int32)
 
-    paired = pair_rows(key_states, value_state_rows)
-    mine, theirs = choose_blocks(paired, chosen)
+    paired = below[0]
+    mine, theirs = choose_blocks(below, above, chosen)
     swapped = lax.ppermute(theirs, "ctx", CORE_SWAP)
     picked = pick_heads(
         paired, mine, swapped, jnp.concatenate([x[None], local[:2]]).astype(jnp.int32)
@@ -384,7 +389,7 @@
         copy.wait()
 
 
-def expert_rows(xs, weights, step=256):
+def expert_rows(xs, weights, step=512):
     width = xs[0].shape[1]
     hidden = weights[0].shape[1]
     tokens = sum(x.shape[0] for x in xs)
@@ -416,50 +421,42 @@
     )(*xs, *weights)
 
 
-def slot_kernel(hidden, router, ids, slots, out, places):
-    experts = router.shape[1]
-    tokens, capacity = hidden.shape[0], slots // experts
-    logits = jnp.dot(hidden[...], router[...], preferred_element_type=jnp.float32)
-    column = lax.broadcasted_iota(jnp.int32, (tokens, experts), 1)
-    onehot = jnp.where(ids[...] == column, 1.0, 0.0)
-    gate_score = 1.0 / (1.0 + jnp.exp(-jnp.sum(logits * onehot, axis=1, keepdims=True)))
+def slot_kernel(hidden, router, ids, out, places):
+    experts, tokens, slots = router.shape[0], hidden.shape[0], out.shape[0]
+    logits = lax.dot_general(router[...], hidden[...], NT, preferred_element_type=jnp.float32)
+    named = ids[...] == lax.broadcasted_iota(jnp.int32, (experts, tokens), 0)
+    onehot = jnp.where(named, 1.0, 0.0)
+    gate_row = 1.0 / (1.0 + jnp.exp(-jnp.sum(logits * onehot, axis=0, keepdims=True)))
     row = lax.broadcasted_iota(jnp.int32, (tokens, tokens), 0)
-    earlier = lax.broadcasted_iota(jnp.int32, (tokens, tokens), 1)
-    upto = jnp.where(earlier <= row, 1.0, 0.0).astype(jnp.bfloat16)
-    counts = jnp.dot(upto, onehot.astype(jnp.bfloat16), preferred_element_type=jnp.float32)
-    rank = jnp.sum(counts * onehot, axis=1, keepdims=True) - 1.0
-    slot = ids[...] * capacity + rank.astype(jnp.int32)
-    target = lax.broadcasted_iota(jnp.int32, (tokens, slots), 1)
+    column = lax.broadcasted_iota(jnp.int32, (tokens, tokens), 1)
+    upto = jnp.where(row <= column, 1.0, 0.0).astype(jnp.bfloat16)
+    counts = jnp.dot(onehot.astype(jnp.bfloat16), upto, preferred_element_type=jnp.float32)
+    rank = jnp.sum(counts * onehot, axis=0, keepdims=True) - 1.0
+    slot = ids[...] * (slots // experts) + rank.astype(jnp.int32)
+    target = lax.broadcasted_iota(jnp.int32, (slots, tokens), 0)
     place = jnp.where(slot == target, 1.0, 0.0).astype(jnp.bfloat16)
     places[...] = place
+    gate_score = jnp.sum(jnp.where(row == column, gate_row, 0.0), axis=1, keepdims=True)
     scaled = (hidden[...].astype(jnp.float32) * gate_score).astype(jnp.bfloat16)
-    out[...] = lax.dot_general(
-        place, scaled, (((0,), (0,)), ((), ())), preferred_element_type=jnp.float32
-    ).astype(jnp.bfloat16)
+    out[...] = jnp.dot(place, scaled, preferred_element_type=jnp.float32).astype(jnp.bfloat16)
 
 
 def fill_slots(hidden, router, expert_ids, slots):
     tokens, width = hidden.shape
     outs = [
         jax.ShapeDtypeStruct((slots, width), jnp.bfloat16),
-        jax.ShapeDtypeStruct((tokens, slots), jnp.bfloat16),
+        jax.ShapeDtypeStruct((slots, tokens), jnp.bfloat16),
     ]
-
-    def kernel(a, b, c, out, places):
-        slot_kernel(a, b, c, slots, out, places)
-
-    call = small(kernel, outs, "fill_slots", 1 << 20)
-    return call(in_specs=[WHOLE] * 3, out_specs=[WHOLE] * 2)(hidden, router, expert_ids)
-
-
-def route_experts(hidden, router, expert_ids, w_gate, w_up, w_down, exchanged, attend_rows):
+    call = small(slot_kernel, outs, "fill_slots", 1 << 20)
+    return call(in_specs=[WHOLE] * 3, out_specs=[WHOLE] * 2)(hidden, router.T, expert_ids.T)
+
+
+def send_tokens(hidden, router, expert_ids):
     expert_table = router.shape[1]
     local_tokens = hidden.shape[0]
     model_width = hidden.shape[1]
     capacity = max(2, 2 * local_tokens // expert_table)
     exp_count = lax.axis_size("exp")
-    own = (w_gate[0], w_up[0], w_down[0])
-    other = tuple(lax.ppermute(w, "ctx", CORE_SWAP) for w in own)
     outgoing, places = fill_slots(hidden, router, expert_ids, expert_table * capacity)
     incoming = lax.all_to_all(
         outgoing.reshape(exp_count, capacity, model_width),
@@ -468,8 +465,16 @@
         concat_axis=0,
         tiled=True,
     )
+    return incoming.reshape(-1, model_width), places
+
+
+def route_experts(incoming, places, w_gate, w_up, w_down, exchanged, attend_rows):
+    model_width = incoming.shape[1]
+    exp_count = lax.axis_size("exp")
+    own = (w_gate[0], w_up[0], w_down[0])
+    other = tuple(lax.ppermute(w, "ctx", CORE_SWAP) for w in own)
     rows = lax.all_gather(
-        incoming.reshape(-1, model_width), "ctx", axis=0, tiled=True, axis_index_groups=RINGS
+        incoming, "ctx", axis=0, tiled=True, axis_index_groups=RINGS
     )
     rows, exchanged = lax.optimization_barrier((rows, exchanged))
     (partial,) = expert_rows([rows], own + other)
@@ -479,14 +484,17 @@
     attention = attend_rows(*exchanged)
     summed_output, attention = lax.optimization_barrier((summed_output, attention))
     returned = lax.all_to_all(
-        summed_output.reshape(exp_count, capacity, model_width),
+        summed_output.reshape(exp_count, -1, model_width),
         "exp",
         split_axis=0,
         concat_axis=0,
         tiled=True,
     )
-    moe_out = jnp.dot(
-        places, returned.reshape(-1, model_width), preferred_element_type=jnp.float32
+    moe_out = lax.dot_general(
+        places,
+        returned.reshape(-1, model_width),
+        (((0,), (0,)), ((), ())),
+        preferred_element_type=jnp.float32,
     ).astype(jnp.bfloat16)
     return attention, moe_out
 
@@ -503,11 +511,13 @@
     w_up,
     w_down,
 ):
-    where, state, qs, rs = exchange_rows(queries, key_states, value_state_rows, block_lists)
+    below, above = pass_blocks(pair_rows(key_states, value_state_rows))
+    incoming, places = send_tokens(hidden, router, expert_ids)
+    incoming, below, above = lax.optimization_barrier((incoming, below, above))
+    where, state, qs, rs = exchange_rows(queries, below, above, block_lists)
     attention, moe_out = route_experts(
-        hidden,
-        router,
-        expert_ids,
+        incoming,
+        places,
         w_gate,
         w_up,
         w_down,

time: 242 us -> 225 us (0.930)
  blocking collectives: 37.1 us -> 18.5 us
  waiting for transfers between devices: 105 us -> 96.4 us
  starting transfers between devices: 41.8 us -> 46.7 us
  Pallas kernels: 34.1 us -> 37.8 us
    all_to_all x2 -> x1, blocking collectives: 37.1 us -> 18.5 us  [route_experts(): lax.all_to_all(summed_output.reshape(exp_count, -1, model_width), 'exp',...]
    ppermute x4, waiting for transfers between devices: 29.7 us -> 11.1 us  [down_z(): return lax.ppermute(v, 'ctx', ring(-1))]
    all_to_all x0 -> x1, starting transfers between devices: none -> 7.48 us  [send_tokens(): lax.all_to_all(outgoing.reshape(exp_count, capacity, model_width), 'exp',...]
    ppermute x4, starting transfers between devices: 17.1 us -> 13 us  [down_z(): return lax.ppermute(v, 'ctx', ring(-1))]
    pallas_call x1, Pallas kernels: 20 us -> 23.7 us  [expert_rows(): pl.pallas_call(lambda *refs: ffn_kernel(len(xs), refs), in_specs=[far] *...]
    all_gather x1, waiting for transfers between devices: 0.01 us -> 3.53 us  [route_experts(): lax.all_gather(incoming, 'ctx', axis=0, tiled=True, axis_index_groups=RINGS)]
    ppermute x3, waiting for transfers between devices: 3.59 us -> 6.52 us  [attend_all(): lax.ppermute(outs[d], 'exp', shift_x(-d))]
  transfers between devices with their start and end apart: 27 -> 28, of which waited for: 17 -> 19; matrix products, arithmetic and copies ran while one was open for 0% -> 1% of each run, Pallas kernels for 6% -> 6%
where the time goes in v4:
time: 225 us; the launch traced here: 224 us
  waiting for transfers between devices  96.4 us (43%)
  starting transfers between devices  46.7 us (21%)
  Pallas kernels  37.8 us (17%)
  blocking collectives  18.5 us (8%)
  between operations  14.2 us (6%)
  local copies, waits for them, and re-layouts  8.87 us (4%)
    reduce_scatter x1, waiting for transfers between devices, route_experts(): lax.psum_scatter(partial, 'ctx', scatter_dimension=0, tiled=True, axis_in...  41.9 us
    pallas_call x1, Pallas kernels, expert_rows(): pl.pallas_call(lambda *refs: ffn_kernel(len(xs), refs), in_specs=[far] *...  23.7 us
    all_to_all x1, blocking collectives, route_experts(): lax.all_to_all(summed_output.reshape(exp_count, -1, model_width), 'exp',...  18.5 us
    ppermute x4, starting transfers between devices, down_z(): return lax.ppermute(v, 'ctx', ring(-1))  13 us
    ppermute x4, waiting for transfers between devices, down_z(): return lax.ppermute(v, 'ctx', ring(-1))  11.1 us
    pallas_call x1, Pallas kernels, attend(): pl.pallas_call(attend_kernel, grid_spec=pltpu.PrefetchScalarGridSpec(num_...  9.24 us
    ppermute x1, waiting for transfers between devices, exchange_rows(): r2 = lax.ppermute(r0, 'exp', shift_y(-1))  9.06 us
    all_to_all x1, starting transfers between devices, send_tokens(): lax.all_to_all(outgoing.reshape(exp_count, capacity, model_width), 'exp',...  7.48 us
  transfers between devices with their start and end apart: 28, of which 19 were waited for; matrix products, arithmetic and copies ran while one was open for 1% of the time, Pallas kernels for 6%

profile of v4, /device:TPU:2, one launch (start us, length us, event | category | flops | bytes accessed | tf_op | source)
XLA Modules:
  0.0 223.9 jit_solution(1887301000426484031)
XLA Ops:
  9.1 5.9 %collective-permute-start.3 = (bf16[2,64,1024]{2,1,0:T(8,128)(2,1)S(1)}, bf16[2,64,1024]{2,1,0:T(8,128)(2,1)S(1)}, u32[]{:S(2)}, u32[]{:S(2)}) collective-permute-start(bf16[2,64,1024]{2,1,0:T(8,128)(2,1)S(1)} %pair_rows.1.refs_0_.own), channel_id=1, source_target_pairs={{0,224},{16,240},{32,0},{48,16},{64,32},{80,48},{96,64},{112,80},{... | collective-permute-start | bytes 786440 | tf_op jit(solution)/shard_map/ppermute | solution.py:68
  19.4 7.5 %all-to-all-start = ((bf16[16,4,5120]{2,1,0:T(4,128)(2,1)}), bf16[16,4,5120]{2,1,0:T(4,128)(2,1)S(1)}, u32[]{:S(2)}, u32[]{:S(2)}) async-start(bf16[16,4,5120]{2,1,0:T(4,128)(2,1)} %reshape.192), calls=%async_computation | async-start | bytes 1310720 | tf_op jit(solution)/shard_map/all_to_all | solution.py:461
  27.0 3.3 %collective-permute-start.4 = (bf16[2,64,1024]{2,1,0:T(8,128)(2,1)S(1)}, bf16[2,64,1024]{2,1,0:T(8,128)(2,1)S(1)}, u32[]{:S(2)}, u32[]{:S(2)}) collective-permute-start(bf16[2,64,1024]{2,1,0:T(8,128)(2,1)S(1)} %collective-permute-done.3.refs_8_), channel_id=1, source_target_pairs={{0,224},{16,240},{32,0},{48,16},{64,32},{80,48},{96,64},{112,80},{... | collective-permute-start | bytes 786440 | tf_op jit(solution)/shard_map/ppermute | solution.py:68
  30.3 4.4 %collective-permute-done.4.refs_7_ = bf16[2,64,1024]{2,1,0:T(8,128)(2,1)S(1)} collective-permute-done((bf16[2,64,1024]{2,1,0:T(8,128)(2,1)S(1)}, bf16[2,64,1024]{2,1,0:T(8,128)(2,1)S(1)}, u32[]{:S(2)}, u32[]{:S(2)}) %collective-permute-start.4) | collective-permute-done | bytes 262176 | tf_op jit(solution)/shard_map/ppermute | solution.py:68
  34.7 3.7 %collective-permute-start.5 = (bf16[2,64,1024]{2,1,0:T(8,128)(2,1)S(1)}, bf16[2,64,1024]{2,1,0:T(8,128)(2,1)S(1)}, u32[]{:S(2)}, u32[]{:S(2)}) collective-permute-start(bf16[2,64,1024]{2,1,0:T(8,128)(2,1)S(1)} %collective-permute-done.4.refs_7_), channel_id=1, source_target_pairs={{0,224},{16,240},{32,0},{48,16},{64,32},{80,48},{96,64},{112,80},{... | collective-permute-start | bytes 786440 | tf_op jit(solution)/shard_map/ppermute | solution.py:68
  39.4 2.9 %collective-permute-done.5.refs_6_ = bf16[2,64,1024]{2,1,0:T(8,128)(2,1)S(1)} collective-permute-done((bf16[2,64,1024]{2,1,0:T(8,128)(2,1)S(1)}, bf16[2,64,1024]{2,1,0:T(8,128)(2,1)S(1)}, u32[]{:S(2)}, u32[]{:S(2)}) %collective-permute-start.5) | collective-permute-done | bytes 262176 | tf_op jit(solution)/shard_map/ppermute | solution.py:68
  42.3 3.7 %collective-permute-done.2.refs_3_ = bf16[2,64,1024]{2,1,0:T(8,128)(2,1)S(1)} collective-permute-done((bf16[2,64,1024]{2,1,0:T(8,128)(2,1)S(1)}, bf16[2,64,1024]{2,1,0:T(8,128)(2,1)S(1)}, u32[]{:S(2)}, u32[]{:S(2)}) %collective-permute-start.2) | collective-permute-done | bytes 262176 | tf_op jit(solution)/shard_map/ppermute | solution.py:64
  49.7 3.8 %collective-permute-done.10.refs_5_ = bf16[1,64,1024]{2,1,0:T(8,128)(2,1)S(1)} collective-permute-done((bf16[1,64,1024]{2,1,0:T(8,128)(2,1)S(1)}, bf16[1,64,1024]{2,1,0:T(8,128)(2,1)S(1)}, u32[]{:S(2)}, u32[]{:S(2)}) %collective-permute-start.10) | collective-permute-done | bytes 131104 | tf_op jit(solution)/shard_map/ppermute | solution.py:68
  55.7 3.2 %collective-permute-done.11.swapped = bf16[2,64,1024]{2,1,0:T(8,128)(2,1)S(1)} collective-permute-done((bf16[2,64,1024]{2,1,0:T(8,128)(2,1)S(1)}, bf16[2,64,1024]{2,1,0:T(8,128)(2,1)S(1)}, u32[]{:S(2)}, u32[]{:S(2)}) %collective-permute-start.11) | collective-permute-done | bytes 262176 | tf_op jit(solution)/shard_map/ppermute | solution.py:312
  62.8 2.7 %collective-permute-done.12.refs_1_ = bf16[4,64,256]{2,1,0:T(8,128)(2,1)S(1)} collective-permute-done((bf16[4,64,256]{2,1,0:T(8,128)(2,1)S(1)}, bf16[4,64,256]{2,1,0:T(8,128)(2,1)S(1)}, u32[]{:S(2)}, u32[]{:S(2)}) %collective-permute-start.12) | collective-permute-done | bytes 131104 | tf_op jit(solution)/shard_map/ppermute | solution.py:318
  67.9 3.5 %collective-permute-start.14 = (bf16[4,64,256]{2,1,0:T(8,128)(2,1)S(1)}, bf16[4,64,256]{2,1,0:T(8,128)(2,1)S(1)}, u32[]{:S(2)}, u32[]{:S(2)}) collective-permute-start(bf16[4,64,256]{2,1,0:T(8,128)(2,1)S(1)} %get-tuple-element.56), channel_id=1, source_target_pairs={{0,12},{1,13},{2,14},{3,15},{4,0},{5,1},{6,2},{7,3},{8,4},{9,5},{1... | collective-permute-start | bytes 393224 | tf_op jit(solution)/shard_map/ppermute | solution.py:318
  74.5 2.8 %collective-permute-start.16 = (bf16[4,4,64,256]{3,2,1,0:T(8,128)(2,1)S(1)}, bf16[4,4,64,256]{3,2,1,0:T(8,128)(2,1)S(1)}, u32[]{:S(2)}, u32[]{:S(2)}) collective-permute-start(bf16[4,4,64,256]{3,2,1,0:T(8,128)(2,1)S(1)} %stack_sources.1), channel_id=1, source_target_pairs={{0,3},{1,0},{2,1},{3,2},{4,7},{5,4},{6,5},{7,6},{8,11},{9,8},{10,9... | collective-permute-start | bytes 1572872 | tf_op jit(solution)/shard_map/ppermute | solution.py:321
  77.3 9.1 %collective-permute-done.16 = bf16[4,4,64,256]{3,2,1,0:T(8,128)(2,1)S(1)} collective-permute-done((bf16[4,4,64,256]{3,2,1,0:T(8,128)(2,1)S(1)}, bf16[4,4,64,256]{3,2,1,0:T(8,128)(2,1)S(1)}, u32[]{:S(2)}, u32[]{:S(2)}) %collective-permute-start.16) | collective-permute-done | bytes 524320 | tf_op jit(solution)/shard_map/ppermute | solution.py:321
  86.4 2.9 %collective-permute-start.7 = (bf16[2,64,640]{2,1,0:T(8,128)(2,1)S(1)}, bf16[2,64,640]{2,1,0:T(8,128)(2,1)S(1)}, u32[]{:S(2)}, u32[]{:S(2)}) collective-permute-start(bf16[2,64,640]{2,1,0:T(8,128)(2,1)S(1)} %get-tuple-element.42), channel_id=1, source_target_pairs={{0,8},{1,9},{2,10},{3,11},{4,12},{5,13},{6,14},{7,15},{8,0},{9,1},... | collective-permute-start | bytes 491528 | tf_op jit(solution)/shard_map/ppermute | solution.py:317
  89.8 2.6 %collective-permute-start.8 = (bf16[2,64,640]{2,1,0:T(8,128)(2,1)S(1)}, bf16[2,64,640]{2,1,0:T(8,128)(2,1)S(1)}, u32[]{:S(2)}, u32[]{:S(2)}) collective-permute-start(bf16[2,64,640]{2,1,0:T(8,128)(2,1)S(1)} %get-tuple-element.43), channel_id=1, source_target_pairs={{0,12},{1,13},{2,14},{3,15},{4,0},{5,1},{6,2},{7,3},{8,4},{9,5},{1... | collective-permute-start | bytes 491528 | tf_op jit(solution)/shard_map/ppermute | solution.py:317
  94.1 2.8 %collective-permute-start.18 = (bf16[2,4,64,256]{3,2,1,0:T(8,128)(2,1)S(1)}, bf16[2,4,64,256]{3,2,1,0:T(8,128)(2,1)S(1)}, u32[]{:S(2)}, u32[]{:S(2)}) collective-permute-start(bf16[2,4,64,256]{3,2,1,0:T(8,128)(2,1)S(1)} %slice.35), channel_id=1, source_target_pairs={{0,3},{1,0},{2,1},{3,2},{4,7},{5,4},{6,5},{7,6},{8,11},{9,8},{10,9... | collective-permute-start | bytes 786440 | tf_op jit(solution)/shard_map/ppermute | solution.py:323
  96.9 3.9 %collective-permute-done.18 = bf16[2,4,64,256]{3,2,1,0:T(8,128)(2,1)S(1)} collective-permute-done((bf16[2,4,64,256]{3,2,1,0:T(8,128)(2,1)S(1)}, bf16[2,4,64,256]{3,2,1,0:T(8,128)(2,1)S(1)}, u32[]{:S(2)}, u32[]{:S(2)}) %collective-permute-start.18) | collective-permute-done | bytes 262176 | tf_op jit(solution)/shard_map/ppermute | solution.py:323
  100.8 3.7 %collective-permute-done.17 = bf16[2,4,64,256]{3,2,1,0:T(8,128)(2,1)S(1)} collective-permute-done((bf16[2,4,64,256]{3,2,1,0:T(8,128)(2,1)S(1)}, bf16[2,4,64,256]{3,2,1,0:T(8,128)(2,1)S(1)}, u32[]{:S(2)}, u32[]{:S(2)}) %collective-permute-start.17) | collective-permute-done | bytes 262176 | tf_op jit(solution)/shard_map/ppermute | solution.py:322
  104.5 3.5 %all-gather.2.cloned.1.call-done.refs_0_ = bf16[512,5120]{1,0:T(8,128)(2,1)} async-done(((bf16[64,5120]{1,0:T(8,128)(2,1)}), bf16[512,5120]{1,0:T(8,128)(2,1)}) %all-gather.2.cloned.1.call-update) | async-done | bytes 5242896 | tf_op jit(solution)/shard_map/all_gather | solution.py:476
  108.0 23.7 %expert_rows.1 = bf16[512,5120]{1,0:T(8,128)(2,1)} custom-call(bf16[512,5120]{1,0:T(8,128)(2,1)} %all-gather.2.cloned.1.call-done.refs_0_, bf16[5120,256]{1,0:T(8,128)(2,1)} %bitcast.32, bf16[5120,256]{1,0:T(8,128)(2,1)} %bitcast.34, bf16[256,5120]{1,0:T(8,128)(2,1)} %bitcast.36, bf16[5120,256]{1,0:T(8,128)(2,1)} %collective-permute-done.19.refs_4_, ...), custom_call_target="tpu_custom_call" | custom-call | flops 8053063680 | bytes 26214400 | tf_op jit(solution)/shard_map/expert_rows/pallas_call | solution.py:399
  131.9 9.2 %attend.1 = (bf16[2,64,640]{2,1,0:T(8,128)(2,1)S(1)}, bf16[2,64,640]{2,1,0:T(8,128)(2,1)S(1)}, bf16[2,64,640]{2,1,0:T(8,128)(2,1)S(1)}, bf16[2,64,640]{2,1,0:T(8,128)(2,1)S(1)}) custom-call(s32[4]{0:T(128)S(1)} %pad_add_fusion.2.where, bf16[2,64,640]{2,1,0:T(8,128)(2,1)S(1)} %get-tuple-element.58.q0, bf16[2,64,640]{2,1,0:T(8,128)(2,1)S(1)} %collective-permute-done.6.q1, ...), custom_call_target="tpu_custom_call" | custom-call | flops 2200000000 | bytes 4194304 | tf_op jit(solution)/shard_map/attend/pallas_call | solution.py:272
  147.4 4.2 %collective-permute-done.23.refs_2_ = bf16[2,64,640]{2,1,0:T(8,128)(2,1)S(1)} collective-permute-done((bf16[2,64,640]{2,1,0:T(8,128)(2,1)S(1)}, bf16[2,64,640]{2,1,0:T(8,128)(2,1)S(1)}, u32[]{:S(2)}, u32[]{:S(2)}) %collective-permute-start.23) | collective-permute-done | bytes 163872 | tf_op jit(solution)/shard_map/ppermute | solution.py:330
  153.9 41.9 %reduce-scatter.2.cloned.1.call-done = bf16[64,5120]{1,0:T(8,128)(2,1)} async-done(((bf16[512,5120]{1,0:T(8,128)(2,1)}), bf16[64,5120]{1,0:T(8,128)(2,1)}) %reduce-scatter.2.cloned.1.call-update) | async-done | bytes 655376 | tf_op jit(solution)/shard_map/reduce_scatter | solution.py:481
  197.4 18.5 %all_to_all.10 = bf16[16,4,5120]{2,1,0:T(4,128)(2,1)S(1)} all-to-all(bf16[16,4,5120]{2,1,0:T(4,128)(2,1)S(1)} %reshape.199), channel_id=1, replica_groups=mesh['ctx'=16,'exp'=16] {'exp'}, dimensions={0} | all-to-all | bytes 1310720 | tf_op jit(solution)/shard_map/all_to_all | solution.py:486
  (77 shorter events, 36.3 us)
Async XLA Ops:
  9.1 17.9 %collective-permute-start.3 = (bf16[2,64,1024]{2,1,0:T(8,128)(2,1)S(1)}, bf16[2,64,1024]{2,1,0:T(8,128)(2,1)S(1)}, u32[]{:S(2)}, u32[]{:S(2)}) collective-permute-start(bf16[2,64,1024]{2,1,0:T(8,128)(2,1)S(1)} %pair_rows.1.refs_0_.own), channel_id=1, source_target_pairs={{0,224},{16,240},{32,0},{48,16},{64,32},{80,48},{96,64},{112,80},{... | collective-permute-start | bytes 786440 | tf_op jit(solution)/shard_map/ppermute | solution.py:68
  15.0 15.3 %collective-permute-start = (bf16[2,64,1024]{2,1,0:T(8,128)(2,1)S(1)}, bf16[2,64,1024]{2,1,0:T(8,128)(2,1)S(1)}, u32[]{:S(2)}, u32[]{:S(2)}) collective-permute-start(bf16[2,64,1024]{2,1,0:T(8,128)(2,1)S(1)} %pair_rows.1.refs_0_.own), channel_id=1, source_target_pairs={{0,32},{16,48},{32,64},{48,80},{64,96},{80,112},{96,128},{112,144}... | collective-permute-start | bytes 786440 | tf_op jit(solution)/shard_map/ppermute | solution.py:64
  19.4 19.0 %all-to-all-start = ((bf16[16,4,5120]{2,1,0:T(4,128)(2,1)}), bf16[16,4,5120]{2,1,0:T(4,128)(2,1)S(1)}, u32[]{:S(2)}, u32[]{:S(2)}) async-start(bf16[16,4,5120]{2,1,0:T(4,128)(2,1)} %reshape.192), calls=%async_computation | async-start | bytes 1310720 | tf_op jit(solution)/shard_map/all_to_all | solution.py:461
  26.9 81.1 %all-gather.2.cloned.1.call-start = ((), (), s32[]{:S(2)}) async-start(), calls=%async_computation.3 | async-start | bytes 5898240 | tf_op jit(solution)/shard_map/all_gather | solution.py:476
  27.0 7.8 %collective-permute-start.4 = (bf16[2,64,1024]{2,1,0:T(8,128)(2,1)S(1)}, bf16[2,64,1024]{2,1,0:T(8,128)(2,1)S(1)}, u32[]{:S(2)}, u32[]{:S(2)}) collective-permute-start(bf16[2,64,1024]{2,1,0:T(8,128)(2,1)S(1)} %collective-permute-done.3.refs_8_), channel_id=1, source_target_pairs={{0,224},{16,240},{32,0},{48,16},{64,32},{80,48},{96,64},{112,80},{... | collective-permute-start | bytes 786440 | tf_op jit(solution)/shard_map/ppermute | solution.py:68
  30.3 8.1 %collective-permute-start.1 = (bf16[2,64,1024]{2,1,0:T(8,128)(2,1)S(1)}, bf16[2,64,1024]{2,1,0:T(8,128)(2,1)S(1)}, u32[]{:S(2)}, u32[]{:S(2)}) collective-permute-start(bf16[2,64,1024]{2,1,0:T(8,128)(2,1)S(1)} %collective-permute-done.refs_1_), channel_id=1, source_target_pairs={{0,32},{16,48},{32,64},{48,80},{64,96},{80,112},{96,128},{112,144}... | collective-permute-start | bytes 786440 | tf_op jit(solution)/shard_map/ppermute | solution.py:64
  34.7 7.6 %collective-permute-start.5 = (bf16[2,64,1024]{2,1,0:T(8,128)(2,1)S(1)}, bf16[2,64,1024]{2,1,0:T(8,128)(2,1)S(1)}, u32[]{:S(2)}, u32[]{:S(2)}) collective-permute-start(bf16[2,64,1024]{2,1,0:T(8,128)(2,1)S(1)} %collective-permute-done.4.refs_7_), channel_id=1, source_target_pairs={{0,224},{16,240},{32,0},{48,16},{64,32},{80,48},{96,64},{112,80},{... | collective-permute-start | bytes 786440 | tf_op jit(solution)/shard_map/ppermute | solution.py:68
  38.4 7.6 %collective-permute-start.2 = (bf16[2,64,1024]{2,1,0:T(8,128)(2,1)S(1)}, bf16[2,64,1024]{2,1,0:T(8,128)(2,1)S(1)}, u32[]{:S(2)}, u32[]{:S(2)}) collective-permute-start(bf16[2,64,1024]{2,1,0:T(8,128)(2,1)S(1)} %collective-permute-done.1.refs_2_), channel_id=1, source_target_pairs={{0,32},{16,48},{32,64},{48,80},{64,96},{80,112},{96,128},{112,144}... | collective-permute-start | bytes 786440 | tf_op jit(solution)/shard_map/ppermute | solution.py:64
  46.0 149.8 %reduce-scatter.2.cloned.1.call-start = ((), (), s32[]{:S(2)}) async-start(), calls=%async_computation.4 | async-start | bytes 5898240 | tf_op jit(solution)/shard_map/reduce_scatter | solution.py:481
  46.1 62.0 %collective-permute-start.19 = (bf16[5120,256]{1,0:T(8,128)(2,1)}, bf16[5120,256]{1,0:T(8,128)(2,1)}, u32[]{:S(2)}, u32[]{:S(2)}) collective-permute-start(bf16[5120,256]{1,0:T(8,128)(2,1)} %bitcast.31), channel_id=1, source_target_pairs={{0,16},{16,0},{32,48},{48,32},{64,80},{80,64},{96,112},{112,96},{1... | collective-permute-start | bytes 7864328 | tf_op jit(solution)/shard_map/ppermute | solution.py:475
  46.2 61.9 %collective-permute-start.20 = (bf16[5120,256]{1,0:T(8,128)(2,1)}, bf16[5120,256]{1,0:T(8,128)(2,1)}, u32[]{:S(2)}, u32[]{:S(2)}) collective-permute-start(bf16[5120,256]{1,0:T(8,128)(2,1)} %bitcast.33), channel_id=1, source_target_pairs={{0,16},{16,0},{32,48},{48,32},{64,80},{80,64},{96,112},{112,96},{1... | collective-permute-start | bytes 7864328 | tf_op jit(solution)/shard_map/ppermute | solution.py:475
  46.7 61.4 %collective-permute-start.21 = (bf16[256,5120]{1,0:T(8,128)(2,1)}, bf16[256,5120]{1,0:T(8,128)(2,1)}, u32[]{:S(2)}, u32[]{:S(2)}) collective-permute-start(bf16[256,5120]{1,0:T(8,128)(2,1)} %bitcast.35), channel_id=1, source_target_pairs={{0,16},{16,0},{32,48},{48,32},{64,80},{80,64},{96,112},{112,96},{1... | collective-permute-start | bytes 7864328 | tf_op jit(solution)/shard_map/ppermute | solution.py:475
  47.7 7.1 %collective-permute-start.9 = (bf16[1,64,1024]{2,1,0:T(8,128)(2,1)S(1)}, bf16[1,64,1024]{2,1,0:T(8,128)(2,1)S(1)}, u32[]{:S(2)}, u32[]{:S(2)}) collective-permute-start(bf16[1,64,1024]{2,1,0:T(8,128)(2,1)S(1)} %slice.26), channel_id=1, source_target_pairs={{0,32},{16,48},{32,64},{48,80},{64,96},{80,112},{96,128},{112,144}... | collective-permute-start | bytes 393224 | tf_op jit(solution)/shard_map/ppermute | solution.py:64
  61.1 6.8 %collective-permute-start.13 = (bf16[4,64,256]{2,1,0:T(8,128)(2,1)S(1)}, bf16[4,64,256]{2,1,0:T(8,128)(2,1)S(1)}, u32[]{:S(2)}, u32[]{:S(2)}) collective-permute-start(bf16[4,64,256]{2,1,0:T(8,128)(2,1)S(1)} %get-tuple-element.55), channel_id=1, source_target_pairs={{0,8},{1,9},{2,10},{3,11},{4,12},{5,13},{6,14},{7,15},{8,0},{9,1},... | collective-permute-start | bytes 393224 | tf_op jit(solution)/shard_map/ppermute | solution.py:318
  65.5 11.7 %collective-permute-start.6 = (bf16[2,64,640]{2,1,0:T(8,128)(2,1)S(1)}, bf16[2,64,640]{2,1,0:T(8,128)(2,1)S(1)}, u32[]{:S(2)}, u32[]{:S(2)}) collective-permute-start(bf16[2,64,640]{2,1,0:T(8,128)(2,1)S(1)} %get-tuple-element.41), channel_id=1, source_target_pairs={{0,4},{1,5},{2,6},{3,7},{4,8},{5,9},{6,10},{7,11},{8,12},{9,13},{1... | collective-permute-start | bytes 491528 | tf_op jit(solution)/shard_map/ppermute | solution.py:317
  74.5 11.8 %collective-permute-start.16 = (bf16[4,4,64,256]{3,2,1,0:T(8,128)(2,1)S(1)}, bf16[4,4,64,256]{3,2,1,0:T(8,128)(2,1)S(1)}, u32[]{:S(2)}, u32[]{:S(2)}) collective-permute-start(bf16[4,4,64,256]{3,2,1,0:T(8,128)(2,1)S(1)} %stack_sources.1), channel_id=1, source_target_pairs={{0,3},{1,0},{2,1},{3,2},{4,7},{5,4},{6,5},{7,6},{8,11},{9,8},{10,9... | collective-permute-start | bytes 1572872 | tf_op jit(solution)/shard_map/ppermute | solution.py:321
  77.3 12.5 %collective-permute-start.15 = (bf16[4,4,64,256]{3,2,1,0:T(8,128)(2,1)S(1)}, bf16[4,4,64,256]{3,2,1,0:T(8,128)(2,1)S(1)}, u32[]{:S(2)}, u32[]{:S(2)}) collective-permute-start(bf16[4,4,64,256]{3,2,1,0:T(8,128)(2,1)S(1)} %stack_sources.1), channel_id=1, source_target_pairs={{0,1},{1,2},{2,3},{3,0},{4,5},{5,6},{6,7},{7,4},{8,9},{9,10},{10,1... | collective-permute-start | bytes 1572872 | tf_op jit(solution)/shard_map/ppermute | solution.py:320
  86.4 7.7 %collective-permute-start.7 = (bf16[2,64,640]{2,1,0:T(8,128)(2,1)S(1)}, bf16[2,64,640]{2,1,0:T(8,128)(2,1)S(1)}, u32[]{:S(2)}, u32[]{:S(2)}) collective-permute-start(bf16[2,64,640]{2,1,0:T(8,128)(2,1)S(1)} %get-tuple-element.42), channel_id=1, source_target_pairs={{0,8},{1,9},{2,10},{3,11},{4,12},{5,13},{6,14},{7,15},{8,0},{9,1},... | collective-permute-start | bytes 491528 | tf_op jit(solution)/shard_map/ppermute | solution.py:317
  89.8 7.1 %collective-permute-start.8 = (bf16[2,64,640]{2,1,0:T(8,128)(2,1)S(1)}, bf16[2,64,640]{2,1,0:T(8,128)(2,1)S(1)}, u32[]{:S(2)}, u32[]{:S(2)}) collective-permute-start(bf16[2,64,640]{2,1,0:T(8,128)(2,1)S(1)} %get-tuple-element.43), channel_id=1, source_target_pairs={{0,12},{1,13},{2,14},{3,15},{4,0},{5,1},{6,2},{7,3},{8,4},{9,5},{1... | collective-permute-start | bytes 491528 | tf_op jit(solution)/shard_map/ppermute | solution.py:317
  94.1 6.7 %collective-permute-start.18 = (bf16[2,4,64,256]{3,2,1,0:T(8,128)(2,1)S(1)}, bf16[2,4,64,256]{3,2,1,0:T(8,128)(2,1)S(1)}, u32[]{:S(2)}, u32[]{:S(2)}) collective-permute-start(bf16[2,4,64,256]{3,2,1,0:T(8,128)(2,1)S(1)} %slice.35), channel_id=1, source_target_pairs={{0,3},{1,0},{2,1},{3,2},{4,7},{5,4},{6,5},{7,6},{8,11},{9,8},{10,9... | collective-permute-start | bytes 786440 | tf_op jit(solution)/shard_map/ppermute | solution.py:323
  96.9 7.6 %collective-permute-start.17 = (bf16[2,4,64,256]{3,2,1,0:T(8,128)(2,1)S(1)}, bf16[2,4,64,256]{3,2,1,0:T(8,128)(2,1)S(1)}, u32[]{:S(2)}, u32[]{:S(2)}) collective-permute-start(bf16[2,4,64,256]{3,2,1,0:T(8,128)(2,1)S(1)} %slice.34), channel_id=1, source_target_pairs={{0,1},{1,2},{2,3},{3,0},{4,5},{5,6},{6,7},{7,4},{8,9},{9,10},{10,1... | collective-permute-start | bytes 786440 | tf_op jit(solution)/shard_map/ppermute | solution.py:322
  141.1 6.3 %collective-permute-start.22 = (bf16[2,64,640]{2,1,0:T(8,128)(2,1)S(1)}, bf16[2,64,640]{2,1,0:T(8,128)(2,1)S(1)}, u32[]{:S(2)}, u32[]{:S(2)}) collective-permute-start(bf16[2,64,640]{2,1,0:T(8,128)(2,1)S(1)} %get-tuple-element.68), channel_id=1, source_target_pairs={{0,12},{1,13},{2,14},{3,15},{4,0},{5,1},{6,2},{7,3},{8,4},{9,5},{1... | collective-permute-start | bytes 491528 | tf_op jit(solution)/shard_map/ppermute | solution.py:330
  141.8 9.8 %collective-permute-start.23 = (bf16[2,64,640]{2,1,0:T(8,128)(2,1)S(1)}, bf16[2,64,640]{2,1,0:T(8,128)(2,1)S(1)}, u32[]{:S(2)}, u32[]{:S(2)}) collective-permute-start(bf16[2,64,640]{2,1,0:T(8,128)(2,1)S(1)} %get-tuple-element.69), channel_id=1, source_target_pairs={{0,8},{1,9},{2,10},{3,11},{4,12},{5,13},{6,14},{7,15},{8,0},{9,1},... | collective-permute-start | bytes 491528 | tf_op jit(solution)/shard_map/ppermute | solution.py:330
  144.2 8.3 %collective-permute-start.24 = (bf16[2,64,640]{2,1,0:T(8,128)(2,1)S(1)}, bf16[2,64,640]{2,1,0:T(8,128)(2,1)S(1)}, u32[]{:S(2)}, u32[]{:S(2)}) collective-permute-start(bf16[2,64,640]{2,1,0:T(8,128)(2,1)S(1)} %get-tuple-element.70), channel_id=1, source_target_pairs={{0,4},{1,5},{2,6},{3,7},{4,8},{5,9},{6,10},{7,11},{8,12},{9,13},{1... | collective-permute-start | bytes 491528 | tf_op jit(solution)/shard_map/ppermute | solution.py:330
  (11 other events, 88.1 us)
Sparse Core Ops, SparseCore 0:
  46.1 61.8 all-gather.1
  131.9 63.8 reduce-scatter.1

commit v5 on v4

--- a/solution.py
+++ b/solution.py
@@ -12,14 +12,6 @@
 SIDE = 4
 RINGS = [[2 * z + c for z in range(8)] for c in range(2)]
 CORE_SWAP = [(i, i ^ 1) for i in range(16)]
-
-
-def shift_x(d):
-    return [(4 * a + b, 4 * ((a + d) % 4) + b) for a in range(4) for b in range(4)]
-
-
-def shift_y(d):
-    return [(4 * a + b, 4 * a + (b + d) % 4) for a in range(4) for b in range(4)]
 
 
 def ordinary(vmem=48):
@@ -80,14 +72,6 @@
         theirs[i] = held[table[2 + i]]
 
 
-def pass_blocks(paired):
-    below, above = [paired], [paired]
-    for _ in range(3):
-        below.append(up_z(below[-1]))
-        above.append(down_z(above[-1]))
-    return below, above
-
-
 def choose_blocks(below, above, table):
     paired = below[0]
     far_low, far_high = up_z(below[3][:1]), down_z(above[3][1:])
@@ -99,135 +83,92 @@
     )
 
 
-def pick_kernel(table, own, mine, swapped, *outs):
-    x = table[0]
-    for d in range(SIDE):
-        h = lax.rem(x + d, SIDE)
-        columns = pl.ds(pl.multiple_of(h * 256, 256), 256)
-        outs[d][0:2] = own[:, :, columns]
-        for i in range(2):
-            here = table[1 + i] > 0
-            outs[d][2 + i] = jnp.where(here, mine[i, :, columns], swapped[i, :, columns])
-
-
-def pick_heads(own, mine, swapped, table):
-    rows = own.shape[1]
-    part = jax.ShapeDtypeStruct((4, rows, 256), own.dtype)
-    call = small(pick_kernel, [part] * SIDE, "pick_heads", 2 << 20)
-    return call(in_specs=[TABLE] + [WHOLE] * 3, out_specs=[WHOLE] * SIDE)(
-        table, own, mine, swapped
-    )
-
-
-def split_kernel(where, source, *outs):
-    x = where[0]
-    width = outs[0].shape[2]
-    for d in range(SIDE):
-        h = lax.rem(x + d, SIDE)
-        outs[d][...] = source[:, :, pl.ds(pl.multiple_of(h * width, 128), width)]
-
-
-def split_queries(queries, where):
-    part = jax.ShapeDtypeStruct(queries.shape[:2] + (queries.shape[2] // SIDE,), queries.dtype)
-    return pl.pallas_call(
-        split_kernel,
-        grid_spec=pltpu.PrefetchScalarGridSpec(
-            num_scalar_prefetch=1,
-            grid=(1,),
-            in_specs=[pl.BlockSpec(queries.shape, lambda i, t: (0, 0, 0))],
-            out_specs=[pl.BlockSpec(part.shape, lambda i, t: (0, 0, 0))] * SIDE,
-        ),
-        out_shape=[part] * SIDE,
-        compiler_params=ordinary(16),
-        cost_estimate=pl.CostEstimate(flops=0, bytes_accessed=1310720, transcendentals=0),
-        name="split_queries",
-    )(where, queries)
-
-
-def stack_kernel(where, *refs):
-    x = where[0]
-    out = refs[SIDE]
-    for d in range(SIDE):
-        out[lax.rem(x + SIDE - d, SIDE)] = refs[d][...]
-
-
-def stack_sources(parts, where):
-    shape = parts[0].shape
-    zeros = (0,) * len(shape)
-    return pl.pallas_call(
-        stack_kernel,
-        grid_spec=pltpu.PrefetchScalarGridSpec(
-            num_scalar_prefetch=1,
-            grid=(1,),
-            in_specs=[pl.BlockSpec(shape, lambda i, t: zeros)] * SIDE,
-            out_specs=pl.BlockSpec((SIDE,) + shape, lambda i, t: (0,) + zeros),
-        ),
-        out_shape=jax.ShapeDtypeStruct((SIDE,) + shape, parts[0].dtype),
-        compiler_params=ordinary(16),
-        cost_estimate=pl.CostEstimate(flops=0, bytes_accessed=1 << 20, transcendentals=0),
-        name="stack_sources",
-    )(where, *parts)
-
-
-def join_kernel(where, *refs):
-    x = where[0]
-    out = refs[SIDE]
-    width = refs[0].shape[2]
-    for d in range(SIDE):
-        h = lax.rem(x + d, SIDE)
-        out[:, :, pl.ds(pl.multiple_of(h * width, 128), width)] = refs[d][...]
-
-
-def join_heads(parts, where):
-    shape = parts[0].shape
-    full = shape[:2] + (shape[2] * SIDE,)
-    return pl.pallas_call(
-        join_kernel,
-        grid_spec=pltpu.PrefetchScalarGridSpec(
-            num_scalar_prefetch=1,
-            grid=(1,),
-            in_specs=[pl.BlockSpec(shape, lambda i, t: (0, 0, 0))] * SIDE,
-            out_specs=pl.BlockSpec(full, lambda i, t: (0, 0, 0)),
-        ),
-        out_shape=jax.ShapeDtypeStruct(full, parts[0].dtype),
-        compiler_params=ordinary(16),
-        cost_estimate=pl.CostEstimate(flops=0, bytes_accessed=1310720, transcendentals=0),
-        name="join_heads",
-    )(where, *parts)
+def pack_own_kernel(own, queries, out):
+    group = queries.shape[2] // (SIDE * HEAD_DIM)
+    for h in range(SIDE):
+        at = h * 256
+        for y in range(SIDE):
+            to = SIDE * h + y
+            for b in range(2):
+                out[to, b * 128 : b * 128 + 64] = own[b, :, at : at + 128]
+                out[to, b * 128 + 64 : b * 128 + 128] = own[b, :, at + 128 : at + 256]
+                for g in range(group):
+                    row = 256 + (b * group + g) * 16
+                    column = (h * group + g) * HEAD_DIM
+                    out[to, row : row + 16] = queries[
+                        b, 16 * y : 16 * y + 16, column : column + HEAD_DIM
+                    ]
+
+
+def pack_own(own, queries):
+    rows = 256 + 2 * 16 * queries.shape[2] // (SIDE * HEAD_DIM)
+    out = jax.ShapeDtypeStruct((SIDE * SIDE, rows, HEAD_DIM), own.dtype)
+    call = small(pack_own_kernel, out, "pack_own", 3 << 20)
+    return call(in_specs=[WHOLE] * 2, out_specs=WHOLE)(own, queries)
+
+
+def pack_listed_kernel(table, mine, swapped, out):
+    for h in range(SIDE):
+        at = h * 256
+        for b in range(2):
+            piece = jnp.where(
+                table[b] > 0, mine[b, :, at : at + 256], swapped[b, :, at : at + 256]
+            )
+            for y in range(SIDE):
+                out[SIDE * h + y, b * 128 : b * 128 + 64] = piece[:, :HEAD_DIM]
+                out[SIDE * h + y, b * 128 + 64 : b * 128 + 128] = piece[:, HEAD_DIM:]
+
+
+def pack_listed(table, mine, swapped):
+    out = jax.ShapeDtypeStruct((SIDE * SIDE, 256, HEAD_DIM), mine.dtype)
+    call = small(pack_listed_kernel, out, "pack_listed", 3 << 20)
+    return call(in_specs=[TABLE] + [WHOLE] * 2, out_specs=WHOLE)(table, mine, swapped)
+
+
+def unpack_kernel(back, out):
+    group = out.shape[2] // (SIDE * HEAD_DIM)
+    for h in range(SIDE):
+        for y in range(SIDE):
+            for p in range(2):
+                for g in range(group):
+                    row = (p * group + g) * 16
+                    column = (h * group + g) * HEAD_DIM
+                    out[p, 16 * y : 16 * y + 16, column : column + HEAD_DIM] = back[
+                        SIDE * h + y, row : row + 16
+                    ]
+
+
+def unpack(back, shape):
+    call = small(unpack_kernel, jax.ShapeDtypeStruct(shape, back.dtype), "unpack", 1310720)
+    return call(in_specs=[WHOLE], out_specs=WHOLE)(back)
 
 
 NT = (((1,), (1,)), ((), ()))
 
 
-def attend_kernel(where, q0, q1, q2, q3, r0, r1, r2, r3a, r3b, o0, o1, o2, o3, kown, vown, klist, vlist, qall, oall):
+def attend_kernel(table, seen, listed, out, kown, vown, klist, vlist):
     p = pl.program_id(0)
-    x, y, usable = where[0], where[1], where[2 + p]
-    pieces = (r0, r1, r2)
-    for xs in range(SIDE):
-        last = r3a if xs < 2 else r3b
-        for turn in range(SIDE):
-            piece = pieces[turn][xs] if turn < 3 else last[xs % 2]
-            at = pl.ds(xs * 256 + turn * 64, 64)
-            kown[at, :] = piece[0, 0, :, :HEAD_DIM]
-            vown[at, :] = piece[0, 0, :, HEAD_DIM:]
-            klist[at, :] = piece[1, 0, :, :HEAD_DIM]
-            vlist[at, :] = piece[1, 0, :, HEAD_DIM:]
+    y, usable = table[0], table[1 + p]
+    own_at = pl.multiple_of(p * 128, 128)
+    for e in range(SIDE * SIDE):
+        at = pl.ds(e * 64, 64)
+        kown[at, :] = seen[e, pl.ds(own_at, 64), :]
+        vown[at, :] = seen[e, pl.ds(own_at + 64, 64), :]
+        klist[at, :] = listed[e, pl.ds(own_at, 64), :]
+        vlist[at, :] = listed[e, pl.ds(own_at + 64, 64), :]
     scaling = HEAD_DIM ** (-0.5)
-    group = q0.shape[2] // HEAD_DIM
+    group = out.shape[1] // 32
     rows = 64 * group
-    qs, outs = (q0, q1, q2, q3), (o0, o1, o2, o3)
-    query_row = lax.rem(lax.broadcasted_iota(jnp.int32, (rows, 256), 0), 64)
-    key_index = lax.broadcasted_iota(jnp.int32, (rows, 256), 1)
-    turn = key_index // 64
-    behind = jnp.where(turn == 0, 0, jnp.where(turn == 1, 3, jnp.where(turn == 2, 1, 2)))
-    key_pos = lax.rem(y + behind, SIDE) * 64 + lax.rem(key_index, 64)
-    diagonal = key_pos <= y * 64 + query_row
-    for d in range(SIDE):
-        qall[lax.rem(x + SIDE - d, SIDE)] = qs[d][0]
+    row = lax.rem(lax.broadcasted_iota(jnp.int32, (rows, 256), 0), 64)
+    query_pos = lax.div(row, 16) * 64 + 16 * y + lax.rem(row, 16)
+    diagonal = lax.broadcasted_iota(jnp.int32, (rows, 256), 1) <= query_pos
     for case in range(SIDE):
-        query = jnp.concatenate(
-            [qall[case, :, g * HEAD_DIM : (g + 1) * HEAD_DIM] for g in range(group)], axis=0
-        )
+        pieces = []
+        for g in range(group):
+            at = pl.multiple_of(256 + (p * group + g) * 16, 16)
+            for e in range(SIDE):
+                pieces.append(seen[SIDE * case + e, pl.ds(at, 16), :])
+        query = jnp.concatenate(pieces, axis=0)
         before = case * 256
         own = lax.dot_general(
             query, kown[pl.ds(before, 256), :], NT, preferred_element_type=jnp.float32
@@ -258,44 +199,41 @@
             )
         mixed = (mixed / total).astype(jnp.bfloat16)
         for g in range(group):
-            oall[case, :, g * HEAD_DIM : (g + 1) * HEAD_DIM] = mixed[g * 64 : (g + 1) * 64]
-    for d in range(SIDE):
-        outs[d][0] = oall[lax.rem(x + SIDE - d, SIDE)]
-
-
-def attend(where, qs, rs):
-    qspec = pl.BlockSpec((1,) + qs[0].shape[1:], lambda i, t: (i, 0, 0))
-
-    def rspec(r):
-        return pl.BlockSpec((r.shape[0], 2, 1) + r.shape[3:], lambda i, t: (0, 0, i, 0, 0))
-
+            at = pl.multiple_of((p * group + g) * 16, 16)
+            for e in range(SIDE):
+                start = g * 64 + e * 16
+                out[SIDE * case + e, pl.ds(at, 16), :] = mixed[start : start + 16]
+
+
+def attend(table, seen, listed):
+    rows = seen.shape[1] - 256
+    out = jax.ShapeDtypeStruct((seen.shape[0], rows, seen.shape[2]), seen.dtype)
+    zeros = lambda i, t: (0, 0, 0)
     return pl.pallas_call(
         attend_kernel,
         grid_spec=pltpu.PrefetchScalarGridSpec(
             num_scalar_prefetch=1,
             grid=(2,),
-            in_specs=[qspec] * SIDE + [rspec(r) for r in rs],
-            out_specs=[qspec] * SIDE,
-            scratch_shapes=[pltpu.VMEM((1024, HEAD_DIM), jnp.bfloat16)] * 4
-            + [pltpu.VMEM((SIDE,) + qs[0].shape[1:], jnp.bfloat16)] * 2,
+            in_specs=[pl.BlockSpec(seen.shape, zeros), pl.BlockSpec(listed.shape, zeros)],
+            out_specs=pl.BlockSpec(out.shape, zeros),
+            scratch_shapes=[pltpu.VMEM((1024, HEAD_DIM), jnp.bfloat16)] * 4,
         ),
-        out_shape=[jax.ShapeDtypeStruct(q.shape, q.dtype) for q in qs],
+        out_shape=out,
         compiler_params=ordinary(40),
         cost_estimate=pl.CostEstimate(
             flops=2200000000, bytes_accessed=4 << 20, transcendentals=4300000
         ),
         name="attend",
-    )(where, *qs, *rs)
-
-
-def exchange_rows(queries, below, above, block_lists):
+    )(table, seen, listed)
+
+
+def exchange_rows(below, above, block_lists):
     ctx_count = lax.axis_size("ctx")
     blocks_total = 2 * ctx_count
     ctx_index = lax.axis_index("ctx")
     exp_index = lax.axis_index("exp")
-    x, y = lax.div(exp_index, SIDE), lax.rem(exp_index, SIDE)
+    y = lax.rem(exp_index, SIDE)
     z, core = lax.div(ctx_index, 2), lax.rem(ctx_index, 2)
-    where = jnp.stack([x, y]).astype(jnp.int32)
     other = ctx_index + 1 - 2 * core
     own_blocks = jnp.stack(
         [ctx_index, blocks_total - 1 - ctx_index, other, blocks_total - 1 - other]
@@ -307,28 +245,14 @@
     chosen = (2 * distance + (listed >= ctx_count).astype(jnp.int32)).astype(jnp.int32)
     local = (lax.rem(holder, 2) == core).astype(jnp.int32)
 
-    paired = below[0]
     mine, theirs = choose_blocks(below, above, chosen)
     swapped = lax.ppermute(theirs, "ctx", CORE_SWAP)
-    picked = pick_heads(
-        paired, mine, swapped, jnp.concatenate([x[None], local[:2]]).astype(jnp.int32)
-    )
-    split = split_queries(queries, where)
-    qs = [split[0]] + [lax.ppermute(split[d], "exp", shift_x(d)) for d in range(1, SIDE)]
-    received = [picked[0]] + [lax.ppermute(picked[d], "exp", shift_x(d)) for d in range(1, SIDE)]
-    r0 = stack_sources(received, where)
-    r1 = lax.ppermute(r0, "exp", shift_y(1))
-    r2 = lax.ppermute(r0, "exp", shift_y(-1))
-    r3a = lax.ppermute(r1[:2], "exp", shift_y(1))
-    r3b = lax.ppermute(r2[2:], "exp", shift_y(-1))
-    rs = [r.reshape((r.shape[0], 2, 2) + r.shape[2:]) for r in (r0, r1, r2, r3a, r3b)]
-    return where, jnp.concatenate([where, usable[:2]]), qs, rs
-
-
-def attend_all(where, state, qs, rs):
-    outs = attend(state, qs, rs)
-    back = [outs[0]] + [lax.ppermute(outs[d], "exp", shift_x(-d)) for d in range(1, SIDE)]
-    return join_heads(back, where)
+    packed = pack_listed(local[:2], mine, swapped)
+    return packed, jnp.concatenate([y[None], usable[:2]]).astype(jnp.int32)
+
+
+def trade(v):
+    return lax.all_to_all(v, "exp", split_axis=0, concat_axis=0, tiled=True)
 
 
 def ffn_kernel(counts, refs):
@@ -389,7 +313,7 @@
         copy.wait()
 
 
-def expert_rows(xs, weights, step=512):
+def expert_rows(xs, weights, step=256):
     width = xs[0].shape[1]
     hidden = weights[0].shape[1]
     tokens = sum(x.shape[0] for x in xs)
@@ -451,45 +375,21 @@
     return call(in_specs=[WHOLE] * 3, out_specs=[WHOLE] * 2)(hidden, router.T, expert_ids.T)
 
 
-def send_tokens(hidden, router, expert_ids):
-    expert_table = router.shape[1]
-    local_tokens = hidden.shape[0]
-    model_width = hidden.shape[1]
-    capacity = max(2, 2 * local_tokens // expert_table)
-    exp_count = lax.axis_size("exp")
-    outgoing, places = fill_slots(hidden, router, expert_ids, expert_table * capacity)
-    incoming = lax.all_to_all(
-        outgoing.reshape(exp_count, capacity, model_width),
-        "exp",
-        split_axis=0,
-        concat_axis=0,
-        tiled=True,
-    )
-    return incoming.reshape(-1, model_width), places
-
-
-def route_experts(incoming, places, w_gate, w_up, w_down, exchanged, attend_rows):
+def route_experts(incoming, places, weights, seen, packed, state, shape):
     model_width = incoming.shape[1]
     exp_count = lax.axis_size("exp")
-    own = (w_gate[0], w_up[0], w_down[0])
-    other = tuple(lax.ppermute(w, "ctx", CORE_SWAP) for w in own)
     rows = lax.all_gather(
         incoming, "ctx", axis=0, tiled=True, axis_index_groups=RINGS
     )
-    rows, exchanged = lax.optimization_barrier((rows, exchanged))
-    (partial,) = expert_rows([rows], own + other)
+    rows, seen, packed = lax.optimization_barrier((rows, seen, packed))
+    listed = trade(packed)
+    (partial,) = expert_rows([rows], weights)
     summed_output = lax.psum_scatter(
         partial, "ctx", scatter_dimension=0, tiled=True, axis_index_groups=RINGS
     )
-    attention = attend_rows(*exchanged)
+    attention = unpack(trade(attend(state, seen, listed)), shape)
     summed_output, attention = lax.optimization_barrier((summed_output, attention))
-    returned = lax.all_to_all(
-        summed_output.reshape(exp_count, -1, model_width),
-        "exp",
-        split_axis=0,
-        concat_axis=0,
-        tiled=True,
-    )
+    returned = trade(summed_output.reshape(exp_count, -1, model_width))
     moe_out = lax.dot_general(
         places,
         returned.reshape(-1, model_width),
@@ -511,18 +411,23 @@
     w_up,
     w_down,
 ):
-    below, above = pass_blocks(pair_rows(key_states, value_state_rows))
-    incoming, places = send_tokens(hidden, router, expert_ids)
-    incoming, below, above = lax.optimization_barrier((incoming, below, above))
-    where, state, qs, rs = exchange_rows(queries, below, above, block_lists)
+    own = (w_gate[0], w_up[0], w_down[0])
+    other = tuple(lax.ppermute(w, "ctx", CORE_SWAP) for w in own)
+    experts, width = router.shape[1], router.shape[0]
+    capacity = 2 * hidden.shape[0] // experts
+    outgoing, places = fill_slots(hidden, router, expert_ids, experts * capacity)
+    paired = pair_rows(key_states, value_state_rows)
+    outgoing, paired = lax.optimization_barrier((outgoing, paired))
+    incoming = trade(outgoing.reshape(experts, capacity, width)).reshape(-1, width)
+    below, above = [paired, up_z(paired)], [paired, down_z(paired)]
+    incoming, below[1], above[1] = lax.optimization_barrier((incoming, below[1], above[1]))
+    for _ in range(2):
+        below.append(up_z(below[-1]))
+        above.append(down_z(above[-1]))
+    seen = trade(pack_own(below[0], queries))
+    packed, state = exchange_rows(below, above, block_lists)
     attention, moe_out = route_experts(
-        incoming,
-        places,
-        w_gate,
-        w_up,
-        w_down,
-        (qs, rs),
-        lambda qs, rs: attend_all(where, state, qs, rs),
+        incoming, places, own + other, seen, packed, state, queries.shape
     )
     return (attention, moe_out)
 

time: 225 us -> 226 us (level)
  blocking collectives: 18.5 us -> 34.4 us
  starting transfers between devices: 46.7 us -> 39.6 us
  waiting for transfers between devices: 96.4 us -> 91.7 us
  Pallas kernels: 37.8 us -> 34.6 us
    ppermute x16 -> x3, waiting for transfers between devices: 31.6 us -> 0.01 us  [shards(): other = tuple((lax.ppermute(w, 'ctx', CORE_SWAP) for w in own))]
    ppermute x4, waiting for transfers between devices: 5 us -> 31.2 us  [up_z(): return lax.ppermute(v, 'ctx', ring(1))]
    reduce_scatter x1, waiting for transfers between devices: 41.9 us -> 15.8 us  [route_experts(): lax.psum_scatter(partial, 'ctx', scatter_dimension=0, tiled=True, axis_in...]
    ppermute x16 -> x3, starting transfers between devices: 24 us -> 0.69 us  [shards(): other = tuple((lax.ppermute(w, 'ctx', CORE_SWAP) for w in own))]
    all_gather x1, waiting for transfers between devices: 3.53 us -> 23.4 us  [route_experts(): lax.all_gather(incoming, 'ctx', axis=0, tiled=True, axis_index_groups=RINGS)]
    all_to_all x1 -> x3, waiting for transfers between devices: 0.01 us -> 19.8 us  [trade(): return lax.all_to_all(v, 'exp', split_axis=0, concat_axis=0, tiled=True)]
    all_to_all x1 -> x2, blocking collectives: 18.5 us -> 34.4 us  [trade(): return lax.all_to_all(v, 'exp', split_axis=0, concat_axis=0, tiled=True)]
    all_to_all x1 -> x3, starting transfers between devices: 7.48 us -> 21.9 us  [trade(): return lax.all_to_all(v, 'exp', split_axis=0, concat_axis=0, tiled=True)]
  transfers between devices with their start and end apart: 28 -> 17, of which waited for: 19 -> 9; matrix products, arithmetic and copies ran while one was open for 1% -> 1% of each run, Pallas kernels for 6% -> 6%
where the time goes in v5:
time: 226 us; the launch traced here: 225 us
  waiting for transfers between devices  91.7 us (41%)
  starting transfers between devices  39.6 us (18%)
  Pallas kernels  34.6 us (15%)
  blocking collectives  34.4 us (15%)
  between operations  14.2 us (6%)
  local copies, waits for them, and re-layouts  9.5 us (4%)
    all_to_all x2, blocking collectives, trade(): return lax.all_to_all(v, 'exp', split_axis=0, concat_axis=0, tiled=True)  34.4 us
    ppermute x4, waiting for transfers between devices, up_z(): return lax.ppermute(v, 'ctx', ring(1))  31.2 us
    all_gather x1, waiting for transfers between devices, route_experts(): lax.all_gather(incoming, 'ctx', axis=0, tiled=True, axis_index_groups=RINGS)  23.4 us
    all_to_all x3, starting transfers between devices, trade(): return lax.all_to_all(v, 'exp', split_axis=0, concat_axis=0, tiled=True)  21.9 us
    pallas_call x1, Pallas kernels, expert_rows(): pl.pallas_call(lambda *refs: ffn_kernel(len(xs), refs), in_specs=[far] *...  20 us
    all_to_all x3, waiting for transfers between devices, trade(): return lax.all_to_all(v, 'exp', split_axis=0, concat_axis=0, tiled=True)  19.8 us
    ppermute x4, starting transfers between devices, down_z(): return lax.ppermute(v, 'ctx', ring(-1))  16.5 us
    reduce_scatter x1, waiting for transfers between devices, route_experts(): lax.psum_scatter(partial, 'ctx', scatter_dimension=0, tiled=True, axis_in...  15.8 us
  transfers between devices with their start and end apart: 17, of which 9 were waited for; matrix products, arithmetic and copies ran while one was open for 1% of the time, Pallas kernels for 6%

profile of v5, /device:TPU:2, one launch (start us, length us, event | category | flops | bytes accessed | tf_op | source)
XLA Modules:
  0.0 225.3 jit_solution(10579883701902013121)
XLA Ops:
  13.1 1.1 reshape.177
  14.2 7.5 %all-to-all-start = ((bf16[16,4,5120]{2,1,0:T(4,128)(2,1)}), bf16[16,4,5120]{2,1,0:T(4,128)(2,1)S(1)}, u32[]{:S(2)}, u32[]{:S(2)}) async-start(bf16[16,4,5120]{2,1,0:T(4,128)(2,1)} %reshape.177), calls=%async_computation | async-start | bytes 1310720 | tf_op jit(solution)/shard_map/all_to_all | solution.py:255
  21.7 5.9 %collective-permute-start.1 = (bf16[2,64,1024]{2,1,0:T(8,128)(2,1)S(1)}, bf16[2,64,1024]{2,1,0:T(8,128)(2,1)S(1)}, u32[]{:S(2)}, u32[]{:S(2)}) collective-permute-start(bf16[2,64,1024]{2,1,0:T(8,128)(2,1)S(1)} %pair_rows.1.own.refs_0_), channel_id=1, source_target_pairs={{0,224},{16,240},{32,0},{48,16},{64,32},{80,48},{96,64},{112,80},{... | collective-permute-start | bytes 786440 | tf_op jit(solution)/shard_map/ppermute | solution.py:60
  27.6 4.6 %all-to-all-done = bf16[16,4,5120]{2,1,0:T(4,128)(2,1)S(1)} async-done(((bf16[16,4,5120]{2,1,0:T(4,128)(2,1)}), bf16[16,4,5120]{2,1,0:T(4,128)(2,1)S(1)}, u32[]{:S(2)}, u32[]{:S(2)}) %all-to-all-start) | async-done | bytes 655392 | tf_op jit(solution)/shard_map/all_to_all | solution.py:255
  33.2 2.8 %collective-permute-done.refs_1_ = bf16[2,64,1024]{2,1,0:T(8,128)(2,1)S(1)} collective-permute-done((bf16[2,64,1024]{2,1,0:T(8,128)(2,1)S(1)}, bf16[2,64,1024]{2,1,0:T(8,128)(2,1)S(1)}, u32[]{:S(2)}, u32[]{:S(2)}) %collective-permute-start) | collective-permute-done | bytes 262176 | tf_op jit(solution)/shard_map/ppermute | solution.py:56
  36.8 1.4 pack_own.1
  38.2 7.2 %all-to-all-start.1 = ((bf16[16,416,128]{2,1,0:T(8,128)(2,1)}), bf16[16,416,128]{2,1,0:T(8,128)(2,1)S(1)}, u32[]{:S(2)}, u32[]{:S(2)}) async-start(bf16[16,416,128]{2,1,0:T(8,128)(2,1)} %pack_own.1), calls=%async_computation.1 | async-start | bytes 3407872 | tf_op jit(solution)/shard_map/all_to_all | solution.py:255
  45.6 3.2 %collective-permute-start.5 = (bf16[2,64,1024]{2,1,0:T(8,128)(2,1)S(1)}, bf16[2,64,1024]{2,1,0:T(8,128)(2,1)S(1)}, u32[]{:S(2)}, u32[]{:S(2)}) collective-permute-start(bf16[2,64,1024]{2,1,0:T(8,128)(2,1)S(1)} %collective-permute-done.1.refs_8_), channel_id=1, source_target_pairs={{0,224},{16,240},{32,0},{48,16},{64,32},{80,48},{96,64},{112,80},{... | collective-permute-start | bytes 786440 | tf_op jit(solution)/shard_map/ppermute | solution.py:60
  48.8 11.8 %collective-permute-done.2.refs_2_ = bf16[2,64,1024]{2,1,0:T(8,128)(2,1)S(1)} collective-permute-done((bf16[2,64,1024]{2,1,0:T(8,128)(2,1)S(1)}, bf16[2,64,1024]{2,1,0:T(8,128)(2,1)S(1)}, u32[]{:S(2)}, u32[]{:S(2)}) %collective-permute-start.2) | collective-permute-done | bytes 262176 | tf_op jit(solution)/shard_map/ppermute | solution.py:56
  60.6 3.7 %collective-permute-start.6 = (bf16[2,64,1024]{2,1,0:T(8,128)(2,1)S(1)}, bf16[2,64,1024]{2,1,0:T(8,128)(2,1)S(1)}, u32[]{:S(2)}, u32[]{:S(2)}) collective-permute-start(bf16[2,64,1024]{2,1,0:T(8,128)(2,1)S(1)} %collective-permute-done.5.refs_7_), channel_id=1, source_target_pairs={{0,224},{16,240},{32,0},{48,16},{64,32},{80,48},{96,64},{112,80},{... | collective-permute-start | bytes 786440 | tf_op jit(solution)/shard_map/ppermute | solution.py:60
  65.0 10.9 %collective-permute-done.3.refs_3_ = bf16[2,64,1024]{2,1,0:T(8,128)(2,1)S(1)} collective-permute-done((bf16[2,64,1024]{2,1,0:T(8,128)(2,1)S(1)}, bf16[2,64,1024]{2,1,0:T(8,128)(2,1)S(1)}, u32[]{:S(2)}, u32[]{:S(2)}) %collective-permute-start.3) | collective-permute-done | bytes 262176 | tf_op jit(solution)/shard_map/ppermute | solution.py:56
  76.0 3.6 %collective-permute-start.7 = (bf16[1,64,1024]{2,1,0:T(8,128)(2,1)S(1)}, bf16[1,64,1024]{2,1,0:T(8,128)(2,1)S(1)}, u32[]{:S(2)}, u32[]{:S(2)}) collective-permute-start(bf16[1,64,1024]{2,1,0:T(8,128)(2,1)S(1)} %slice.26), channel_id=1, source_target_pairs={{0,224},{16,240},{32,0},{48,16},{64,32},{80,48},{96,64},{112,80},{... | collective-permute-start | bytes 393224 | tf_op jit(solution)/shard_map/ppermute | solution.py:60
  79.7 5.8 %collective-permute-done.4.refs_4_ = bf16[1,64,1024]{2,1,0:T(8,128)(2,1)S(1)} collective-permute-done((bf16[1,64,1024]{2,1,0:T(8,128)(2,1)S(1)}, bf16[1,64,1024]{2,1,0:T(8,128)(2,1)S(1)}, u32[]{:S(2)}, u32[]{:S(2)}) %collective-permute-start.4) | collective-permute-done | bytes 131104 | tf_op jit(solution)/shard_map/ppermute | solution.py:56
  86.5 1.4 collective-permute-done.8.swapped
  88.0 1.7 pack_listed.1
  89.7 23.4 %all-gather.2.cloned.1.call-done.refs_0_ = bf16[512,5120]{1,0:T(8,128)(2,1)} async-done(((bf16[64,5120]{1,0:T(8,128)(2,1)}), bf16[512,5120]{1,0:T(8,128)(2,1)}) %all-gather.2.cloned.1.call-update) | async-done | bytes 5242896 | tf_op jit(solution)/shard_map/all_gather | solution.py:381
  113.1 20.0 %expert_rows.1 = bf16[512,5120]{1,0:T(8,128)(2,1)} custom-call(bf16[512,5120]{1,0:T(8,128)(2,1)} %all-gather.2.cloned.1.call-done.refs_0_, bf16[5120,256]{1,0:T(8,128)(2,1)} %bitcast.21, bf16[5120,256]{1,0:T(8,128)(2,1)} %bitcast.23, bf16[256,5120]{1,0:T(8,128)(2,1)} %bitcast.25, bf16[5120,256]{1,0:T(8,128)(2,1)} %collective-permute-done.9.refs_4_, ...), custom_call_target="tpu_custom_call" | custom-call | flops 8053063680 | bytes 26214400 | tf_op jit(solution)/shard_map/expert_rows/pallas_call | solution.py:323
  133.1 7.2 %all-to-all-start.2 = ((bf16[16,256,128]{2,1,0:T(8,128)(2,1)}), bf16[16,256,128]{2,1,0:T(8,128)(2,1)S(1)}, u32[]{:S(2)}, u32[]{:S(2)}) async-start(bf16[16,256,128]{2,1,0:T(8,128)(2,1)} %pack_listed.1), calls=%async_computation.3 | async-start | bytes 2097152 | tf_op jit(solution)/shard_map/all_to_all | solution.py:255
  140.4 15.1 %all-to-all-done.2.listed = bf16[16,256,128]{2,1,0:T(8,128)(2,1)S(1)} async-done(((bf16[16,256,128]{2,1,0:T(8,128)(2,1)}), bf16[16,256,128]{2,1,0:T(8,128)(2,1)S(1)}, u32[]{:S(2)}, u32[]{:S(2)}) %all-to-all-start.2) | async-done | bytes 1048608 | tf_op jit(solution)/shard_map/all_to_all | solution.py:255
  155.5 9.0 %attend.1 = bf16[16,160,128]{2,1,0:T(8,128)(2,1)S(1)} custom-call(s32[3]{0:T(128)S(1)} %pad_add_fusion.table, bf16[16,416,128]{2,1,0:T(8,128)(2,1)S(1)} %all-to-all-done.1.seen, bf16[16,256,128]{2,1,0:T(8,128)(2,1)S(1)} %all-to-all-done.2.listed), custom_call_target="tpu_custom_call" | custom-call | flops 2200000000 | bytes 4194304 | tf_op jit(solution)/shard_map/attend/pallas_call | solution.py:212
  164.6 15.9 %all_to_all.25.back = bf16[16,160,128]{2,1,0:T(8,128)(2,1)S(1)} all-to-all(bf16[16,160,128]{2,1,0:T(8,128)(2,1)S(1)} %attend.1), channel_id=1, replica_groups=mesh['ctx'=16,'exp'=16] {'exp'}, dimensions={0} | all-to-all | bytes 1310720 | tf_op jit(solution)/shard_map/all_to_all | solution.py:255
  181.4 15.8 %reduce-scatter.2.cloned.1.call-done = bf16[64,5120]{1,0:T(8,128)(2,1)} async-done(((bf16[512,5120]{1,0:T(8,128)(2,1)}), bf16[64,5120]{1,0:T(8,128)(2,1)}) %reduce-scatter.2.cloned.1.call-update) | async-done | bytes 655376 | tf_op jit(solution)/shard_map/reduce_scatter | solution.py:387
  197.2 1.6 reshape.179
  198.8 18.5 %all_to_all.26 = bf16[16,4,5120]{2,1,0:T(4,128)(2,1)S(1)} all-to-all(bf16[16,4,5120]{2,1,0:T(4,128)(2,1)S(1)} %reshape.179), channel_id=1, replica_groups=mesh['ctx'=16,'exp'=16] {'exp'}, dimensions={0} | all-to-all | bytes 1310720 | tf_op jit(solution)/shard_map/all_to_all | solution.py:255
  (55 shorter events, 11.9 us)
Async XLA Ops:
  7.2 57.2 %copy-start = (s32[32]{0:T(128)S(1)}, s32[32]{0:T(128)}, u32[]{:S(2)}) copy-start(s32[32]{0:T(128)} %param.13) | copy-start | bytes 388
  7.2 0.9 copy-start.4
  8.1 0.9 copy-start.5
  9.1 27.7 %copy-start.1 = (bf16[2,64,2560]{2,1,0:T(8,128)(2,1)S(1)}, bf16[2,64,2560]{2,1,0:T(8,128)(2,1)}, u32[]{:S(2)}) copy-start(bf16[2,64,2560]{2,1,0:T(8,128)(2,1)} %queries.1) | copy-start | bytes 1966084
  9.1 1.0 copy-start.2
  10.1 0.9 copy-start.3
  14.2 18.1 %all-to-all-start = ((bf16[16,4,5120]{2,1,0:T(4,128)(2,1)}), bf16[16,4,5120]{2,1,0:T(4,128)(2,1)S(1)}, u32[]{:S(2)}, u32[]{:S(2)}) async-start(bf16[16,4,5120]{2,1,0:T(4,128)(2,1)} %reshape.177), calls=%async_computation | async-start | bytes 1310720 | tf_op jit(solution)/shard_map/all_to_all | solution.py:255
  21.6 91.4 %all-gather.2.cloned.1.call-start = ((), (), s32[]{:S(2)}) async-start(), calls=%async_computation.6 | async-start | bytes 5898240 | tf_op jit(solution)/shard_map/all_gather | solution.py:381
  21.7 11.6 %collective-permute-start.1 = (bf16[2,64,1024]{2,1,0:T(8,128)(2,1)S(1)}, bf16[2,64,1024]{2,1,0:T(8,128)(2,1)S(1)}, u32[]{:S(2)}, u32[]{:S(2)}) collective-permute-start(bf16[2,64,1024]{2,1,0:T(8,128)(2,1)S(1)} %pair_rows.1.own.refs_0_), channel_id=1, source_target_pairs={{0,224},{16,240},{32,0},{48,16},{64,32},{80,48},{96,64},{112,80},{... | collective-permute-start | bytes 786440 | tf_op jit(solution)/shard_map/ppermute | solution.py:60
  27.6 8.4 %collective-permute-start = (bf16[2,64,1024]{2,1,0:T(8,128)(2,1)S(1)}, bf16[2,64,1024]{2,1,0:T(8,128)(2,1)S(1)}, u32[]{:S(2)}, u32[]{:S(2)}) collective-permute-start(bf16[2,64,1024]{2,1,0:T(8,128)(2,1)S(1)} %pair_rows.1.own.refs_0_), channel_id=1, source_target_pairs={{0,32},{16,48},{32,64},{48,80},{64,96},{80,112},{96,128},{112,144}... | collective-permute-start | bytes 786440 | tf_op jit(solution)/shard_map/ppermute | solution.py:56
  36.1 77.0 %collective-permute-start.9 = (bf16[5120,256]{1,0:T(8,128)(2,1)}, bf16[5120,256]{1,0:T(8,128)(2,1)}, u32[]{:S(2)}, u32[]{:S(2)}) collective-permute-start(bf16[5120,256]{1,0:T(8,128)(2,1)} %bitcast.20), channel_id=1, source_target_pairs={{0,16},{16,0},{32,48},{48,32},{64,80},{80,64},{96,112},{112,96},{1... | collective-permute-start | bytes 7864328 | tf_op jit(solution)/shard_map/ppermute | solution.py:415
  36.2 76.9 %collective-permute-start.10 = (bf16[5120,256]{1,0:T(8,128)(2,1)}, bf16[5120,256]{1,0:T(8,128)(2,1)}, u32[]{:S(2)}, u32[]{:S(2)}) collective-permute-start(bf16[5120,256]{1,0:T(8,128)(2,1)} %bitcast.22), channel_id=1, source_target_pairs={{0,16},{16,0},{32,48},{48,32},{64,80},{80,64},{96,112},{112,96},{1... | collective-permute-start | bytes 7864328 | tf_op jit(solution)/shard_map/ppermute | solution.py:415
  36.7 76.4 %collective-permute-start.11 = (bf16[256,5120]{1,0:T(8,128)(2,1)}, bf16[256,5120]{1,0:T(8,128)(2,1)}, u32[]{:S(2)}, u32[]{:S(2)}) collective-permute-start(bf16[256,5120]{1,0:T(8,128)(2,1)} %bitcast.24), channel_id=1, source_target_pairs={{0,16},{16,0},{32,48},{48,32},{64,80},{80,64},{96,112},{112,96},{1... | collective-permute-start | bytes 7864328 | tf_op jit(solution)/shard_map/ppermute | solution.py:415
  38.2 51.4 %all-to-all-start.1 = ((bf16[16,416,128]{2,1,0:T(8,128)(2,1)}), bf16[16,416,128]{2,1,0:T(8,128)(2,1)S(1)}, u32[]{:S(2)}, u32[]{:S(2)}) async-start(bf16[16,416,128]{2,1,0:T(8,128)(2,1)} %pack_own.1), calls=%async_computation.1 | async-start | bytes 3407872 | tf_op jit(solution)/shard_map/all_to_all | solution.py:255
  45.4 151.8 %reduce-scatter.2.cloned.1.call-start = ((), (), s32[]{:S(2)}) async-start(), calls=%async_computation.7 | async-start | bytes 5898240 | tf_op jit(solution)/shard_map/reduce_scatter | solution.py:387
  45.5 15.1 %collective-permute-start.2 = (bf16[2,64,1024]{2,1,0:T(8,128)(2,1)S(1)}, bf16[2,64,1024]{2,1,0:T(8,128)(2,1)S(1)}, u32[]{:S(2)}, u32[]{:S(2)}) collective-permute-start(bf16[2,64,1024]{2,1,0:T(8,128)(2,1)S(1)} %collective-permute-done.refs_1_), channel_id=1, source_target_pairs={{0,32},{16,48},{32,64},{48,80},{64,96},{80,112},{96,128},{112,144}... | collective-permute-start | bytes 786440 | tf_op jit(solution)/shard_map/ppermute | solution.py:56
  45.6 15.0 %collective-permute-start.5 = (bf16[2,64,1024]{2,1,0:T(8,128)(2,1)S(1)}, bf16[2,64,1024]{2,1,0:T(8,128)(2,1)S(1)}, u32[]{:S(2)}, u32[]{:S(2)}) collective-permute-start(bf16[2,64,1024]{2,1,0:T(8,128)(2,1)S(1)} %collective-permute-done.1.refs_8_), channel_id=1, source_target_pairs={{0,224},{16,240},{32,0},{48,16},{64,32},{80,48},{96,64},{112,80},{... | collective-permute-start | bytes 786440 | tf_op jit(solution)/shard_map/ppermute | solution.py:60
  60.6 15.3 %collective-permute-start.3 = (bf16[2,64,1024]{2,1,0:T(8,128)(2,1)S(1)}, bf16[2,64,1024]{2,1,0:T(8,128)(2,1)S(1)}, u32[]{:S(2)}, u32[]{:S(2)}) collective-permute-start(bf16[2,64,1024]{2,1,0:T(8,128)(2,1)S(1)} %collective-permute-done.2.refs_2_), channel_id=1, source_target_pairs={{0,32},{16,48},{32,64},{48,80},{64,96},{80,112},{96,128},{112,144}... | collective-permute-start | bytes 786440 | tf_op jit(solution)/shard_map/ppermute | solution.py:56
  60.6 15.4 %collective-permute-start.6 = (bf16[2,64,1024]{2,1,0:T(8,128)(2,1)S(1)}, bf16[2,64,1024]{2,1,0:T(8,128)(2,1)S(1)}, u32[]{:S(2)}, u32[]{:S(2)}) collective-permute-start(bf16[2,64,1024]{2,1,0:T(8,128)(2,1)S(1)} %collective-permute-done.5.refs_7_), channel_id=1, source_target_pairs={{0,224},{16,240},{32,0},{48,16},{64,32},{80,48},{96,64},{112,80},{... | collective-permute-start | bytes 786440 | tf_op jit(solution)/shard_map/ppermute | solution.py:60
  75.9 9.5 %collective-permute-start.4 = (bf16[1,64,1024]{2,1,0:T(8,128)(2,1)S(1)}, bf16[1,64,1024]{2,1,0:T(8,128)(2,1)S(1)}, u32[]{:S(2)}, u32[]{:S(2)}) collective-permute-start(bf16[1,64,1024]{2,1,0:T(8,128)(2,1)S(1)} %slice.25), channel_id=1, source_target_pairs={{0,32},{16,48},{32,64},{48,80},{64,96},{80,112},{96,128},{112,144}... | collective-permute-start | bytes 393224 | tf_op jit(solution)/shard_map/ppermute | solution.py:56
  76.0 9.4 %collective-permute-start.7 = (bf16[1,64,1024]{2,1,0:T(8,128)(2,1)S(1)}, bf16[1,64,1024]{2,1,0:T(8,128)(2,1)S(1)}, u32[]{:S(2)}, u32[]{:S(2)}) collective-permute-start(bf16[1,64,1024]{2,1,0:T(8,128)(2,1)S(1)} %slice.26), channel_id=1, source_target_pairs={{0,224},{16,240},{32,0},{48,16},{64,32},{80,48},{96,64},{112,80},{... | collective-permute-start | bytes 393224 | tf_op jit(solution)/shard_map/ppermute | solution.py:60
  86.2 1.8 collective-permute-start.8
  133.1 22.5 %all-to-all-start.2 = ((bf16[16,256,128]{2,1,0:T(8,128)(2,1)}), bf16[16,256,128]{2,1,0:T(8,128)(2,1)S(1)}, u32[]{:S(2)}, u32[]{:S(2)}) async-start(bf16[16,256,128]{2,1,0:T(8,128)(2,1)} %pack_listed.1), calls=%async_computation.3 | async-start | bytes 2097152 | tf_op jit(solution)/shard_map/all_to_all | solution.py:255
  180.5 37.0 %copy-start.7 = (bf16[64,32]{1,0:T(8,128)(2,1)S(1)}, bf16[64,32]{1,0:T(8,128)(2,1)}, u32[]{:S(2)}) copy-start(bf16[64,32]{1,0:T(8,128)(2,1)} %copy-done.6) | copy-start | bytes 12292
  (2 other events, 1.3 us)
Sparse Core Ops, SparseCore 0:
  36.2 76.8 all-gather.1
  133.2 64.0 reduce-scatter.1

commit v6 on v5

--- a/solution.py
+++ b/solution.py
@@ -58,29 +58,6 @@
 
 def down_z(v):
     return lax.ppermute(v, "ctx", ring(-1))
-
-
-def choose_kernel(table, *refs):
-    own, b1, b2, b3, far_low, far_high, a3, a2, a1, mine, theirs, held = refs
-    for k, block in ((0, own), (1, b1), (2, b2), (3, b3), (5, a3), (6, a2), (7, a1)):
-        held[2 * k] = block[0]
-        held[2 * k + 1] = block[1]
-    held[8] = far_low[0]
-    held[9] = far_high[0]
-    for i in range(2):
-        mine[i] = held[table[i]]
-        theirs[i] = held[table[2 + i]]
-
-
-def choose_blocks(below, above, table):
-    paired = below[0]
-    far_low, far_high = up_z(below[3][:1]), down_z(above[3][1:])
-    out = jax.ShapeDtypeStruct(paired.shape, paired.dtype)
-    held = pltpu.VMEM((16,) + paired.shape[1:], paired.dtype)
-    call = small(choose_kernel, [out, out], "choose_blocks", 3 << 20, [held])
-    return call(in_specs=[TABLE] + [WHOLE] * 9, out_specs=[WHOLE] * 2)(
-        table, paired, *below[1:], far_low, far_high, above[3], above[2], above[1]
-    )
 
 
 def pack_own_kernel(own, queries, out):
@@ -107,22 +84,29 @@
     return call(in_specs=[WHOLE] * 2, out_specs=WHOLE)(own, queries)
 
 
-def pack_listed_kernel(table, mine, swapped, out):
+def pack_listed_kernel(table, block, out):
     for h in range(SIDE):
         at = h * 256
-        for b in range(2):
-            piece = jnp.where(
-                table[b] > 0, mine[b, :, at : at + 256], swapped[b, :, at : at + 256]
-            )
-            for y in range(SIDE):
-                out[SIDE * h + y, b * 128 : b * 128 + 64] = piece[:, :HEAD_DIM]
-                out[SIDE * h + y, b * 128 + 64 : b * 128 + 128] = piece[:, HEAD_DIM:]
-
-
-def pack_listed(table, mine, swapped):
-    out = jax.ShapeDtypeStruct((SIDE * SIDE, 256, HEAD_DIM), mine.dtype)
-    call = small(pack_listed_kernel, out, "pack_listed", 3 << 20)
-    return call(in_specs=[TABLE] + [WHOLE] * 2, out_specs=WHOLE)(table, mine, swapped)
+        for y in range(SIDE):
+            out[SIDE * h + y, :64] = block[0, :, at : at + 128]
+            out[SIDE * h + y, 64:] = block[0, :, at + 128 : at + 256]
+
+
+def pack_listed(table, everyone):
+    rows, width = everyone.shape[1], everyone.shape[2]
+    return pl.pallas_call(
+        pack_listed_kernel,
+        grid_spec=pltpu.PrefetchScalarGridSpec(
+            num_scalar_prefetch=1,
+            grid=(2,),
+            in_specs=[pl.BlockSpec((1, rows, width), lambda i, t: (t[i], 0, 0))],
+            out_specs=pl.BlockSpec((16, 128, HEAD_DIM), lambda i, t: (0, i, 0)),
+        ),
+        out_shape=jax.ShapeDtypeStruct((16, 256, HEAD_DIM), everyone.dtype),
+        compiler_params=ordinary(16),
+        cost_estimate=pl.CostEstimate(flops=0, bytes_accessed=2 << 20, transcendentals=0),
+        name="pack_listed",
+    )(table, everyone)
 
 
 def unpack_kernel(back, out):
@@ -227,122 +211,103 @@
     )(table, seen, listed)
 
 
-def exchange_rows(below, above, block_lists):
+def listed_rows(block_lists):
     ctx_count = lax.axis_size("ctx")
     blocks_total = 2 * ctx_count
     ctx_index = lax.axis_index("ctx")
-    exp_index = lax.axis_index("exp")
-    y = lax.rem(exp_index, SIDE)
-    z, core = lax.div(ctx_index, 2), lax.rem(ctx_index, 2)
-    other = ctx_index + 1 - 2 * core
-    own_blocks = jnp.stack(
-        [ctx_index, blocks_total - 1 - ctx_index, other, blocks_total - 1 - other]
-    )
+    y = lax.rem(lax.axis_index("exp"), SIDE)
+    own_blocks = jnp.stack([ctx_index, blocks_total - 1 - ctx_index])
     listed = block_lists[own_blocks]
     usable = (listed != own_blocks).astype(jnp.int32)
     holder = jnp.minimum(listed, blocks_total - 1 - listed)
-    distance = lax.rem(z + 8 - lax.div(holder, 2), 8)
-    chosen = (2 * distance + (listed >= ctx_count).astype(jnp.int32)).astype(jnp.int32)
-    local = (lax.rem(holder, 2) == core).astype(jnp.int32)
-
-    mine, theirs = choose_blocks(below, above, chosen)
-    swapped = lax.ppermute(theirs, "ctx", CORE_SWAP)
-    packed = pack_listed(local[:2], mine, swapped)
-    return packed, jnp.concatenate([y[None], usable[:2]]).astype(jnp.int32)
+    row = (2 * holder + (listed >= ctx_count).astype(jnp.int32)).astype(jnp.int32)
+    return row, jnp.concatenate([y[None], usable]).astype(jnp.int32)
 
 
 def trade(v):
     return lax.all_to_all(v, "exp", split_axis=0, concat_axis=0, tiled=True)
 
 
-def ffn_kernel(counts, refs):
-    xs, ws, outs = refs[:counts], refs[counts : counts + 6], refs[counts + 6 : 2 * counts + 6]
-    rows, gates, downs, results, act, w_sem, x_sem, o_sem = refs[2 * counts + 6 :]
+def ffn_kernel(places, n_in, refs):
+    table, xs, ws = refs[0], refs[1 : 1 + len(places)], refs[1 + len(places) : 7 + len(places)]
+    out = refs[n_in]
+    rows, gates, downs, act, results, w_sem, x_sem, o_sem = refs[n_in + 1 :]
     width, hidden = gates.shape[1], gates.shape[2]
-    step = rows.shape[1]
-    parts = []
-    for x, out in zip(xs, outs):
-        for at in range(0, x.shape[0], step):
-            parts.append((x, out, at, min(step, x.shape[0] - at)))
-    loads = [
-        pltpu.make_async_copy(
-            x.at[pl.ds(at, n), :], rows.at[k, pl.ds(0, n), :], x_sem.at[k]
+    loads, stores, at = [], [], 0
+    for k, (x, (distance, start)) in enumerate(zip(xs, places)):
+        size = x.shape[0]
+        span = pl.ds(at, size)
+        block = lax.rem(table[0] + distance + 8, 8)
+        loads.append(pltpu.make_async_copy(x, rows.at[span, :], x_sem.at[k]))
+        stores.append(
+            pltpu.make_async_copy(
+                results.at[span, :], out.at[block, pl.ds(start, size), :], o_sem.at[k]
+            )
         )
-        for k, (x, _, at, n) in enumerate(parts)
-    ]
-    stores = [
-        pltpu.make_async_copy(
-            results.at[k, pl.ds(0, n), :], out.at[pl.ds(at, n), :], o_sem.at[k]
-        )
-        for k, (_, out, at, n) in enumerate(parts)
-    ]
+        at += size
     targets = [gates.at[0], gates.at[1], gates.at[2], gates.at[3]]
     targets += [downs.at[pl.ds(0, hidden), :], downs.at[pl.ds(hidden, hidden), :]]
     order = (0, 1, 3, 4, 2, 5)
     weights = [pltpu.make_async_copy(ws[w], targets[k], w_sem.at[k]) for k, w in enumerate(order)]
-    loads[0].start()
-    for copy in weights:
+    for copy in loads + weights:
         copy.start()
-    for copy in loads[1:]:
+    for copy in loads:
+        copy.wait()
+    for half in range(2):
+        weights[2 * half].wait()
+        gate = jnp.dot(rows[...], gates[2 * half], preferred_element_type=jnp.float32)
+        weights[2 * half + 1].wait()
+        up = jnp.dot(rows[...], gates[2 * half + 1], preferred_element_type=jnp.float32)
+        act[:, half * hidden : (half + 1) * hidden] = (
+            gate / (1.0 + jnp.exp(-gate)) * up
+        ).astype(jnp.bfloat16)
+    weights[4].wait()
+    weights[5].wait()
+    block = 512
+
+    @pl.loop(0, width // block)
+    def _(c):
+        columns = pl.ds(pl.multiple_of(c * block, block), block)
+        part = jnp.dot(act[...], downs[:, columns], preferred_element_type=jnp.float32)
+        results[:, columns] = part.astype(jnp.bfloat16)
+
+    for copy in stores:
         copy.start()
-    block = 1024
-    for k, (x, out, at, n) in enumerate(parts):
-        loads[k].wait()
-        for half in range(2):
-            if k == 0:
-                weights[2 * half].wait()
-            gate = jnp.dot(rows[k, :n], gates[2 * half], preferred_element_type=jnp.float32)
-            if k == 0:
-                weights[2 * half + 1].wait()
-            up = jnp.dot(rows[k, :n], gates[2 * half + 1], preferred_element_type=jnp.float32)
-            act[:n, half * hidden : (half + 1) * hidden] = (
-                gate / (1.0 + jnp.exp(-gate)) * up
-            ).astype(jnp.bfloat16)
-        if k == 0:
-            weights[4].wait()
-            weights[5].wait()
-
-        @pl.loop(0, width // block)
-        def _(c, k=k, n=n):
-            columns = pl.ds(pl.multiple_of(c * block, block), block)
-            part = jnp.dot(act[:n], downs[:, columns], preferred_element_type=jnp.float32)
-            results[k, :n, columns] = part.astype(jnp.bfloat16)
-
-        stores[k].start()
     for copy in stores:
         copy.wait()
 
 
-def expert_rows(xs, weights, step=256):
+def expert_rows(xs, places, weights, table, earlier=None):
     width = xs[0].shape[1]
     hidden = weights[0].shape[1]
     tokens = sum(x.shape[0] for x in xs)
-    step = min(step, max(x.shape[0] for x in xs))
-    parts = sum(-(-x.shape[0] // step) for x in xs)
     far = pl.BlockSpec(memory_space=pltpu.HBM)
+    operands = [table, *xs, *weights] + ([] if earlier is None else [earlier])
+    n_in = len(operands)
     return pl.pallas_call(
-        lambda *refs: ffn_kernel(len(xs), refs),
-        in_specs=[far] * (len(xs) + 6),
-        out_specs=[far] * len(xs),
-        out_shape=[jax.ShapeDtypeStruct(x.shape, jnp.bfloat16) for x in xs],
+        lambda *refs: ffn_kernel(places, n_in, refs),
+        in_specs=[TABLE] + [far] * (n_in - 1),
+        out_specs=far,
+        out_shape=jax.ShapeDtypeStruct((8, 64, width), jnp.bfloat16),
+        input_output_aliases={} if earlier is None else {n_in - 1: 0},
         scratch_shapes=[
-            pltpu.VMEM((parts, step, width), jnp.bfloat16),
+            pltpu.VMEM((tokens, width), jnp.bfloat16),
             pltpu.VMEM((4, width, hidden), jnp.bfloat16),
             pltpu.VMEM((2 * hidden, width), jnp.bfloat16),
-            pltpu.VMEM((parts, step, width), jnp.bfloat16),
-            pltpu.VMEM((step, 2 * hidden), jnp.bfloat16),
+            pltpu.VMEM((tokens, 2 * hidden), jnp.bfloat16),
+            pltpu.VMEM((tokens, width), jnp.bfloat16),
             pltpu.SemaphoreType.DMA((6,)),
-            pltpu.SemaphoreType.DMA((parts,)),
-            pltpu.SemaphoreType.DMA((parts,)),
+            pltpu.SemaphoreType.DMA((len(xs),)),
+            pltpu.SemaphoreType.DMA((len(xs),)),
         ],
-        compiler_params=pltpu.CompilerParams(vmem_limit_bytes=60 * 1024 * 1024),
+        compiler_params=pltpu.CompilerParams(vmem_limit_bytes=58 * 1024 * 1024),
         cost_estimate=pl.CostEstimate(
             flops=12 * tokens * width * hidden,
             bytes_accessed=12 * width * hidden + 4 * tokens * width,
             transcendentals=2 * tokens * hidden,
         ),
         name="expert_rows",
-    )(*xs, *weights)
+    )(*operands)
 
 
 def slot_kernel(hidden, router, ids, out, places):
@@ -375,17 +340,35 @@
     return call(in_specs=[WHOLE] * 3, out_specs=[WHOLE] * 2)(hidden, router.T, expert_ids.T)
 
 
-def route_experts(incoming, places, weights, seen, packed, state, shape):
+def route_experts(incoming, places, weights, packed, everyone, row, state, shape):
     model_width = incoming.shape[1]
     exp_count = lax.axis_size("exp")
-    rows = lax.all_gather(
-        incoming, "ctx", axis=0, tiled=True, axis_index_groups=RINGS
-    )
-    rows, seen, packed = lax.optimization_barrier((rows, seen, packed))
-    listed = trade(packed)
-    (partial,) = expert_rows([rows], weights)
+    half = incoming.shape[0] // 2
+    table = lax.div(lax.axis_index("ctx"), 2)[None].astype(jnp.int32)
+    below, above = [incoming], [incoming]
+    for _ in range(3):
+        below.append(up_z(below[-1]))
+        above.append(down_z(above[-1]))
+    near = expert_rows(
+        [incoming, below[1], above[1], below[2], above[2]],
+        [(0, 0), (-1, 0), (1, 0), (-2, 0), (2, 0)],
+        weights,
+        table,
+    )
+    low, high, near, packed = lax.optimization_barrier((below[3], above[3], near, packed))
+    far_low, far_high = up_z(low[:half]), down_z(high[half:])
+    listed = trade(pack_listed(row, everyone))
+    seen = trade(packed)
+    far_low, far_high, listed = lax.optimization_barrier((far_low, far_high, listed))
+    partial = expert_rows(
+        [low, high, far_low, far_high], [(-3, 0), (3, 0), (4, 0), (4, half)], weights, table, near
+    )
     summed_output = lax.psum_scatter(
-        partial, "ctx", scatter_dimension=0, tiled=True, axis_index_groups=RINGS
+        partial.reshape(-1, model_width),
+        "ctx",
+        scatter_dimension=0,
+        tiled=True,
+        axis_index_groups=RINGS,
     )
     attention = unpack(trade(attend(state, seen, listed)), shape)
     summed_output, attention = lax.optimization_barrier((summed_output, attention))
@@ -417,17 +400,12 @@
     capacity = 2 * hidden.shape[0] // experts
     outgoing, places = fill_slots(hidden, router, expert_ids, experts * capacity)
     paired = pair_rows(key_states, value_state_rows)
-    outgoing, paired = lax.optimization_barrier((outgoing, paired))
+    everyone = lax.all_gather(paired, "ctx", axis=0, tiled=True)
     incoming = trade(outgoing.reshape(experts, capacity, width)).reshape(-1, width)
-    below, above = [paired, up_z(paired)], [paired, down_z(paired)]
-    incoming, below[1], above[1] = lax.optimization_barrier((incoming, below[1], above[1]))
-    for _ in range(2):
-        below.append(up_z(below[-1]))
-        above.append(down_z(above[-1]))
-    seen = trade(pack_own(below[0], queries))
-    packed, state = exchange_rows(below, above, block_lists)
+    packed = pack_own(paired, queries)
+    row, state = listed_rows(block_lists)
     attention, moe_out = route_experts(
-        incoming, places, own + other, seen, packed, state, queries.shape
+        incoming, places, own + other, packed, everyone, row, state, queries.shape
     )
     return (attention, moe_out)
 

time: 226 us -> 236 us (1.044)
  blocking collectives: 34.4 us -> 52.2 us
  waiting for transfers between devices: 91.7 us -> 77.1 us
  Pallas kernels: 34.6 us -> 47.8 us
  starting transfers between devices: 39.6 us -> 31 us
    ppermute x4, waiting for transfers between devices: 0.02 us -> 40.4 us  [down_z(): return lax.ppermute(v, 'ctx', ring(-1))]
    ppermute x4, waiting for transfers between devices: 31.2 us -> 3.7 us  [up_z(): return lax.ppermute(v, 'ctx', ring(1))]
    all_gather x1, waiting for transfers between devices: 23.4 us -> 0.02 us  [shards(): everyone = lax.all_gather(paired, 'ctx', axis=0, tiled=True)]
    all_to_all x2 -> x3, blocking collectives: 34.4 us -> 52.2 us  [trade(): return lax.all_to_all(v, 'exp', split_axis=0, concat_axis=0, tiled=True)]
    pallas_call x3, Pallas kernels: 22.3 us -> 33.9 us  [the longest x2 32.3 us: expert_rows(): pl.pallas_call(lambda *refs: ffn_kernel(places, n_in, refs), in_specs=[TA...]
    all_to_all x3 -> x2, starting transfers between devices: 21.9 us -> 13.5 us  [trade(): return lax.all_to_all(v, 'exp', split_axis=0, concat_axis=0, tiled=True)]
    unnamed x18 -> x28, local copies, waits for them, and re-layouts: 5.03 us -> 7.27 us
    all_to_all x3 -> x2, waiting for transfers between devices: 19.8 us -> 18.6 us  [trade(): return lax.all_to_all(v, 'exp', split_axis=0, concat_axis=0, tiled=True)]
  transfers between devices with their start and end apart: 17 -> 15, of which waited for: 9 -> 6; matrix products, arithmetic and copies ran while one was open for 1% -> 1% of each run, Pallas kernels for 6% -> 14%
where the time goes in v6:
time: 236 us; the launch traced here: 235 us
  waiting for transfers between devices  77.1 us (33%)
  blocking collectives  52.2 us (22%)
  Pallas kernels  47.8 us (20%)
  starting transfers between devices  31 us (13%)
  between operations  14.2 us (6%)
  local copies, waits for them, and re-layouts  11.3 us (5%)
    all_to_all x3, blocking collectives, trade(): return lax.all_to_all(v, 'exp', split_axis=0, concat_axis=0, tiled=True)  52.2 us
    ppermute x4, waiting for transfers between devices, down_z(): return lax.ppermute(v, 'ctx', ring(-1))  40.4 us
    pallas_call x2, Pallas kernels, expert_rows(): pl.pallas_call(lambda *refs: ffn_kernel(places, n_in, refs), in_specs=[TA...  32.3 us
    all_to_all x2, waiting for transfers between devices, trade(): return lax.all_to_all(v, 'exp', split_axis=0, concat_axis=0, tiled=True)  18.6 us
    ppermute x4, starting transfers between devices, down_z(): return lax.ppermute(v, 'ctx', ring(-1))  16.5 us
    reduce_scatter x1, waiting for transfers between devices, route_experts(): lax.psum_scatter(partial.reshape(-1, model_width), 'ctx', scatter_dimensi...  14.4 us
    all_to_all x2, starting transfers between devices, trade(): return lax.all_to_all(v, 'exp', split_axis=0, concat_axis=0, tiled=True)  13.5 us
    pallas_call x1, Pallas kernels, attend(): pl.pallas_call(attend_kernel, grid_spec=pltpu.PrefetchScalarGridSpec(num_...  9.04 us
  transfers between devices with their start and end apart: 15, of which 6 were waited for; matrix products, arithmetic and copies ran while one was open for 1% of the time, Pallas kernels for 14%

profile of v6, /device:TPU:2, one launch (start us, length us, event | category | flops | bytes accessed | tf_op | source)
XLA Modules:
  0.0 234.9 jit_solution(10292793117275925499)
XLA Ops:
  14.1 19.2 %all_to_all.25 = bf16[16,4,5120]{2,1,0:T(4,128)(2,1)S(1)} all-to-all(bf16[16,4,5120]{2,1,0:T(4,128)(2,1)S(1)} %reshape.104), channel_id=1, replica_groups=mesh['ctx'=16,'exp'=16] {'exp'}, dimensions={0} | all-to-all | bytes 1310720 | tf_op jit(solution)/shard_map/all_to_all | solution.py:228
  33.5 5.9 %collective-permute-start.3 = (bf16[64,5120]{1,0:T(8,128)(2,1)S(1)}, bf16[64,5120]{1,0:T(8,128)(2,1)S(1)}, u32[]{:S(2)}, u32[]{:S(2)}) collective-permute-start(bf16[64,5120]{1,0:T(8,128)(2,1)S(1)} %reshape.105.refs_1_), channel_id=1, source_target_pairs={{0,224},{16,240},{32,0},{48,16},{64,32},{80,48},{96,64},{112,80},{... | collective-permute-start | bytes 1966088 | tf_op jit(solution)/shard_map/ppermute | solution.py:60
  39.4 23.2 %collective-permute-done.3.refs_3_ = bf16[64,5120]{1,0:T(8,128)(2,1)S(1)} collective-permute-done((bf16[64,5120]{1,0:T(8,128)(2,1)S(1)}, bf16[64,5120]{1,0:T(8,128)(2,1)S(1)}, u32[]{:S(2)}, u32[]{:S(2)}) %collective-permute-start.3) | collective-permute-done | bytes 655392 | tf_op jit(solution)/shard_map/ppermute | solution.py:60
  62.6 3.5 %collective-permute-start.4 = (bf16[64,5120]{1,0:T(8,128)(2,1)S(1)}, bf16[64,5120]{1,0:T(8,128)(2,1)}, u32[]{:S(2)}, u32[]{:S(2)}) collective-permute-start(bf16[64,5120]{1,0:T(8,128)(2,1)S(1)} %collective-permute-done.3.refs_3_), channel_id=1, source_target_pairs={{0,224},{16,240},{32,0},{48,16},{64,32},{80,48},{96,64},{112,80},{... | collective-permute-start | bytes 1966088 | tf_op jit(solution)/shard_map/ppermute | solution.py:60
  66.9 12.6 %collective-permute-done.4.refs_5_ = bf16[64,5120]{1,0:T(8,128)(2,1)} collective-permute-done((bf16[64,5120]{1,0:T(8,128)(2,1)S(1)}, bf16[64,5120]{1,0:T(8,128)(2,1)}, u32[]{:S(2)}, u32[]{:S(2)}) %collective-permute-start.4) | collective-permute-done | bytes 655392 | tf_op jit(solution)/shard_map/ppermute | solution.py:60
  79.5 3.8 %collective-permute-start.5 = (bf16[64,5120]{1,0:T(8,128)(2,1)}, bf16[64,5120]{1,0:T(8,128)(2,1)S(1)}, u32[]{:S(2)}, u32[]{:S(2)}) collective-permute-start(bf16[64,5120]{1,0:T(8,128)(2,1)} %collective-permute-done.4.refs_5_), channel_id=1, source_target_pairs={{0,224},{16,240},{32,0},{48,16},{64,32},{80,48},{96,64},{112,80},{... | collective-permute-start | bytes 1966088 | tf_op jit(solution)/shard_map/ppermute | solution.py:60
  83.4 2.2 copy-done.1
  85.6 1.6 pack_listed.1
  87.2 6.3 %all-to-all-start.1 = ((bf16[16,256,128]{2,1,0:T(8,128)(2,1)}), bf16[16,256,128]{2,1,0:T(8,128)(2,1)S(1)}, u32[]{:S(2)}, u32[]{:S(2)}) async-start(bf16[16,256,128]{2,1,0:T(8,128)(2,1)} %pack_listed.1), calls=%async_computation.1 | async-start | bytes 2097152 | tf_op jit(solution)/shard_map/all_to_all | solution.py:228
  93.7 2.4 %pack_own.1 = bf16[16,416,128]{2,1,0:T(8,128)(2,1)} custom-call(bf16[2,64,1024]{2,1,0:T(8,128)(2,1)} %pair_rows.1.own, bf16[2,64,2560]{2,1,0:T(8,128)(2,1)S(1)} %copy-done.2), custom_call_target="tpu_custom_call" | custom-call | bytes 3145728 | tf_op jit(solution)/shard_map/pack_own/pallas_call | solution.py:84
  96.1 18.3 %expert_rows.2.refs_11_ = bf16[8,64,5120]{2,1,0:T(8,128)(2,1)} custom-call(s32[1]{0:T(128)} %bitcast.refs_0_, bf16[64,5120]{1,0:T(8,128)(2,1)} %copy-done.8, bf16[64,5120]{1,0:T(8,128)(2,1)} %copy-done.11, bf16[64,5120]{1,0:T(8,128)(2,1)} %copy-done.10, bf16[64,5120]{1,0:T(8,128)(2,1)} %collective-permute-done.1.refs_4_, ...), custom_call_target="tpu_custom_call" | custom-call | flops 5033164800 | bytes 22282240 | tf_op jit(solution)/shard_map/expert_rows/pallas_call | solution.py:287
  114.4 1.2 slice.6
  115.7 3.2 %collective-permute-start.10 = (bf16[32,5120]{1,0:T(8,128)(2,1)S(1)}, bf16[32,5120]{1,0:T(8,128)(2,1)S(1)}, u32[]{:S(2)}, u32[]{:S(2)}) collective-permute-start(bf16[32,5120]{1,0:T(8,128)(2,1)S(1)} %slice.7), channel_id=1, source_target_pairs={{0,224},{16,240},{32,0},{48,16},{64,32},{80,48},{96,64},{112,80},{... | collective-permute-start | bytes 983048 | tf_op jit(solution)/shard_map/ppermute | solution.py:60
  118.9 4.6 %collective-permute-done.10.refs_4_ = bf16[32,5120]{1,0:T(8,128)(2,1)S(1)} collective-permute-done((bf16[32,5120]{1,0:T(8,128)(2,1)S(1)}, bf16[32,5120]{1,0:T(8,128)(2,1)S(1)}, u32[]{:S(2)}, u32[]{:S(2)}) %collective-permute-start.10) | collective-permute-done | bytes 327712 | tf_op jit(solution)/shard_map/ppermute | solution.py:60
  123.5 3.7 %collective-permute-done.9.refs_3_ = bf16[32,5120]{1,0:T(8,128)(2,1)S(1)} collective-permute-done((bf16[32,5120]{1,0:T(8,128)(2,1)S(1)}, bf16[32,5120]{1,0:T(8,128)(2,1)S(1)}, u32[]{:S(2)}, u32[]{:S(2)}) %collective-permute-start.9) | collective-permute-done | bytes 327712 | tf_op jit(solution)/shard_map/ppermute | solution.py:56
  127.9 14.0 %expert_rows.3 = bf16[8,64,5120]{2,1,0:T(8,128)(2,1)} custom-call(s32[1]{0:T(128)} %bitcast.refs_0_, bf16[64,5120]{1,0:T(8,128)(2,1)} %collective-permute-done.2.refs_1_, bf16[64,5120]{1,0:T(8,128)(2,1)} %copy-done.9, bf16[32,5120]{1,0:T(8,128)(2,1)} %copy-done.13, bf16[32,5120]{1,0:T(8,128)(2,1)} %copy-done.12, ...), custom_call_target="tpu_custom_call", output_to_operand_aliasing={{}: (11, {})} | custom-call | flops 3019898880 | bytes 19660800 | tf_op jit(solution)/shard_map/expert_rows/pallas_call | solution.py:287
  142.0 7.2 %all-to-all-start.2 = ((bf16[16,416,128]{2,1,0:T(8,128)(2,1)}), bf16[16,416,128]{2,1,0:T(8,128)(2,1)S(1)}, u32[]{:S(2)}, u32[]{:S(2)}) async-start(bf16[16,416,128]{2,1,0:T(8,128)(2,1)} %pack_own.1), calls=%async_computation.3 | async-start | bytes 3407872 | tf_op jit(solution)/shard_map/all_to_all | solution.py:228
  149.4 18.6 %all-to-all-done.2.seen = bf16[16,416,128]{2,1,0:T(8,128)(2,1)S(1)} async-done(((bf16[16,416,128]{2,1,0:T(8,128)(2,1)}), bf16[16,416,128]{2,1,0:T(8,128)(2,1)S(1)}, u32[]{:S(2)}, u32[]{:S(2)}) %all-to-all-start.2) | async-done | bytes 1703968 | tf_op jit(solution)/shard_map/all_to_all | solution.py:228
  168.0 9.0 %attend.1 = bf16[16,160,128]{2,1,0:T(8,128)(2,1)S(1)} custom-call(s32[3]{0:T(128)S(1)} %pad_add_fusion.table, bf16[16,416,128]{2,1,0:T(8,128)(2,1)S(1)} %all-to-all-done.2.seen, bf16[16,256,128]{2,1,0:T(8,128)(2,1)S(1)} %all-to-all-done.1.listed), custom_call_target="tpu_custom_call" | custom-call | flops 2200000000 | bytes 4194304 | tf_op jit(solution)/shard_map/attend/pallas_call | solution.py:196
  177.0 14.5 %all_to_all.26.back = bf16[16,160,128]{2,1,0:T(8,128)(2,1)S(1)} all-to-all(bf16[16,160,128]{2,1,0:T(8,128)(2,1)S(1)} %attend.1), channel_id=1, replica_groups=mesh['ctx'=16,'exp'=16] {'exp'}, dimensions={0} | all-to-all | bytes 1310720 | tf_op jit(solution)/shard_map/all_to_all | solution.py:228
  192.5 14.4 %reduce-scatter.2.cloned.1.call-done = bf16[64,5120]{1,0:T(8,128)(2,1)} async-done(((bf16[512,5120]{1,0:T(8,128)(2,1)}), bf16[64,5120]{1,0:T(8,128)(2,1)}) %reduce-scatter.2.cloned.1.call-update) | async-done | bytes 655376 | tf_op jit(solution)/shard_map/reduce_scatter | solution.py:366
  206.8 1.6 reshape.107
  208.5 18.5 %all_to_all.27 = bf16[16,4,5120]{2,1,0:T(4,128)(2,1)S(1)} all-to-all(bf16[16,4,5120]{2,1,0:T(4,128)(2,1)S(1)} %reshape.107), channel_id=1, replica_groups=mesh['ctx'=16,'exp'=16] {'exp'}, dimensions={0} | all-to-all | bytes 1310720 | tf_op jit(solution)/shard_map/all_to_all | solution.py:228
  227.1 1.0 convolution_convert_fusion
  (60 shorter events, 10.1 us)
Async XLA Ops:
  7.2 59.1 %copy-start = (s32[32]{0:T(128)S(1)}, s32[32]{0:T(128)}, u32[]{:S(2)}) copy-start(s32[32]{0:T(128)} %param.13) | copy-start | bytes 388
  7.2 76.2 %all-gather.2.cloned.1.call-start = ((), (), s32[]{:S(2)}) async-start(), calls=%async_computation.6 | async-start | bytes 4456448 | tf_op jit(solution)/shard_map/all_gather | solution.py:403
  9.8 86.2 %collective-permute-start.6 = (bf16[5120,256]{1,0:T(8,128)(2,1)}, bf16[5120,256]{1,0:T(8,128)(2,1)}, u32[]{:S(2)}, u32[]{:S(2)}) collective-permute-start(bf16[5120,256]{1,0:T(8,128)(2,1)} %bitcast.19), channel_id=1, source_target_pairs={{0,16},{16,0},{32,48},{48,32},{64,80},{80,64},{96,112},{112,96},{1... | collective-permute-start | bytes 7864328 | tf_op jit(solution)/shard_map/ppermute | solution.py:398
  9.9 86.1 %collective-permute-start.7 = (bf16[5120,256]{1,0:T(8,128)(2,1)}, bf16[5120,256]{1,0:T(8,128)(2,1)}, u32[]{:S(2)}, u32[]{:S(2)}) collective-permute-start(bf16[5120,256]{1,0:T(8,128)(2,1)} %bitcast.22), channel_id=1, source_target_pairs={{0,16},{16,0},{32,48},{48,32},{64,80},{80,64},{96,112},{112,96},{1... | collective-permute-start | bytes 7864328 | tf_op jit(solution)/shard_map/ppermute | solution.py:398
  10.4 85.6 %collective-permute-start.8 = (bf16[256,5120]{1,0:T(8,128)(2,1)}, bf16[256,5120]{1,0:T(8,128)(2,1)}, u32[]{:S(2)}, u32[]{:S(2)}) collective-permute-start(bf16[256,5120]{1,0:T(8,128)(2,1)} %bitcast.25), channel_id=1, source_target_pairs={{0,16},{16,0},{32,48},{48,32},{64,80},{80,64},{96,112},{112,96},{1... | collective-permute-start | bytes 7864328 | tf_op jit(solution)/shard_map/ppermute | solution.py:398
  10.5 1.0 copy-start.3
  33.4 53.7 %copy-start.8 = (bf16[64,5120]{1,0:T(8,128)(2,1)}, bf16[64,5120]{1,0:T(8,128)(2,1)S(1)}, u32[]{:S(2)}) copy-start(bf16[64,5120]{1,0:T(8,128)(2,1)S(1)} %reshape.105.refs_1_) | copy-start | bytes 1966084
  33.5 29.2 %collective-permute-start.3 = (bf16[64,5120]{1,0:T(8,128)(2,1)S(1)}, bf16[64,5120]{1,0:T(8,128)(2,1)S(1)}, u32[]{:S(2)}, u32[]{:S(2)}) collective-permute-start(bf16[64,5120]{1,0:T(8,128)(2,1)S(1)} %reshape.105.refs_1_), channel_id=1, source_target_pairs={{0,224},{16,240},{32,0},{48,16},{64,32},{80,48},{96,64},{112,80},{... | collective-permute-start | bytes 1966088 | tf_op jit(solution)/shard_map/ppermute | solution.py:60
  39.4 26.8 %collective-permute-start = (bf16[64,5120]{1,0:T(8,128)(2,1)S(1)}, bf16[64,5120]{1,0:T(8,128)(2,1)S(1)}, u32[]{:S(2)}, u32[]{:S(2)}) collective-permute-start(bf16[64,5120]{1,0:T(8,128)(2,1)S(1)} %reshape.105.refs_1_), channel_id=1, source_target_pairs={{0,32},{16,48},{32,64},{48,80},{64,96},{80,112},{96,128},{112,144}... | collective-permute-start | bytes 1966088 | tf_op jit(solution)/shard_map/ppermute | solution.py:56
  62.6 24.6 %copy-start.10 = (bf16[64,5120]{1,0:T(8,128)(2,1)}, bf16[64,5120]{1,0:T(8,128)(2,1)S(1)}, u32[]{:S(2)}) copy-start(bf16[64,5120]{1,0:T(8,128)(2,1)S(1)} %collective-permute-done.3.refs_3_) | copy-start | bytes 1966084
  62.6 16.9 %collective-permute-start.4 = (bf16[64,5120]{1,0:T(8,128)(2,1)S(1)}, bf16[64,5120]{1,0:T(8,128)(2,1)}, u32[]{:S(2)}, u32[]{:S(2)}) collective-permute-start(bf16[64,5120]{1,0:T(8,128)(2,1)S(1)} %collective-permute-done.3.refs_3_), channel_id=1, source_target_pairs={{0,224},{16,240},{32,0},{48,16},{64,32},{80,48},{96,64},{112,80},{... | collective-permute-start | bytes 1966088 | tf_op jit(solution)/shard_map/ppermute | solution.py:60
  66.2 17.2 %copy-start.11 = (bf16[64,5120]{1,0:T(8,128)(2,1)}, bf16[64,5120]{1,0:T(8,128)(2,1)S(1)}, u32[]{:S(2)}) copy-start(bf16[64,5120]{1,0:T(8,128)(2,1)S(1)} %collective-permute-done.refs_2_) | copy-start | bytes 1966084
  66.2 17.1 %collective-permute-start.1 = (bf16[64,5120]{1,0:T(8,128)(2,1)S(1)}, bf16[64,5120]{1,0:T(8,128)(2,1)}, u32[]{:S(2)}, u32[]{:S(2)}) collective-permute-start(bf16[64,5120]{1,0:T(8,128)(2,1)S(1)} %collective-permute-done.refs_2_), channel_id=1, source_target_pairs={{0,32},{16,48},{32,64},{48,80},{64,96},{80,112},{96,128},{112,144}... | collective-permute-start | bytes 1966088 | tf_op jit(solution)/shard_map/ppermute | solution.py:56
  79.5 34.8 %collective-permute-start.5 = (bf16[64,5120]{1,0:T(8,128)(2,1)}, bf16[64,5120]{1,0:T(8,128)(2,1)S(1)}, u32[]{:S(2)}, u32[]{:S(2)}) collective-permute-start(bf16[64,5120]{1,0:T(8,128)(2,1)} %collective-permute-done.4.refs_5_), channel_id=1, source_target_pairs={{0,224},{16,240},{32,0},{48,16},{64,32},{80,48},{96,64},{112,80},{... | collective-permute-start | bytes 1966088 | tf_op jit(solution)/shard_map/ppermute | solution.py:60
  83.3 31.1 %collective-permute-start.2 = (bf16[64,5120]{1,0:T(8,128)(2,1)}, bf16[64,5120]{1,0:T(8,128)(2,1)}, u32[]{:S(2)}, u32[]{:S(2)}) collective-permute-start(bf16[64,5120]{1,0:T(8,128)(2,1)} %collective-permute-done.1.refs_4_), channel_id=1, source_target_pairs={{0,32},{16,48},{32,64},{48,80},{64,96},{80,112},{96,128},{112,144}... | collective-permute-start | bytes 1966088 | tf_op jit(solution)/shard_map/ppermute | solution.py:56
  83.4 2.2 copy-start.1
  85.5 8.1 %copy-start.2 = (bf16[2,64,2560]{2,1,0:T(8,128)(2,1)S(1)}, bf16[2,64,2560]{2,1,0:T(8,128)(2,1)}, u32[]{:S(2)}) copy-start(bf16[2,64,2560]{2,1,0:T(8,128)(2,1)} %queries.1) | copy-start | bytes 1966084
  87.2 40.0 %all-to-all-start.1 = ((bf16[16,256,128]{2,1,0:T(8,128)(2,1)}), bf16[16,256,128]{2,1,0:T(8,128)(2,1)S(1)}, u32[]{:S(2)}, u32[]{:S(2)}) async-start(bf16[16,256,128]{2,1,0:T(8,128)(2,1)} %pack_listed.1), calls=%async_computation.1 | async-start | bytes 2097152 | tf_op jit(solution)/shard_map/all_to_all | solution.py:228
  93.5 113.4 %reduce-scatter.2.cloned.1.call-start = ((), (), s32[]{:S(2)}) async-start(), calls=%async_computation.7 | async-start | bytes 5898240 | tf_op jit(solution)/shard_map/reduce_scatter | solution.py:366
  114.4 12.8 %copy-start.9 = (bf16[64,5120]{1,0:T(8,128)(2,1)}, bf16[64,5120]{1,0:T(8,128)(2,1)S(1)}, u32[]{:S(2)}) copy-start(bf16[64,5120]{1,0:T(8,128)(2,1)S(1)} %collective-permute-done.5.refs_2_) | copy-start | bytes 1966084
  115.7 7.8 %collective-permute-start.10 = (bf16[32,5120]{1,0:T(8,128)(2,1)S(1)}, bf16[32,5120]{1,0:T(8,128)(2,1)S(1)}, u32[]{:S(2)}, u32[]{:S(2)}) collective-permute-start(bf16[32,5120]{1,0:T(8,128)(2,1)S(1)} %slice.7), channel_id=1, source_target_pairs={{0,224},{16,240},{32,0},{48,16},{64,32},{80,48},{96,64},{112,80},{... | collective-permute-start | bytes 983048 | tf_op jit(solution)/shard_map/ppermute | solution.py:60
  118.9 8.3 %collective-permute-start.9 = (bf16[32,5120]{1,0:T(8,128)(2,1)S(1)}, bf16[32,5120]{1,0:T(8,128)(2,1)S(1)}, u32[]{:S(2)}, u32[]{:S(2)}) collective-permute-start(bf16[32,5120]{1,0:T(8,128)(2,1)S(1)} %slice.6), channel_id=1, source_target_pairs={{0,32},{16,48},{32,64},{48,80},{64,96},{80,112},{96,128},{112,144}... | collective-permute-start | bytes 983048 | tf_op jit(solution)/shard_map/ppermute | solution.py:56
  123.5 3.7 %copy-start.12 = (bf16[32,5120]{1,0:T(8,128)(2,1)}, bf16[32,5120]{1,0:T(8,128)(2,1)S(1)}, u32[]{:S(2)}) copy-start(bf16[32,5120]{1,0:T(8,128)(2,1)S(1)} %collective-permute-done.10.refs_4_) | copy-start | bytes 983044
  142.0 26.0 %all-to-all-start.2 = ((bf16[16,416,128]{2,1,0:T(8,128)(2,1)}), bf16[16,416,128]{2,1,0:T(8,128)(2,1)S(1)}, u32[]{:S(2)}, u32[]{:S(2)}) async-start(bf16[16,416,128]{2,1,0:T(8,128)(2,1)} %pack_own.1), calls=%async_computation.3 | async-start | bytes 3407872 | tf_op jit(solution)/shard_map/all_to_all | solution.py:228
  (5 other events, 4.1 us)
Sparse Core Ops, SparseCore 0:
  10.4 53.1 all-gather.1
  142.1 64.7 reduce-scatter.1

commit v7 on v6

--- a/solution.py
+++ b/solution.py
@@ -229,22 +229,26 @@
 
 
 def ffn_kernel(places, n_in, refs):
-    table, xs, ws = refs[0], refs[1 : 1 + len(places)], refs[1 + len(places) : 7 + len(places)]
+    count = len(places)
+    table, xs, ws = refs[0], refs[1 : 1 + count], refs[1 + count : 7 + count]
     out = refs[n_in]
     rows, gates, downs, act, results, w_sem, x_sem, o_sem = refs[n_in + 1 :]
     width, hidden = gates.shape[1], gates.shape[2]
     loads, stores, at = [], [], 0
-    for k, (x, (distance, start)) in enumerate(zip(xs, places)):
-        size = x.shape[0]
-        span = pl.ds(at, size)
-        block = lax.rem(table[0] + distance + 8, 8)
-        loads.append(pltpu.make_async_copy(x, rows.at[span, :], x_sem.at[k]))
-        stores.append(
-            pltpu.make_async_copy(
-                results.at[span, :], out.at[block, pl.ds(start, size), :], o_sem.at[k]
+    for k, x in enumerate(xs):
+        loads.append(
+            pltpu.make_async_copy(x, rows.at[pl.ds(at, x.shape[0]), :], x_sem.at[k])
+        )
+        for size, relative, number, start in places[k]:
+            block = lax.rem(table[0] + number + 8, 8) if relative else number
+            stores.append(
+                pltpu.make_async_copy(
+                    results.at[pl.ds(at, size), :],
+                    out.at[block, pl.ds(start, size), :],
+                    o_sem.at[len(stores)],
+                )
             )
-        )
-        at += size
+            at += size
     targets = [gates.at[0], gates.at[1], gates.at[2], gates.at[3]]
     targets += [downs.at[pl.ds(0, hidden), :], downs.at[pl.ds(hidden, hidden), :]]
     order = (0, 1, 3, 4, 2, 5)
@@ -298,7 +302,7 @@
             pltpu.VMEM((tokens, width), jnp.bfloat16),
             pltpu.SemaphoreType.DMA((6,)),
             pltpu.SemaphoreType.DMA((len(xs),)),
-            pltpu.SemaphoreType.DMA((len(xs),)),
+            pltpu.SemaphoreType.DMA((sum(len(p) for p in places),)),
         ],
         compiler_params=pltpu.CompilerParams(vmem_limit_bytes=58 * 1024 * 1024),
         cost_estimate=pl.CostEstimate(
@@ -343,26 +347,43 @@
 def route_experts(incoming, places, weights, packed, everyone, row, state, shape):
     model_width = incoming.shape[1]
     exp_count = lax.axis_size("exp")
-    half = incoming.shape[0] // 2
+    part = incoming.shape[0] // 2
+    half = part // 2
     table = lax.div(lax.axis_index("ctx"), 2)[None].astype(jnp.int32)
-    below, above = [incoming], [incoming]
+    rows = lax.all_gather(
+        incoming[part:], "ctx", axis=0, tiled=True, axis_index_groups=RINGS
+    )
+    kept = incoming[:part]
+    below, above = [kept], [kept]
     for _ in range(3):
         below.append(up_z(below[-1]))
         above.append(down_z(above[-1]))
     near = expert_rows(
-        [incoming, below[1], above[1], below[2], above[2]],
-        [(0, 0), (-1, 0), (1, 0), (-2, 0), (2, 0)],
+        [kept, below[1], above[1], below[2], above[2]],
+        [[(part, True, d, 0)] for d in (0, -1, 1, -2, 2)],
         weights,
         table,
     )
-    low, high, near, packed = lax.optimization_barrier((below[3], above[3], near, packed))
-    far_low, far_high = up_z(low[:half]), down_z(high[half:])
+    far_low, far_high = up_z(below[3][:half]), down_z(above[3][half:])
+    seen = trade(packed)
+    near, far_low, far_high, rows, seen = lax.optimization_barrier(
+        (near, far_low, far_high, rows, seen)
+    )
+    partial = expert_rows(
+        [below[3], above[3], far_low, far_high, rows],
+        [
+            [(part, True, -3, 0)],
+            [(part, True, 3, 0)],
+            [(half, True, 4, 0)],
+            [(half, True, 4, half)],
+            [(part, False, j, part) for j in range(8)],
+        ],
+        weights,
+        table,
+        near,
+    )
+    everyone, partial = lax.optimization_barrier((everyone, partial))
     listed = trade(pack_listed(row, everyone))
-    seen = trade(packed)
-    far_low, far_high, listed = lax.optimization_barrier((far_low, far_high, listed))
-    partial = expert_rows(
-        [low, high, far_low, far_high], [(-3, 0), (3, 0), (4, 0), (4, half)], weights, table, near
-    )
     summed_output = lax.psum_scatter(
         partial.reshape(-1, model_width),
         "ctx",

time: 236 us -> 228 us (0.966)
  waiting for transfers between devices: 77.1 us -> 71.4 us
    ppermute x4, waiting for transfers between devices: 40.4 us -> 31.6 us  [down_z(): return lax.ppermute(v, 'ctx', ring(-1))]
    all_gather x1, waiting for transfers between devices: 0.02 us -> 7.4 us  [shards(): everyone = lax.all_gather(paired, 'ctx', axis=0, tiled=True)]
    all_to_all x2, waiting for transfers between devices: 18.6 us -> 15.4 us  [trade(): return lax.all_to_all(v, 'exp', split_axis=0, concat_axis=0, tiled=True)]
    unnamed x28 -> x26, local copies, waits for them, and re-layouts: 7.27 us -> 4.77 us
  transfers between devices with their start and end apart: 15 -> 16, of which waited for: 6 -> 9; matrix products, arithmetic and copies ran while one was open for 1% -> 1% of each run, Pallas kernels for 14% -> 21%
where the time goes in v7:
time: 228 us; the launch traced here: 227 us
  waiting for transfers between devices  71.4 us (31%)
  blocking collectives  53.4 us (23%)
  Pallas kernels  48.4 us (21%)
  starting transfers between devices  29.4 us (13%)
  between operations  14 us (6%)
  local copies, waits for them, and re-layouts  9.23 us (4%)
    all_to_all x3, blocking collectives, trade(): return lax.all_to_all(v, 'exp', split_axis=0, concat_axis=0, tiled=True)  53.4 us
    pallas_call x2, Pallas kernels, expert_rows(): pl.pallas_call(lambda *refs: ffn_kernel(places, n_in, refs), in_specs=[TA...  32.8 us
    ppermute x4, waiting for transfers between devices, down_z(): return lax.ppermute(v, 'ctx', ring(-1))  31.6 us
    ppermute x4, starting transfers between devices, down_z(): return lax.ppermute(v, 'ctx', ring(-1))  16.6 us
    all_to_all x2, waiting for transfers between devices, trade(): return lax.all_to_all(v, 'exp', split_axis=0, concat_axis=0, tiled=True)  15.4 us
    reduce_scatter x1, waiting for transfers between devices, route_experts(): lax.psum_scatter(partial.reshape(-1, model_width), 'ctx', scatter_dimensi...  12.8 us
    all_to_all x2, starting transfers between devices, trade(): return lax.all_to_all(v, 'exp', split_axis=0, concat_axis=0, tiled=True)  12 us
    pallas_call x1, Pallas kernels, attend(): pl.pallas_call(attend_kernel, grid_spec=pltpu.PrefetchScalarGridSpec(num_...  9.04 us
  transfers between devices with their start and end apart: 16, of which 9 were waited for; matrix products, arithmetic and copies ran while one was open for 1% of the time, Pallas kernels for 21%

profile of v7, /device:TPU:2, one launch (start us, length us, event | category | flops | bytes accessed | tf_op | source)
XLA Modules:
  0.0 227.0 jit_solution(8133741119606706294)
XLA Ops:
  10.8 18.6 %all_to_all.25 = bf16[16,4,5120]{2,1,0:T(4,128)(2,1)S(1)} all-to-all(bf16[16,4,5120]{2,1,0:T(4,128)(2,1)S(1)} %reshape.104), channel_id=1, replica_groups=mesh['ctx'=16,'exp'=16] {'exp'}, dimensions={0} | all-to-all | bytes 1310720 | tf_op jit(solution)/shard_map/all_to_all | solution.py:228
  32.1 2.4 %pack_own.1 = bf16[16,416,128]{2,1,0:T(8,128)(2,1)} custom-call(bf16[2,64,1024]{2,1,0:T(8,128)(2,1)} %pair_rows.1.own, bf16[2,64,2560]{2,1,0:T(8,128)(2,1)S(1)} %copy-done.2), custom_call_target="tpu_custom_call" | custom-call | bytes 3145728 | tf_op jit(solution)/shard_map/pack_own/pallas_call | solution.py:84
  34.5 5.1 %all-to-all-start.1 = ((bf16[16,416,128]{2,1,0:T(8,128)(2,1)}), bf16[16,416,128]{2,1,0:T(8,128)(2,1)S(1)}, u32[]{:S(2)}, u32[]{:S(2)}) async-start(bf16[16,416,128]{2,1,0:T(8,128)(2,1)} %pack_own.1), calls=%async_computation.1 | async-start | bytes 3407872 | tf_op jit(solution)/shard_map/all_to_all | solution.py:228
  39.7 5.9 %collective-permute-start.3 = (bf16[32,5120]{1,0:T(8,128)(2,1)S(1)}, bf16[32,5120]{1,0:T(8,128)(2,1)S(1)}, u32[]{:S(2)}, u32[]{:S(2)}) collective-permute-start(bf16[32,5120]{1,0:T(8,128)(2,1)S(1)} %slice.19.refs_1_), channel_id=1, source_target_pairs={{0,224},{16,240},{32,0},{48,16},{64,32},{80,48},{96,64},{112,80},{... | collective-permute-start | bytes 983048 | tf_op jit(solution)/shard_map/ppermute | solution.py:60
  45.6 13.1 %collective-permute-done.3.refs_3_ = bf16[32,5120]{1,0:T(8,128)(2,1)S(1)} collective-permute-done((bf16[32,5120]{1,0:T(8,128)(2,1)S(1)}, bf16[32,5120]{1,0:T(8,128)(2,1)S(1)}, u32[]{:S(2)}, u32[]{:S(2)}) %collective-permute-start.3) | collective-permute-done | bytes 327712 | tf_op jit(solution)/shard_map/ppermute | solution.py:60
  58.7 3.7 %collective-permute-start.4 = (bf16[32,5120]{1,0:T(8,128)(2,1)S(1)}, bf16[32,5120]{1,0:T(8,128)(2,1)}, u32[]{:S(2)}, u32[]{:S(2)}) collective-permute-start(bf16[32,5120]{1,0:T(8,128)(2,1)S(1)} %collective-permute-done.3.refs_3_), channel_id=1, source_target_pairs={{0,224},{16,240},{32,0},{48,16},{64,32},{80,48},{96,64},{112,80},{... | collective-permute-start | bytes 983048 | tf_op jit(solution)/shard_map/ppermute | solution.py:60
  62.4 1.5 collective-permute-done.refs_2_
  64.0 11.9 %collective-permute-done.4.refs_5_ = bf16[32,5120]{1,0:T(8,128)(2,1)} collective-permute-done((bf16[32,5120]{1,0:T(8,128)(2,1)S(1)}, bf16[32,5120]{1,0:T(8,128)(2,1)}, u32[]{:S(2)}, u32[]{:S(2)}) %collective-permute-start.4) | collective-permute-done | bytes 327712 | tf_op jit(solution)/shard_map/ppermute | solution.py:60
  75.8 3.8 %collective-permute-start.5 = (bf16[32,5120]{1,0:T(8,128)(2,1)}, bf16[32,5120]{1,0:T(8,128)(2,1)S(1)}, u32[]{:S(2)}, u32[]{:S(2)}) collective-permute-start(bf16[32,5120]{1,0:T(8,128)(2,1)} %collective-permute-done.4.refs_5_), channel_id=1, source_target_pairs={{0,224},{16,240},{32,0},{48,16},{64,32},{80,48},{96,64},{112,80},{... | collective-permute-start | bytes 983048 | tf_op jit(solution)/shard_map/ppermute | solution.py:60
  79.6 2.4 %collective-permute-done.1.refs_4_ = bf16[32,5120]{1,0:T(8,128)(2,1)} collective-permute-done((bf16[32,5120]{1,0:T(8,128)(2,1)S(1)}, bf16[32,5120]{1,0:T(8,128)(2,1)}, u32[]{:S(2)}, u32[]{:S(2)}) %collective-permute-start.1) | collective-permute-done | bytes 327712 | tf_op jit(solution)/shard_map/ppermute | solution.py:56
  82.0 6.6 %collective-permute-done.5.refs_2_ = bf16[32,5120]{1,0:T(8,128)(2,1)S(1)} collective-permute-done((bf16[32,5120]{1,0:T(8,128)(2,1)}, bf16[32,5120]{1,0:T(8,128)(2,1)S(1)}, u32[]{:S(2)}, u32[]{:S(2)}) %collective-permute-start.5) | collective-permute-done | bytes 327712 | tf_op jit(solution)/shard_map/ppermute | solution.py:60
  88.7 3.1 %collective-permute-start.10 = (bf16[16,5120]{1,0:T(8,128)(2,1)S(1)}, bf16[16,5120]{1,0:T(8,128)(2,1)}, u32[]{:S(2)}, u32[]{:S(2)}) collective-permute-start(bf16[16,5120]{1,0:T(8,128)(2,1)S(1)} %slice.28), channel_id=1, source_target_pairs={{0,224},{16,240},{32,0},{48,16},{64,32},{80,48},{96,64},{112,80},{... | collective-permute-start | bytes 491528 | tf_op jit(solution)/shard_map/ppermute | solution.py:60
  92.8 13.1 %expert_rows.2.refs_12_ = bf16[8,64,5120]{2,1,0:T(8,128)(2,1)} custom-call(s32[1]{0:T(128)} %bitcast.refs_0_, bf16[32,5120]{1,0:T(8,128)(2,1)} %copy-done.8, bf16[32,5120]{1,0:T(8,128)(2,1)} %copy-done.12, bf16[32,5120]{1,0:T(8,128)(2,1)} %copy-done.11, bf16[32,5120]{1,0:T(8,128)(2,1)} %collective-permute-done.1.refs_4_, ...), custom_call_target="tpu_custom_call" | custom-call | flops 2516582400 | bytes 19005440 | tf_op jit(solution)/shard_map/expert_rows/pallas_call | solution.py:291
  105.9 19.7 %expert_rows.3 = bf16[8,64,5120]{2,1,0:T(8,128)(2,1)} custom-call(s32[1]{0:T(128)} %bitcast.refs_0_, bf16[32,5120]{1,0:T(8,128)(2,1)} %copy-done.10, bf16[32,5120]{1,0:T(8,128)(2,1)} %copy-done.9, bf16[16,5120]{1,0:T(8,128)(2,1)} %collective-permute-done.9.refs_3_, ...), custom_call_target="tpu_custom_call", output_to_operand_aliasing={{}: (12, {})} | custom-call | flops 5536481280 | bytes 22937600 | tf_op jit(solution)/shard_map/expert_rows/pallas_call | solution.py:291
  125.6 7.4 %all-gather.3.cloned.1.call-done.block = bf16[32,64,1024]{2,1,0:T(8,128)(2,1)} async-done(((bf16[2,64,1024]{2,1,0:T(8,128)(2,1)}), bf16[32,64,1024]{2,1,0:T(8,128)(2,1)}) %all-gather.3.cloned.1.call-update) | async-done | bytes 4194320 | tf_op jit(solution)/shard_map/all_gather | solution.py:424
  133.8 2.2 copy-done.1
  136.0 1.7 pack_listed.1
  137.6 7.0 %all-to-all-start.2 = ((bf16[16,256,128]{2,1,0:T(8,128)(2,1)}), bf16[16,256,128]{2,1,0:T(8,128)(2,1)S(1)}, u32[]{:S(2)}, u32[]{:S(2)}) async-start(bf16[16,256,128]{2,1,0:T(8,128)(2,1)} %pack_listed.1), calls=%async_computation.3 | async-start | bytes 2097152 | tf_op jit(solution)/shard_map/all_to_all | solution.py:228
  144.8 15.3 %all-to-all-done.2.listed = bf16[16,256,128]{2,1,0:T(8,128)(2,1)S(1)} async-done(((bf16[16,256,128]{2,1,0:T(8,128)(2,1)}), bf16[16,256,128]{2,1,0:T(8,128)(2,1)S(1)}, u32[]{:S(2)}, u32[]{:S(2)}) %all-to-all-start.2) | async-done | bytes 1048608 | tf_op jit(solution)/shard_map/all_to_all | solution.py:228
  160.1 9.0 %attend.1 = bf16[16,160,128]{2,1,0:T(8,128)(2,1)S(1)} custom-call(s32[3]{0:T(128)S(1)} %pad_add_fusion.table, bf16[16,416,128]{2,1,0:T(8,128)(2,1)S(1)} %all-to-all-done.1.seen, bf16[16,256,128]{2,1,0:T(8,128)(2,1)S(1)} %all-to-all-done.2.listed), custom_call_target="tpu_custom_call" | custom-call | flops 2200000000 | bytes 4194304 | tf_op jit(solution)/shard_map/attend/pallas_call | solution.py:196
  169.2 16.3 %all_to_all.26.back = bf16[16,160,128]{2,1,0:T(8,128)(2,1)S(1)} all-to-all(bf16[16,160,128]{2,1,0:T(8,128)(2,1)S(1)} %attend.1), channel_id=1, replica_groups=mesh['ctx'=16,'exp'=16] {'exp'}, dimensions={0} | all-to-all | bytes 1310720 | tf_op jit(solution)/shard_map/all_to_all | solution.py:228
  186.5 12.8 %reduce-scatter.2.cloned.1.call-done = bf16[64,5120]{1,0:T(8,128)(2,1)} async-done(((bf16[512,5120]{1,0:T(8,128)(2,1)}), bf16[64,5120]{1,0:T(8,128)(2,1)}) %reduce-scatter.2.cloned.1.call-update) | async-done | bytes 655376 | tf_op jit(solution)/shard_map/reduce_scatter | solution.py:387
  199.3 1.6 reshape.106
  200.9 18.5 %all_to_all.27 = bf16[16,4,5120]{2,1,0:T(4,128)(2,1)S(1)} all-to-all(bf16[16,4,5120]{2,1,0:T(4,128)(2,1)S(1)} %reshape.106), channel_id=1, replica_groups=mesh['ctx'=16,'exp'=16] {'exp'}, dimensions={0} | all-to-all | bytes 1310720 | tf_op jit(solution)/shard_map/all_to_all | solution.py:228
  (63 shorter events, 10.3 us)
Async XLA Ops:
  7.2 126.0 %copy-start = (s32[32]{0:T(128)S(1)}, s32[32]{0:T(128)}, u32[]{:S(2)}) copy-start(s32[32]{0:T(128)} %param.13) | copy-start | bytes 388
  7.2 98.7 %all-gather.5.cloned.1.call-start = ((), (), s32[]{:S(2)}) async-start(), calls=%async_computation.7 | async-start | bytes 2949120 | tf_op jit(solution)/shard_map/all_gather | solution.py:353
  9.8 20.8 %copy-start.5 = (bf16[2,64,512]{2,1,0:T(8,128)(2,1)S(1)}, bf16[2,64,512]{2,1,0:T(8,128)(2,1)}, u32[]{:S(2)}) copy-start(bf16[2,64,512]{2,1,0:T(8,128)(2,1)} %keys.1) | copy-start | bytes 393220
  9.8 20.8 %copy-start.6 = (bf16[2,64,512]{2,1,0:T(8,128)(2,1)S(1)}, bf16[2,64,512]{2,1,0:T(8,128)(2,1)}, u32[]{:S(2)}) copy-start(bf16[2,64,512]{2,1,0:T(8,128)(2,1)} %values.1) | copy-start | bytes 393220
  10.6 21.5 %copy-start.2 = (bf16[2,64,2560]{2,1,0:T(8,128)(2,1)S(1)}, bf16[2,64,2560]{2,1,0:T(8,128)(2,1)}, u32[]{:S(2)}) copy-start(bf16[2,64,2560]{2,1,0:T(8,128)(2,1)} %queries.1) | copy-start | bytes 1966084
  30.5 102.5 %all-gather.3.cloned.1.call-start = ((), (), s32[]{:S(2)}) async-start(), calls=%async_computation.6 | async-start | bytes 4456448 | tf_op jit(solution)/shard_map/all_gather | solution.py:424
  31.4 61.3 %collective-permute-start.6 = (bf16[5120,256]{1,0:T(8,128)(2,1)}, bf16[5120,256]{1,0:T(8,128)(2,1)}, u32[]{:S(2)}, u32[]{:S(2)}) collective-permute-start(bf16[5120,256]{1,0:T(8,128)(2,1)} %bitcast.19), channel_id=1, source_target_pairs={{0,16},{16,0},{32,48},{48,32},{64,80},{80,64},{96,112},{112,96},{1... | collective-permute-start | bytes 7864328 | tf_op jit(solution)/shard_map/ppermute | solution.py:419
  31.5 61.2 %collective-permute-start.7 = (bf16[5120,256]{1,0:T(8,128)(2,1)}, bf16[5120,256]{1,0:T(8,128)(2,1)}, u32[]{:S(2)}, u32[]{:S(2)}) collective-permute-start(bf16[5120,256]{1,0:T(8,128)(2,1)} %bitcast.22), channel_id=1, source_target_pairs={{0,16},{16,0},{32,48},{48,32},{64,80},{80,64},{96,112},{112,96},{1... | collective-permute-start | bytes 7864328 | tf_op jit(solution)/shard_map/ppermute | solution.py:419
  32.0 60.7 %collective-permute-start.8 = (bf16[256,5120]{1,0:T(8,128)(2,1)}, bf16[256,5120]{1,0:T(8,128)(2,1)}, u32[]{:S(2)}, u32[]{:S(2)}) collective-permute-start(bf16[256,5120]{1,0:T(8,128)(2,1)} %bitcast.25), channel_id=1, source_target_pairs={{0,16},{16,0},{32,48},{48,32},{64,80},{80,64},{96,112},{112,96},{1... | collective-permute-start | bytes 7864328 | tf_op jit(solution)/shard_map/ppermute | solution.py:419
  34.5 71.4 %all-to-all-start.1 = ((bf16[16,416,128]{2,1,0:T(8,128)(2,1)}), bf16[16,416,128]{2,1,0:T(8,128)(2,1)S(1)}, u32[]{:S(2)}, u32[]{:S(2)}) async-start(bf16[16,416,128]{2,1,0:T(8,128)(2,1)} %pack_own.1), calls=%async_computation.1 | async-start | bytes 3407872 | tf_op jit(solution)/shard_map/all_to_all | solution.py:228
  39.5 159.7 %reduce-scatter.2.cloned.1.call-start = ((), (), s32[]{:S(2)}) async-start(), calls=%async_computation.8 | async-start | bytes 5898240 | tf_op jit(solution)/shard_map/reduce_scatter | solution.py:387
  39.7 53.1 %copy-start.8 = (bf16[32,5120]{1,0:T(8,128)(2,1)}, bf16[32,5120]{1,0:T(8,128)(2,1)S(1)}, u32[]{:S(2)}) copy-start(bf16[32,5120]{1,0:T(8,128)(2,1)S(1)} %slice.19.refs_1_) | copy-start | bytes 983044
  39.7 19.0 %collective-permute-start.3 = (bf16[32,5120]{1,0:T(8,128)(2,1)S(1)}, bf16[32,5120]{1,0:T(8,128)(2,1)S(1)}, u32[]{:S(2)}, u32[]{:S(2)}) collective-permute-start(bf16[32,5120]{1,0:T(8,128)(2,1)S(1)} %slice.19.refs_1_), channel_id=1, source_target_pairs={{0,224},{16,240},{32,0},{48,16},{64,32},{80,48},{96,64},{112,80},{... | collective-permute-start | bytes 983048 | tf_op jit(solution)/shard_map/ppermute | solution.py:60
  45.6 18.3 %collective-permute-start = (bf16[32,5120]{1,0:T(8,128)(2,1)S(1)}, bf16[32,5120]{1,0:T(8,128)(2,1)S(1)}, u32[]{:S(2)}, u32[]{:S(2)}) collective-permute-start(bf16[32,5120]{1,0:T(8,128)(2,1)S(1)} %slice.19.refs_1_), channel_id=1, source_target_pairs={{0,32},{16,48},{32,64},{48,80},{64,96},{80,112},{96,128},{112,144}... | collective-permute-start | bytes 983048 | tf_op jit(solution)/shard_map/ppermute | solution.py:56
  58.7 34.0 %copy-start.11 = (bf16[32,5120]{1,0:T(8,128)(2,1)}, bf16[32,5120]{1,0:T(8,128)(2,1)S(1)}, u32[]{:S(2)}) copy-start(bf16[32,5120]{1,0:T(8,128)(2,1)S(1)} %collective-permute-done.3.refs_3_) | copy-start | bytes 983044
  58.7 17.1 %collective-permute-start.4 = (bf16[32,5120]{1,0:T(8,128)(2,1)S(1)}, bf16[32,5120]{1,0:T(8,128)(2,1)}, u32[]{:S(2)}, u32[]{:S(2)}) collective-permute-start(bf16[32,5120]{1,0:T(8,128)(2,1)S(1)} %collective-permute-done.3.refs_3_), channel_id=1, source_target_pairs={{0,224},{16,240},{32,0},{48,16},{64,32},{80,48},{96,64},{112,80},{... | collective-permute-start | bytes 983048 | tf_op jit(solution)/shard_map/ppermute | solution.py:60
  64.0 28.8 %copy-start.12 = (bf16[32,5120]{1,0:T(8,128)(2,1)}, bf16[32,5120]{1,0:T(8,128)(2,1)S(1)}, u32[]{:S(2)}) copy-start(bf16[32,5120]{1,0:T(8,128)(2,1)S(1)} %collective-permute-done.refs_2_) | copy-start | bytes 983044
  64.0 18.1 %collective-permute-start.1 = (bf16[32,5120]{1,0:T(8,128)(2,1)S(1)}, bf16[32,5120]{1,0:T(8,128)(2,1)}, u32[]{:S(2)}, u32[]{:S(2)}) collective-permute-start(bf16[32,5120]{1,0:T(8,128)(2,1)S(1)} %collective-permute-done.refs_2_), channel_id=1, source_target_pairs={{0,32},{16,48},{32,64},{48,80},{64,96},{80,112},{96,128},{112,144}... | collective-permute-start | bytes 983048 | tf_op jit(solution)/shard_map/ppermute | solution.py:56
  75.8 12.9 %collective-permute-start.5 = (bf16[32,5120]{1,0:T(8,128)(2,1)}, bf16[32,5120]{1,0:T(8,128)(2,1)S(1)}, u32[]{:S(2)}, u32[]{:S(2)}) collective-permute-start(bf16[32,5120]{1,0:T(8,128)(2,1)} %collective-permute-done.4.refs_5_), channel_id=1, source_target_pairs={{0,224},{16,240},{32,0},{48,16},{64,32},{80,48},{96,64},{112,80},{... | collective-permute-start | bytes 983048 | tf_op jit(solution)/shard_map/ppermute | solution.py:60
  82.0 10.0 %collective-permute-start.2 = (bf16[32,5120]{1,0:T(8,128)(2,1)}, bf16[32,5120]{1,0:T(8,128)(2,1)S(1)}, u32[]{:S(2)}, u32[]{:S(2)}) collective-permute-start(bf16[32,5120]{1,0:T(8,128)(2,1)} %collective-permute-done.1.refs_4_), channel_id=1, source_target_pairs={{0,32},{16,48},{32,64},{48,80},{64,96},{80,112},{96,128},{112,144}... | collective-permute-start | bytes 983048 | tf_op jit(solution)/shard_map/ppermute | solution.py:56
  88.7 17.1 %copy-start.9 = (bf16[32,5120]{1,0:T(8,128)(2,1)}, bf16[32,5120]{1,0:T(8,128)(2,1)S(1)}, u32[]{:S(2)}) copy-start(bf16[32,5120]{1,0:T(8,128)(2,1)S(1)} %collective-permute-done.5.refs_2_) | copy-start | bytes 983044
  88.7 17.2 %collective-permute-start.10 = (bf16[16,5120]{1,0:T(8,128)(2,1)S(1)}, bf16[16,5120]{1,0:T(8,128)(2,1)}, u32[]{:S(2)}, u32[]{:S(2)}) collective-permute-start(bf16[16,5120]{1,0:T(8,128)(2,1)S(1)} %slice.28), channel_id=1, source_target_pairs={{0,224},{16,240},{32,0},{48,16},{64,32},{80,48},{96,64},{112,80},{... | collective-permute-start | bytes 491528 | tf_op jit(solution)/shard_map/ppermute | solution.py:60
  92.7 13.2 %collective-permute-start.9 = (bf16[16,5120]{1,0:T(8,128)(2,1)}, bf16[16,5120]{1,0:T(8,128)(2,1)}, u32[]{:S(2)}, u32[]{:S(2)}) collective-permute-start(bf16[16,5120]{1,0:T(8,128)(2,1)} %slice.27), channel_id=1, source_target_pairs={{0,32},{16,48},{32,64},{48,80},{64,96},{80,112},{96,128},{112,144}... | collective-permute-start | bytes 491528 | tf_op jit(solution)/shard_map/ppermute | solution.py:56
  137.6 22.5 %all-to-all-start.2 = ((bf16[16,256,128]{2,1,0:T(8,128)(2,1)}), bf16[16,256,128]{2,1,0:T(8,128)(2,1)S(1)}, u32[]{:S(2)}, u32[]{:S(2)}) async-start(bf16[16,256,128]{2,1,0:T(8,128)(2,1)} %pack_listed.1), calls=%async_computation.3 | async-start | bytes 2097152 | tf_op jit(solution)/shard_map/all_to_all | solution.py:228
  (5 other events, 18.6 us)
Sparse Core Ops, SparseCore 0:
  30.6 57.0 all-gather.4
  89.6 43.3 all-gather.2
  135.6 63.6 reduce-scatter.1

commit v8 on v5

--- a/solution.py
+++ b/solution.py
@@ -258,7 +258,7 @@
 def ffn_kernel(counts, refs):
     xs, ws, outs = refs[:counts], refs[counts : counts + 6], refs[counts + 6 : 2 * counts + 6]
     rows, gates, downs, results, act, w_sem, x_sem, o_sem = refs[2 * counts + 6 :]
-    width, hidden = gates.shape[1], gates.shape[2]
+    width, hidden = gates.shape[1], gates.shape[2] // 2
     step = rows.shape[1]
     parts = []
     for x, out in zip(xs, outs):
@@ -276,7 +276,7 @@
         )
         for k, (_, out, at, n) in enumerate(parts)
     ]
-    targets = [gates.at[0], gates.at[1], gates.at[2], gates.at[3]]
+    targets = [gates.at[h, :, pl.ds(c * hidden, hidden)] for h in range(2) for c in range(2)]
     targets += [downs.at[pl.ds(0, hidden), :], downs.at[pl.ds(hidden, hidden), :]]
     order = (0, 1, 3, 4, 2, 5)
     weights = [pltpu.make_async_copy(ws[w], targets[k], w_sem.at[k]) for k, w in enumerate(order)]
@@ -291,10 +291,9 @@
         for half in range(2):
             if k == 0:
                 weights[2 * half].wait()
-            gate = jnp.dot(rows[k, :n], gates[2 * half], preferred_element_type=jnp.float32)
-            if k == 0:
                 weights[2 * half + 1].wait()
-            up = jnp.dot(rows[k, :n], gates[2 * half + 1], preferred_element_type=jnp.float32)
+            both = jnp.dot(rows[k, :n], gates[half], preferred_element_type=jnp.float32)
+            gate, up = both[:, :hidden], both[:, hidden:]
             act[:n, half * hidden : (half + 1) * hidden] = (
                 gate / (1.0 + jnp.exp(-gate)) * up
             ).astype(jnp.bfloat16)
@@ -327,7 +326,7 @@
         out_shape=[jax.ShapeDtypeStruct(x.shape, jnp.bfloat16) for x in xs],
         scratch_shapes=[
             pltpu.VMEM((parts, step, width), jnp.bfloat16),
-            pltpu.VMEM((4, width, hidden), jnp.bfloat16),
+            pltpu.VMEM((2, width, 2 * hidden), jnp.bfloat16),
             pltpu.VMEM((2 * hidden, width), jnp.bfloat16),
             pltpu.VMEM((parts, step, width), jnp.bfloat16),
             pltpu.VMEM((step, 2 * hidden), jnp.bfloat16),
@@ -417,13 +416,14 @@
     capacity = 2 * hidden.shape[0] // experts
     outgoing, places = fill_slots(hidden, router, expert_ids, experts * capacity)
     paired = pair_rows(key_states, value_state_rows)
-    outgoing, paired = lax.optimization_barrier((outgoing, paired))
     incoming = trade(outgoing.reshape(experts, capacity, width)).reshape(-1, width)
-    below, above = [paired, up_z(paired)], [paired, down_z(paired)]
-    incoming, below[1], above[1] = lax.optimization_barrier((incoming, below[1], above[1]))
-    for _ in range(2):
+    below, above = [paired], [paired]
+    for _ in range(3):
         below.append(up_z(below[-1]))
         above.append(down_z(above[-1]))
+    incoming, below[3], above[3] = lax.optimization_barrier(
+        (incoming, below[3], above[3])
+    )
     seen = trade(pack_own(below[0], queries))
     packed, state = exchange_rows(below, above, block_lists)
     attention, moe_out = route_experts(

time: 226 us -> 221 us (0.978)
  Pallas kernels: 34.6 us -> 31.6 us
    ppermute x4, waiting for transfers between devices: 31.2 us -> 4.99 us  [up_z(): return lax.ppermute(v, 'ctx', ring(1))]
    ppermute x4, waiting for transfers between devices: 0.02 us -> 14.1 us  [down_z(): return lax.ppermute(v, 'ctx', ring(-1))]
    all_gather x1, waiting for transfers between devices: 23.4 us -> 31.9 us  [route_experts(): lax.all_gather(incoming, 'ctx', axis=0, tiled=True, axis_index_groups=RINGS)]
    all_to_all x3, waiting for transfers between devices: 19.8 us -> 23.3 us  [trade(): return lax.all_to_all(v, 'exp', split_axis=0, concat_axis=0, tiled=True)]
    ppermute x4, starting transfers between devices: 16.5 us -> 13 us  [down_z(): return lax.ppermute(v, 'ctx', ring(-1))]
    pallas_call x1, Pallas kernels: 20 us -> 17 us  [expert_rows(): pl.pallas_call(lambda *refs: ffn_kernel(len(xs), refs), in_specs=[far] *...]
  transfers between devices with their start and end apart: 17 -> 17, of which waited for: 9 -> 10; matrix products, arithmetic and copies ran while one was open for 1% -> 1% of each run, Pallas kernels for 6% -> 7%
where the time goes in v8:
time: 221 us; the launch traced here: 220 us
  waiting for transfers between devices  91.6 us (41%)
  starting transfers between devices  38.1 us (17%)
  blocking collectives  34.1 us (15%)
  Pallas kernels  31.6 us (14%)
  between operations  14.2 us (6%)
  local copies, waits for them, and re-layouts  8.85 us (4%)
    all_to_all x2, blocking collectives, trade(): return lax.all_to_all(v, 'exp', split_axis=0, concat_axis=0, tiled=True)  34.1 us
    all_gather x1, waiting for transfers between devices, route_experts(): lax.all_gather(incoming, 'ctx', axis=0, tiled=True, axis_index_groups=RINGS)  31.9 us
    all_to_all x3, waiting for transfers between devices, trade(): return lax.all_to_all(v, 'exp', split_axis=0, concat_axis=0, tiled=True)  23.3 us
    all_to_all x3, starting transfers between devices, trade(): return lax.all_to_all(v, 'exp', split_axis=0, concat_axis=0, tiled=True)  22 us
    pallas_call x1, Pallas kernels, expert_rows(): pl.pallas_call(lambda *refs: ffn_kernel(len(xs), refs), in_specs=[far] *...  17 us
    reduce_scatter x1, waiting for transfers between devices, route_experts(): lax.psum_scatter(partial, 'ctx', scatter_dimension=0, tiled=True, axis_in...  15.8 us
    ppermute x4, waiting for transfers between devices, down_z(): return lax.ppermute(v, 'ctx', ring(-1))  14.1 us
    ppermute x4, starting transfers between devices, down_z(): return lax.ppermute(v, 'ctx', ring(-1))  13 us
  transfers between devices with their start and end apart: 17, of which 10 were waited for; matrix products, arithmetic and copies ran while one was open for 1% of the time, Pallas kernels for 7%

profile of v8, /device:TPU:2, one launch (start us, length us, event | category | flops | bytes accessed | tf_op | source)
XLA Modules:
  0.0 219.8 jit_solution(6294564748199654470)
XLA Ops:
  9.1 5.9 %collective-permute-start.3 = (bf16[2,64,1024]{2,1,0:T(8,128)(2,1)S(1)}, bf16[2,64,1024]{2,1,0:T(8,128)(2,1)S(1)}, u32[]{:S(2)}, u32[]{:S(2)}) collective-permute-start(bf16[2,64,1024]{2,1,0:T(8,128)(2,1)S(1)} %pair_rows.1.own.refs_0_), channel_id=1, source_target_pairs={{0,224},{16,240},{32,0},{48,16},{64,32},{80,48},{96,64},{112,80},{... | collective-permute-start | bytes 786440 | tf_op jit(solution)/shard_map/ppermute | solution.py:60
  19.4 7.5 %all-to-all-start = ((bf16[16,4,5120]{2,1,0:T(4,128)(2,1)}), bf16[16,4,5120]{2,1,0:T(4,128)(2,1)S(1)}, u32[]{:S(2)}, u32[]{:S(2)}) async-start(bf16[16,4,5120]{2,1,0:T(4,128)(2,1)} %reshape.177), calls=%async_computation | async-start | bytes 1310720 | tf_op jit(solution)/shard_map/all_to_all | solution.py:255
  27.0 3.3 %collective-permute-start.4 = (bf16[2,64,1024]{2,1,0:T(8,128)(2,1)S(1)}, bf16[2,64,1024]{2,1,0:T(8,128)(2,1)S(1)}, u32[]{:S(2)}, u32[]{:S(2)}) collective-permute-start(bf16[2,64,1024]{2,1,0:T(8,128)(2,1)S(1)} %collective-permute-done.3.refs_8_), channel_id=1, source_target_pairs={{0,224},{16,240},{32,0},{48,16},{64,32},{80,48},{96,64},{112,80},{... | collective-permute-start | bytes 786440 | tf_op jit(solution)/shard_map/ppermute | solution.py:60
  30.3 4.4 %collective-permute-done.4.refs_7_ = bf16[2,64,1024]{2,1,0:T(8,128)(2,1)S(1)} collective-permute-done((bf16[2,64,1024]{2,1,0:T(8,128)(2,1)S(1)}, bf16[2,64,1024]{2,1,0:T(8,128)(2,1)S(1)}, u32[]{:S(2)}, u32[]{:S(2)}) %collective-permute-start.4) | collective-permute-done | bytes 262176 | tf_op jit(solution)/shard_map/ppermute | solution.py:60
  34.7 3.7 %collective-permute-start.5 = (bf16[2,64,1024]{2,1,0:T(8,128)(2,1)S(1)}, bf16[2,64,1024]{2,1,0:T(8,128)(2,1)S(1)}, u32[]{:S(2)}, u32[]{:S(2)}) collective-permute-start(bf16[2,64,1024]{2,1,0:T(8,128)(2,1)S(1)} %collective-permute-done.4.refs_7_), channel_id=1, source_target_pairs={{0,224},{16,240},{32,0},{48,16},{64,32},{80,48},{96,64},{112,80},{... | collective-permute-start | bytes 786440 | tf_op jit(solution)/shard_map/ppermute | solution.py:60
  39.4 2.9 %collective-permute-done.5.refs_6_ = bf16[2,64,1024]{2,1,0:T(8,128)(2,1)S(1)} collective-permute-done((bf16[2,64,1024]{2,1,0:T(8,128)(2,1)S(1)}, bf16[2,64,1024]{2,1,0:T(8,128)(2,1)S(1)}, u32[]{:S(2)}, u32[]{:S(2)}) %collective-permute-start.5) | collective-permute-done | bytes 262176 | tf_op jit(solution)/shard_map/ppermute | solution.py:60
  42.3 3.7 %collective-permute-done.2.refs_3_ = bf16[2,64,1024]{2,1,0:T(8,128)(2,1)S(1)} collective-permute-done((bf16[2,64,1024]{2,1,0:T(8,128)(2,1)S(1)}, bf16[2,64,1024]{2,1,0:T(8,128)(2,1)S(1)}, u32[]{:S(2)}, u32[]{:S(2)}) %collective-permute-start.2) | collective-permute-done | bytes 262176 | tf_op jit(solution)/shard_map/ppermute | solution.py:56
  46.7 1.4 pack_own.1
  48.2 7.2 %all-to-all-start.1 = ((bf16[16,416,128]{2,1,0:T(8,128)(2,1)}), bf16[16,416,128]{2,1,0:T(8,128)(2,1)S(1)}, u32[]{:S(2)}, u32[]{:S(2)}) async-start(bf16[16,416,128]{2,1,0:T(8,128)(2,1)} %pack_own.1), calls=%async_computation.1 | async-start | bytes 3407872 | tf_op jit(solution)/shard_map/all_to_all | solution.py:255
  56.3 2.0 collective-permute-start.6
  58.4 6.7 %collective-permute-done.7.refs_5_ = bf16[1,64,1024]{2,1,0:T(8,128)(2,1)S(1)} collective-permute-done((bf16[1,64,1024]{2,1,0:T(8,128)(2,1)S(1)}, bf16[1,64,1024]{2,1,0:T(8,128)(2,1)S(1)}, u32[]{:S(2)}, u32[]{:S(2)}) %collective-permute-start.7) | collective-permute-done | bytes 131104 | tf_op jit(solution)/shard_map/ppermute | solution.py:60
  65.1 1.3 collective-permute-done.6.refs_4_
  67.5 1.4 collective-permute-done.8.swapped
  68.9 1.7 pack_listed.1
  70.6 8.3 %all-to-all-done.1.seen = bf16[16,416,128]{2,1,0:T(8,128)(2,1)S(1)} async-done(((bf16[16,416,128]{2,1,0:T(8,128)(2,1)}), bf16[16,416,128]{2,1,0:T(8,128)(2,1)S(1)}, u32[]{:S(2)}, u32[]{:S(2)}) %all-to-all-start.1) | async-done | bytes 1703968 | tf_op jit(solution)/shard_map/all_to_all | solution.py:255
  78.9 31.9 %all-gather.2.cloned.1.call-done.refs_0_ = bf16[512,5120]{1,0:T(8,128)(2,1)} async-done(((bf16[64,5120]{1,0:T(8,128)(2,1)}), bf16[512,5120]{1,0:T(8,128)(2,1)}) %all-gather.2.cloned.1.call-update) | async-done | bytes 5242896 | tf_op jit(solution)/shard_map/all_gather | solution.py:380
  110.9 17.0 %expert_rows.1 = bf16[512,5120]{1,0:T(8,128)(2,1)} custom-call(bf16[512,5120]{1,0:T(8,128)(2,1)} %all-gather.2.cloned.1.call-done.refs_0_, bf16[5120,256]{1,0:T(8,128)(2,1)} %bitcast.21, bf16[5120,256]{1,0:T(8,128)(2,1)} %bitcast.23, bf16[256,5120]{1,0:T(8,128)(2,1)} %bitcast.25, bf16[5120,256]{1,0:T(8,128)(2,1)} %collective-permute-done.9.refs_4_, ...), custom_call_target="tpu_custom_call" | custom-call | flops 8053063680 | bytes 26214400 | tf_op jit(solution)/shard_map/expert_rows/pallas_call | solution.py:322
  127.9 7.3 %all-to-all-start.2 = ((bf16[16,256,128]{2,1,0:T(8,128)(2,1)}), bf16[16,256,128]{2,1,0:T(8,128)(2,1)S(1)}, u32[]{:S(2)}, u32[]{:S(2)}) async-start(bf16[16,256,128]{2,1,0:T(8,128)(2,1)} %pack_listed.1), calls=%async_computation.3 | async-start | bytes 2097152 | tf_op jit(solution)/shard_map/all_to_all | solution.py:255
  135.3 15.0 %all-to-all-done.2.listed = bf16[16,256,128]{2,1,0:T(8,128)(2,1)S(1)} async-done(((bf16[16,256,128]{2,1,0:T(8,128)(2,1)}), bf16[16,256,128]{2,1,0:T(8,128)(2,1)S(1)}, u32[]{:S(2)}, u32[]{:S(2)}) %all-to-all-start.2) | async-done | bytes 1048608 | tf_op jit(solution)/shard_map/all_to_all | solution.py:255
  150.3 9.0 %attend.1 = bf16[16,160,128]{2,1,0:T(8,128)(2,1)S(1)} custom-call(s32[3]{0:T(128)S(1)} %pad_add_fusion.table, bf16[16,416,128]{2,1,0:T(8,128)(2,1)S(1)} %all-to-all-done.1.seen, bf16[16,256,128]{2,1,0:T(8,128)(2,1)S(1)} %all-to-all-done.2.listed), custom_call_target="tpu_custom_call" | custom-call | flops 2200000000 | bytes 4194304 | tf_op jit(solution)/shard_map/attend/pallas_call | solution.py:212
  159.3 15.6 %all_to_all.25.back = bf16[16,160,128]{2,1,0:T(8,128)(2,1)S(1)} all-to-all(bf16[16,160,128]{2,1,0:T(8,128)(2,1)S(1)} %attend.1), channel_id=1, replica_groups=mesh['ctx'=16,'exp'=16] {'exp'}, dimensions={0} | all-to-all | bytes 1310720 | tf_op jit(solution)/shard_map/all_to_all | solution.py:255
  175.9 15.8 %reduce-scatter.2.cloned.1.call-done = bf16[64,5120]{1,0:T(8,128)(2,1)} async-done(((bf16[512,5120]{1,0:T(8,128)(2,1)}), bf16[64,5120]{1,0:T(8,128)(2,1)}) %reduce-scatter.2.cloned.1.call-update) | async-done | bytes 655376 | tf_op jit(solution)/shard_map/reduce_scatter | solution.py:386
  191.7 1.6 reshape.179
  193.3 18.5 %all_to_all.26 = bf16[16,4,5120]{2,1,0:T(4,128)(2,1)S(1)} all-to-all(bf16[16,4,5120]{2,1,0:T(4,128)(2,1)S(1)} %reshape.179), channel_id=1, replica_groups=mesh['ctx'=16,'exp'=16] {'exp'}, dimensions={0} | all-to-all | bytes 1310720 | tf_op jit(solution)/shard_map/all_to_all | solution.py:255
  (55 shorter events, 12.2 us)
Async XLA Ops:
  7.2 48.4 %copy-start = (s32[32]{0:T(128)S(1)}, s32[32]{0:T(128)}, u32[]{:S(2)}) copy-start(s32[32]{0:T(128)} %param.13) | copy-start | bytes 388
  7.2 0.9 copy-start.4
  9.1 37.7 %copy-start.1 = (bf16[2,64,2560]{2,1,0:T(8,128)(2,1)S(1)}, bf16[2,64,2560]{2,1,0:T(8,128)(2,1)}, u32[]{:S(2)}) copy-start(bf16[2,64,2560]{2,1,0:T(8,128)(2,1)} %queries.1) | copy-start | bytes 1966084
  9.1 17.9 %collective-permute-start.3 = (bf16[2,64,1024]{2,1,0:T(8,128)(2,1)S(1)}, bf16[2,64,1024]{2,1,0:T(8,128)(2,1)S(1)}, u32[]{:S(2)}, u32[]{:S(2)}) collective-permute-start(bf16[2,64,1024]{2,1,0:T(8,128)(2,1)S(1)} %pair_rows.1.own.refs_0_), channel_id=1, source_target_pairs={{0,224},{16,240},{32,0},{48,16},{64,32},{80,48},{96,64},{112,80},{... | collective-permute-start | bytes 786440 | tf_op jit(solution)/shard_map/ppermute | solution.py:60
  15.0 15.3 %collective-permute-start = (bf16[2,64,1024]{2,1,0:T(8,128)(2,1)S(1)}, bf16[2,64,1024]{2,1,0:T(8,128)(2,1)S(1)}, u32[]{:S(2)}, u32[]{:S(2)}) collective-permute-start(bf16[2,64,1024]{2,1,0:T(8,128)(2,1)S(1)} %pair_rows.1.own.refs_0_), channel_id=1, source_target_pairs={{0,32},{16,48},{32,64},{48,80},{64,96},{80,112},{96,128},{112,144}... | collective-permute-start | bytes 786440 | tf_op jit(solution)/shard_map/ppermute | solution.py:56
  15.0 1.0 copy-start.2
  16.0 0.9 copy-start.3
  18.4 29.8 %copy-start.6 = (bf16[64,32]{1,0:T(8,128)(2,1)}, bf16[64,32]{1,0:T(8,128)(2,1)S(1)}, u32[]{:S(2)}) copy-start(bf16[64,32]{1,0:T(8,128)(2,1)S(1)} %get-tuple-element.24) | copy-start | bytes 12292
  19.4 19.0 %all-to-all-start = ((bf16[16,4,5120]{2,1,0:T(4,128)(2,1)}), bf16[16,4,5120]{2,1,0:T(4,128)(2,1)S(1)}, u32[]{:S(2)}, u32[]{:S(2)}) async-start(bf16[16,4,5120]{2,1,0:T(4,128)(2,1)} %reshape.177), calls=%async_computation | async-start | bytes 1310720 | tf_op jit(solution)/shard_map/all_to_all | solution.py:255
  26.9 83.9 %all-gather.2.cloned.1.call-start = ((), (), s32[]{:S(2)}) async-start(), calls=%async_computation.6 | async-start | bytes 5898240 | tf_op jit(solution)/shard_map/all_gather | solution.py:380
  27.0 7.8 %collective-permute-start.4 = (bf16[2,64,1024]{2,1,0:T(8,128)(2,1)S(1)}, bf16[2,64,1024]{2,1,0:T(8,128)(2,1)S(1)}, u32[]{:S(2)}, u32[]{:S(2)}) collective-permute-start(bf16[2,64,1024]{2,1,0:T(8,128)(2,1)S(1)} %collective-permute-done.3.refs_8_), channel_id=1, source_target_pairs={{0,224},{16,240},{32,0},{48,16},{64,32},{80,48},{96,64},{112,80},{... | collective-permute-start | bytes 786440 | tf_op jit(solution)/shard_map/ppermute | solution.py:60
  30.3 8.1 %collective-permute-start.1 = (bf16[2,64,1024]{2,1,0:T(8,128)(2,1)S(1)}, bf16[2,64,1024]{2,1,0:T(8,128)(2,1)S(1)}, u32[]{:S(2)}, u32[]{:S(2)}) collective-permute-start(bf16[2,64,1024]{2,1,0:T(8,128)(2,1)S(1)} %collective-permute-done.refs_1_), channel_id=1, source_target_pairs={{0,32},{16,48},{32,64},{48,80},{64,96},{80,112},{96,128},{112,144}... | collective-permute-start | bytes 786440 | tf_op jit(solution)/shard_map/ppermute | solution.py:56
  34.7 7.6 %collective-permute-start.5 = (bf16[2,64,1024]{2,1,0:T(8,128)(2,1)S(1)}, bf16[2,64,1024]{2,1,0:T(8,128)(2,1)S(1)}, u32[]{:S(2)}, u32[]{:S(2)}) collective-permute-start(bf16[2,64,1024]{2,1,0:T(8,128)(2,1)S(1)} %collective-permute-done.4.refs_7_), channel_id=1, source_target_pairs={{0,224},{16,240},{32,0},{48,16},{64,32},{80,48},{96,64},{112,80},{... | collective-permute-start | bytes 786440 | tf_op jit(solution)/shard_map/ppermute | solution.py:60
  38.4 7.6 %collective-permute-start.2 = (bf16[2,64,1024]{2,1,0:T(8,128)(2,1)S(1)}, bf16[2,64,1024]{2,1,0:T(8,128)(2,1)S(1)}, u32[]{:S(2)}, u32[]{:S(2)}) collective-permute-start(bf16[2,64,1024]{2,1,0:T(8,128)(2,1)S(1)} %collective-permute-done.1.refs_2_), channel_id=1, source_target_pairs={{0,32},{16,48},{32,64},{48,80},{64,96},{80,112},{96,128},{112,144}... | collective-permute-start | bytes 786440 | tf_op jit(solution)/shard_map/ppermute | solution.py:56
  46.0 64.8 %collective-permute-start.9 = (bf16[5120,256]{1,0:T(8,128)(2,1)}, bf16[5120,256]{1,0:T(8,128)(2,1)}, u32[]{:S(2)}, u32[]{:S(2)}) collective-permute-start(bf16[5120,256]{1,0:T(8,128)(2,1)} %bitcast.20), channel_id=1, source_target_pairs={{0,16},{16,0},{32,48},{48,32},{64,80},{80,64},{96,112},{112,96},{1... | collective-permute-start | bytes 7864328 | tf_op jit(solution)/shard_map/ppermute | solution.py:414
  46.1 64.7 %collective-permute-start.10 = (bf16[5120,256]{1,0:T(8,128)(2,1)}, bf16[5120,256]{1,0:T(8,128)(2,1)}, u32[]{:S(2)}, u32[]{:S(2)}) collective-permute-start(bf16[5120,256]{1,0:T(8,128)(2,1)} %bitcast.22), channel_id=1, source_target_pairs={{0,16},{16,0},{32,48},{48,32},{64,80},{80,64},{96,112},{112,96},{1... | collective-permute-start | bytes 7864328 | tf_op jit(solution)/shard_map/ppermute | solution.py:414
  46.6 64.2 %collective-permute-start.11 = (bf16[256,5120]{1,0:T(8,128)(2,1)}, bf16[256,5120]{1,0:T(8,128)(2,1)}, u32[]{:S(2)}, u32[]{:S(2)}) collective-permute-start(bf16[256,5120]{1,0:T(8,128)(2,1)} %bitcast.24), channel_id=1, source_target_pairs={{0,16},{16,0},{32,48},{48,32},{64,80},{80,64},{96,112},{112,96},{1... | collective-permute-start | bytes 7864328 | tf_op jit(solution)/shard_map/ppermute | solution.py:414
  48.2 30.7 %all-to-all-start.1 = ((bf16[16,416,128]{2,1,0:T(8,128)(2,1)}), bf16[16,416,128]{2,1,0:T(8,128)(2,1)S(1)}, u32[]{:S(2)}, u32[]{:S(2)}) async-start(bf16[16,416,128]{2,1,0:T(8,128)(2,1)} %pack_own.1), calls=%async_computation.1 | async-start | bytes 3407872 | tf_op jit(solution)/shard_map/all_to_all | solution.py:255
  55.4 136.3 %reduce-scatter.2.cloned.1.call-start = ((), (), s32[]{:S(2)}) async-start(), calls=%async_computation.7 | async-start | bytes 5898240 | tf_op jit(solution)/shard_map/reduce_scatter | solution.py:386
  56.2 8.9 %collective-permute-start.7 = (bf16[1,64,1024]{2,1,0:T(8,128)(2,1)S(1)}, bf16[1,64,1024]{2,1,0:T(8,128)(2,1)S(1)}, u32[]{:S(2)}, u32[]{:S(2)}) collective-permute-start(bf16[1,64,1024]{2,1,0:T(8,128)(2,1)S(1)} %slice.20), channel_id=1, source_target_pairs={{0,224},{16,240},{32,0},{48,16},{64,32},{80,48},{96,64},{112,80},{... | collective-permute-start | bytes 393224 | tf_op jit(solution)/shard_map/ppermute | solution.py:60
  56.3 10.0 %collective-permute-start.6 = (bf16[1,64,1024]{2,1,0:T(8,128)(2,1)S(1)}, bf16[1,64,1024]{2,1,0:T(8,128)(2,1)S(1)}, u32[]{:S(2)}, u32[]{:S(2)}) collective-permute-start(bf16[1,64,1024]{2,1,0:T(8,128)(2,1)S(1)} %slice.19), channel_id=1, source_target_pairs={{0,32},{16,48},{32,64},{48,80},{64,96},{80,112},{96,128},{112,144}... | collective-permute-start | bytes 393224 | tf_op jit(solution)/shard_map/ppermute | solution.py:56
  67.1 1.8 collective-permute-start.8
  127.9 22.4 %all-to-all-start.2 = ((bf16[16,256,128]{2,1,0:T(8,128)(2,1)}), bf16[16,256,128]{2,1,0:T(8,128)(2,1)S(1)}, u32[]{:S(2)}, u32[]{:S(2)}) async-start(bf16[16,256,128]{2,1,0:T(8,128)(2,1)} %pack_listed.1), calls=%async_computation.3 | async-start | bytes 2097152 | tf_op jit(solution)/shard_map/all_to_all | solution.py:255
  174.9 37.0 %copy-start.7 = (bf16[64,32]{1,0:T(8,128)(2,1)S(1)}, bf16[64,32]{1,0:T(8,128)(2,1)}, u32[]{:S(2)}) copy-start(bf16[64,32]{1,0:T(8,128)(2,1)} %copy-done.6) | copy-start | bytes 12292
  (2 other events, 1.6 us)
Sparse Core Ops, SparseCore 0:
  46.2 64.6 all-gather.1
  128.0 63.6 reduce-scatter.1

commit v9 on v8

--- a/solution.py
+++ b/solution.py
@@ -285,7 +285,7 @@
         copy.start()
     for copy in loads[1:]:
         copy.start()
-    block = 1024
+    block = 2560
     for k, (x, out, at, n) in enumerate(parts):
         loads[k].wait()
         for half in range(2):
@@ -418,12 +418,15 @@
     paired = pair_rows(key_states, value_state_rows)
     incoming = trade(outgoing.reshape(experts, capacity, width)).reshape(-1, width)
     below, above = [paired], [paired]
-    for _ in range(3):
+    for _ in range(2):
         below.append(up_z(below[-1]))
         above.append(down_z(above[-1]))
-    incoming, below[3], above[3] = lax.optimization_barrier(
-        (incoming, below[3], above[3])
-    )
+    incoming, below[2], above[2] = lax.optimization_barrier(
+        (incoming, below[2], above[2])
+    )
+    for _ in range(1):
+        below.append(up_z(below[-1]))
+        above.append(down_z(above[-1]))
     seen = trade(pack_own(below[0], queries))
     packed, state = exchange_rows(below, above, block_lists)
     attention, moe_out = route_experts(

time: 221 us -> 221 us (level)
    ppermute x4, waiting for transfers between devices: 4.99 us -> 21.3 us  [up_z(): return lax.ppermute(v, 'ctx', ring(1))]
    all_to_all x3, waiting for transfers between devices: 23.3 us -> 15 us  [trade(): return lax.all_to_all(v, 'exp', split_axis=0, concat_axis=0, tiled=True)]
    ppermute x4, waiting for transfers between devices: 14.1 us -> 8.09 us  [down_z(): return lax.ppermute(v, 'ctx', ring(-1))]
    ppermute x4, starting transfers between devices: 13 us -> 16.1 us  [down_z(): return lax.ppermute(v, 'ctx', ring(-1))]
  transfers between devices with their start and end apart: 17 -> 17, of which waited for: 10 -> 9; matrix products, arithmetic and copies ran while one was open for 1% -> 1% of each run, Pallas kernels for 7% -> 6%
where the time goes in v9:
time: 221 us; the launch traced here: 220 us
  waiting for transfers between devices  93.2 us (42%)
  starting transfers between devices  39.3 us (18%)
  blocking collectives  34.1 us (15%)
  Pallas kernels  30.6 us (14%)
  between operations  14.2 us (6%)
  local copies, waits for them, and re-layouts  7.05 us (3%)
    all_to_all x2, blocking collectives, trade(): return lax.all_to_all(v, 'exp', split_axis=0, concat_axis=0, tiled=True)  34.1 us
    all_gather x1, waiting for transfers between devices, route_experts(): lax.all_gather(incoming, 'ctx', axis=0, tiled=True, axis_index_groups=RINGS)  31.5 us
    all_to_all x3, starting transfers between devices, trade(): return lax.all_to_all(v, 'exp', split_axis=0, concat_axis=0, tiled=True)  22 us
    ppermute x4, waiting for transfers between devices, up_z(): return lax.ppermute(v, 'ctx', ring(1))  21.3 us
    ppermute x4, starting transfers between devices, down_z(): return lax.ppermute(v, 'ctx', ring(-1))  16.1 us
    pallas_call x1, Pallas kernels, expert_rows(): pl.pallas_call(lambda *refs: ffn_kernel(len(xs), refs), in_specs=[far] *...  15.9 us
    reduce_scatter x1, waiting for transfers between devices, route_experts(): lax.psum_scatter(partial, 'ctx', scatter_dimension=0, tiled=True, axis_in...  15.8 us
    all_to_all x3, waiting for transfers between devices, trade(): return lax.all_to_all(v, 'exp', split_axis=0, concat_axis=0, tiled=True)  15 us
  transfers between devices with their start and end apart: 17, of which 9 were waited for; matrix products, arithmetic and copies ran while one was open for 1% of the time, Pallas kernels for 6%

profile of v9, /device:TPU:2, one launch (start us, length us, event | category | flops | bytes accessed | tf_op | source)
XLA Modules:
  0.0 219.8 jit_solution(4936145290123188709)
XLA Ops:
  10.6 1.1 reshape.177
  11.6 7.5 %all-to-all-start = ((bf16[16,4,5120]{2,1,0:T(4,128)(2,1)}), bf16[16,4,5120]{2,1,0:T(4,128)(2,1)S(1)}, u32[]{:S(2)}, u32[]{:S(2)}) async-start(bf16[16,4,5120]{2,1,0:T(4,128)(2,1)} %reshape.177), calls=%async_computation | async-start | bytes 1310720 | tf_op jit(solution)/shard_map/all_to_all | solution.py:255
  19.3 5.9 %collective-permute-start.2 = (bf16[2,64,1024]{2,1,0:T(8,128)(2,1)S(1)}, bf16[2,64,1024]{2,1,0:T(8,128)(2,1)S(1)}, u32[]{:S(2)}, u32[]{:S(2)}) collective-permute-start(bf16[2,64,1024]{2,1,0:T(8,128)(2,1)S(1)} %pair_rows.1.own.refs_0_), channel_id=1, source_target_pairs={{0,224},{16,240},{32,0},{48,16},{64,32},{80,48},{96,64},{112,80},{... | collective-permute-start | bytes 786440 | tf_op jit(solution)/shard_map/ppermute | solution.py:60
  25.2 5.0 %collective-permute-done.2.refs_8_ = bf16[2,64,1024]{2,1,0:T(8,128)(2,1)S(1)} collective-permute-done((bf16[2,64,1024]{2,1,0:T(8,128)(2,1)S(1)}, bf16[2,64,1024]{2,1,0:T(8,128)(2,1)S(1)}, u32[]{:S(2)}, u32[]{:S(2)}) %collective-permute-start.2) | collective-permute-done | bytes 262176 | tf_op jit(solution)/shard_map/ppermute | solution.py:60
  30.2 3.7 %collective-permute-start.3 = (bf16[2,64,1024]{2,1,0:T(8,128)(2,1)S(1)}, bf16[2,64,1024]{2,1,0:T(8,128)(2,1)S(1)}, u32[]{:S(2)}, u32[]{:S(2)}) collective-permute-start(bf16[2,64,1024]{2,1,0:T(8,128)(2,1)S(1)} %collective-permute-done.2.refs_8_), channel_id=1, source_target_pairs={{0,224},{16,240},{32,0},{48,16},{64,32},{80,48},{96,64},{112,80},{... | collective-permute-start | bytes 786440 | tf_op jit(solution)/shard_map/ppermute | solution.py:60
  34.9 3.1 %collective-permute-done.3.refs_7_ = bf16[2,64,1024]{2,1,0:T(8,128)(2,1)S(1)} collective-permute-done((bf16[2,64,1024]{2,1,0:T(8,128)(2,1)S(1)}, bf16[2,64,1024]{2,1,0:T(8,128)(2,1)S(1)}, u32[]{:S(2)}, u32[]{:S(2)}) %collective-permute-start.3) | collective-permute-done | bytes 262176 | tf_op jit(solution)/shard_map/ppermute | solution.py:60
  38.0 3.5 %collective-permute-done.1.refs_2_ = bf16[2,64,1024]{2,1,0:T(8,128)(2,1)S(1)} collective-permute-done((bf16[2,64,1024]{2,1,0:T(8,128)(2,1)S(1)}, bf16[2,64,1024]{2,1,0:T(8,128)(2,1)S(1)}, u32[]{:S(2)}, u32[]{:S(2)}) %collective-permute-start.1) | collective-permute-done | bytes 262176 | tf_op jit(solution)/shard_map/ppermute | solution.py:56
  42.2 1.4 pack_own.1
  43.6 7.2 %all-to-all-start.1 = ((bf16[16,416,128]{2,1,0:T(8,128)(2,1)}), bf16[16,416,128]{2,1,0:T(8,128)(2,1)S(1)}, u32[]{:S(2)}, u32[]{:S(2)}) async-start(bf16[16,416,128]{2,1,0:T(8,128)(2,1)} %pack_own.1), calls=%async_computation.1 | async-start | bytes 3407872 | tf_op jit(solution)/shard_map/all_to_all | solution.py:255
  51.0 3.2 %collective-permute-start.6 = (bf16[2,64,1024]{2,1,0:T(8,128)(2,1)S(1)}, bf16[2,64,1024]{2,1,0:T(8,128)(2,1)S(1)}, u32[]{:S(2)}, u32[]{:S(2)}) collective-permute-start(bf16[2,64,1024]{2,1,0:T(8,128)(2,1)S(1)} %collective-permute-done.3.refs_7_), channel_id=1, source_target_pairs={{0,224},{16,240},{32,0},{48,16},{64,32},{80,48},{96,64},{112,80},{... | collective-permute-start | bytes 786440 | tf_op jit(solution)/shard_map/ppermute | solution.py:60
  55.0 11.5 %collective-permute-done.4.refs_3_ = bf16[2,64,1024]{2,1,0:T(8,128)(2,1)S(1)} collective-permute-done((bf16[2,64,1024]{2,1,0:T(8,128)(2,1)S(1)}, bf16[2,64,1024]{2,1,0:T(8,128)(2,1)S(1)}, u32[]{:S(2)}, u32[]{:S(2)}) %collective-permute-start.4) | collective-permute-done | bytes 262176 | tf_op jit(solution)/shard_map/ppermute | solution.py:56
  66.6 3.3 %collective-permute-start.7 = (bf16[1,64,1024]{2,1,0:T(8,128)(2,1)S(1)}, bf16[1,64,1024]{2,1,0:T(8,128)(2,1)S(1)}, u32[]{:S(2)}, u32[]{:S(2)}) collective-permute-start(bf16[1,64,1024]{2,1,0:T(8,128)(2,1)S(1)} %slice.26), channel_id=1, source_target_pairs={{0,224},{16,240},{32,0},{48,16},{64,32},{80,48},{96,64},{112,80},{... | collective-permute-start | bytes 393224 | tf_op jit(solution)/shard_map/ppermute | solution.py:60
  69.9 6.3 %collective-permute-done.5.refs_4_ = bf16[1,64,1024]{2,1,0:T(8,128)(2,1)S(1)} collective-permute-done((bf16[1,64,1024]{2,1,0:T(8,128)(2,1)S(1)}, bf16[1,64,1024]{2,1,0:T(8,128)(2,1)S(1)}, u32[]{:S(2)}, u32[]{:S(2)}) %collective-permute-start.5) | collective-permute-done | bytes 131104 | tf_op jit(solution)/shard_map/ppermute | solution.py:56
  77.3 1.4 collective-permute-done.8.swapped
  78.7 1.7 pack_listed.1
  80.4 31.5 %all-gather.2.cloned.1.call-done.refs_0_ = bf16[512,5120]{1,0:T(8,128)(2,1)} async-done(((bf16[64,5120]{1,0:T(8,128)(2,1)}), bf16[512,5120]{1,0:T(8,128)(2,1)}) %all-gather.2.cloned.1.call-update) | async-done | bytes 5242896 | tf_op jit(solution)/shard_map/all_gather | solution.py:380
  112.0 15.9 %expert_rows.1 = bf16[512,5120]{1,0:T(8,128)(2,1)} custom-call(bf16[512,5120]{1,0:T(8,128)(2,1)} %all-gather.2.cloned.1.call-done.refs_0_, bf16[5120,256]{1,0:T(8,128)(2,1)} %bitcast.21, bf16[5120,256]{1,0:T(8,128)(2,1)} %bitcast.23, bf16[256,5120]{1,0:T(8,128)(2,1)} %bitcast.25, bf16[5120,256]{1,0:T(8,128)(2,1)} %collective-permute-done.9.refs_4_, ...), custom_call_target="tpu_custom_call" | custom-call | flops 8053063680 | bytes 26214400 | tf_op jit(solution)/shard_map/expert_rows/pallas_call | solution.py:322
  127.9 7.3 %all-to-all-start.2 = ((bf16[16,256,128]{2,1,0:T(8,128)(2,1)}), bf16[16,256,128]{2,1,0:T(8,128)(2,1)S(1)}, u32[]{:S(2)}, u32[]{:S(2)}) async-start(bf16[16,256,128]{2,1,0:T(8,128)(2,1)} %pack_listed.1), calls=%async_computation.3 | async-start | bytes 2097152 | tf_op jit(solution)/shard_map/all_to_all | solution.py:255
  135.3 15.0 %all-to-all-done.2.listed = bf16[16,256,128]{2,1,0:T(8,128)(2,1)S(1)} async-done(((bf16[16,256,128]{2,1,0:T(8,128)(2,1)}), bf16[16,256,128]{2,1,0:T(8,128)(2,1)S(1)}, u32[]{:S(2)}, u32[]{:S(2)}) %all-to-all-start.2) | async-done | bytes 1048608 | tf_op jit(solution)/shard_map/all_to_all | solution.py:255
  150.3 9.0 %attend.1 = bf16[16,160,128]{2,1,0:T(8,128)(2,1)S(1)} custom-call(s32[3]{0:T(128)S(1)} %pad_add_fusion.table, bf16[16,416,128]{2,1,0:T(8,128)(2,1)S(1)} %all-to-all-done.1.seen, bf16[16,256,128]{2,1,0:T(8,128)(2,1)S(1)} %all-to-all-done.2.listed), custom_call_target="tpu_custom_call" | custom-call | flops 2200000000 | bytes 4194304 | tf_op jit(solution)/shard_map/attend/pallas_call | solution.py:212
  159.3 15.6 %all_to_all.25.back = bf16[16,160,128]{2,1,0:T(8,128)(2,1)S(1)} all-to-all(bf16[16,160,128]{2,1,0:T(8,128)(2,1)S(1)} %attend.1), channel_id=1, replica_groups=mesh['ctx'=16,'exp'=16] {'exp'}, dimensions={0} | all-to-all | bytes 1310720 | tf_op jit(solution)/shard_map/all_to_all | solution.py:255
  175.9 15.8 %reduce-scatter.2.cloned.1.call-done = bf16[64,5120]{1,0:T(8,128)(2,1)} async-done(((bf16[512,5120]{1,0:T(8,128)(2,1)}), bf16[64,5120]{1,0:T(8,128)(2,1)}) %reduce-scatter.2.cloned.1.call-update) | async-done | bytes 655376 | tf_op jit(solution)/shard_map/reduce_scatter | solution.py:386
  191.7 1.6 reshape.179
  193.3 18.5 %all_to_all.26 = bf16[16,4,5120]{2,1,0:T(4,128)(2,1)S(1)} all-to-all(bf16[16,4,5120]{2,1,0:T(4,128)(2,1)S(1)} %reshape.179), channel_id=1, replica_groups=mesh['ctx'=16,'exp'=16] {'exp'}, dimensions={0} | all-to-all | bytes 1310720 | tf_op jit(solution)/shard_map/all_to_all | solution.py:255
  (55 shorter events, 9.4 us)
Async XLA Ops:
  7.2 47.2 %copy-start = (s32[32]{0:T(128)S(1)}, s32[32]{0:T(128)}, u32[]{:S(2)}) copy-start(s32[32]{0:T(128)} %param.13) | copy-start | bytes 388
  7.2 1.0 copy-start.2
  9.7 9.4 %copy-start.4 = (bf16[2,64,512]{2,1,0:T(8,128)(2,1)S(1)}, bf16[2,64,512]{2,1,0:T(8,128)(2,1)}, u32[]{:S(2)}) copy-start(bf16[2,64,512]{2,1,0:T(8,128)(2,1)} %keys.1) | copy-start | bytes 393220
  9.7 9.4 %copy-start.5 = (bf16[2,64,512]{2,1,0:T(8,128)(2,1)S(1)}, bf16[2,64,512]{2,1,0:T(8,128)(2,1)}, u32[]{:S(2)}) copy-start(bf16[2,64,512]{2,1,0:T(8,128)(2,1)} %values.1) | copy-start | bytes 393220
  10.5 8.6 %copy-start.6 = (bf16[64,32]{1,0:T(8,128)(2,1)}, bf16[64,32]{1,0:T(8,128)(2,1)S(1)}, u32[]{:S(2)}) copy-start(bf16[64,32]{1,0:T(8,128)(2,1)S(1)} %get-tuple-element.24) | copy-start | bytes 12292
  10.5 31.7 %copy-start.1 = (bf16[2,64,2560]{2,1,0:T(8,128)(2,1)S(1)}, bf16[2,64,2560]{2,1,0:T(8,128)(2,1)}, u32[]{:S(2)}) copy-start(bf16[2,64,2560]{2,1,0:T(8,128)(2,1)} %queries.1) | copy-start | bytes 1966084
  11.6 22.3 %all-to-all-start = ((bf16[16,4,5120]{2,1,0:T(4,128)(2,1)}), bf16[16,4,5120]{2,1,0:T(4,128)(2,1)S(1)}, u32[]{:S(2)}, u32[]{:S(2)}) async-start(bf16[16,4,5120]{2,1,0:T(4,128)(2,1)} %reshape.177), calls=%async_computation | async-start | bytes 1310720 | tf_op jit(solution)/shard_map/all_to_all | solution.py:255
  19.1 92.8 %all-gather.2.cloned.1.call-start = ((), (), s32[]{:S(2)}) async-start(), calls=%async_computation.6 | async-start | bytes 5898240 | tf_op jit(solution)/shard_map/all_gather | solution.py:380
  19.3 10.9 %collective-permute-start.2 = (bf16[2,64,1024]{2,1,0:T(8,128)(2,1)S(1)}, bf16[2,64,1024]{2,1,0:T(8,128)(2,1)S(1)}, u32[]{:S(2)}, u32[]{:S(2)}) collective-permute-start(bf16[2,64,1024]{2,1,0:T(8,128)(2,1)S(1)} %pair_rows.1.own.refs_0_), channel_id=1, source_target_pairs={{0,224},{16,240},{32,0},{48,16},{64,32},{80,48},{96,64},{112,80},{... | collective-permute-start | bytes 786440 | tf_op jit(solution)/shard_map/ppermute | solution.py:60
  25.2 8.7 %collective-permute-start = (bf16[2,64,1024]{2,1,0:T(8,128)(2,1)S(1)}, bf16[2,64,1024]{2,1,0:T(8,128)(2,1)S(1)}, u32[]{:S(2)}, u32[]{:S(2)}) collective-permute-start(bf16[2,64,1024]{2,1,0:T(8,128)(2,1)S(1)} %pair_rows.1.own.refs_0_), channel_id=1, source_target_pairs={{0,32},{16,48},{32,64},{48,80},{64,96},{80,112},{96,128},{112,144}... | collective-permute-start | bytes 786440 | tf_op jit(solution)/shard_map/ppermute | solution.py:56
  30.2 7.8 %collective-permute-start.3 = (bf16[2,64,1024]{2,1,0:T(8,128)(2,1)S(1)}, bf16[2,64,1024]{2,1,0:T(8,128)(2,1)S(1)}, u32[]{:S(2)}, u32[]{:S(2)}) collective-permute-start(bf16[2,64,1024]{2,1,0:T(8,128)(2,1)S(1)} %collective-permute-done.2.refs_8_), channel_id=1, source_target_pairs={{0,224},{16,240},{32,0},{48,16},{64,32},{80,48},{96,64},{112,80},{... | collective-permute-start | bytes 786440 | tf_op jit(solution)/shard_map/ppermute | solution.py:60
  33.9 7.6 %collective-permute-start.1 = (bf16[2,64,1024]{2,1,0:T(8,128)(2,1)S(1)}, bf16[2,64,1024]{2,1,0:T(8,128)(2,1)S(1)}, u32[]{:S(2)}, u32[]{:S(2)}) collective-permute-start(bf16[2,64,1024]{2,1,0:T(8,128)(2,1)S(1)} %collective-permute-done.refs_1_), channel_id=1, source_target_pairs={{0,32},{16,48},{32,64},{48,80},{64,96},{80,112},{96,128},{112,144}... | collective-permute-start | bytes 786440 | tf_op jit(solution)/shard_map/ppermute | solution.py:56
  41.5 70.4 %collective-permute-start.9 = (bf16[5120,256]{1,0:T(8,128)(2,1)}, bf16[5120,256]{1,0:T(8,128)(2,1)}, u32[]{:S(2)}, u32[]{:S(2)}) collective-permute-start(bf16[5120,256]{1,0:T(8,128)(2,1)} %bitcast.20), channel_id=1, source_target_pairs={{0,16},{16,0},{32,48},{48,32},{64,80},{80,64},{96,112},{112,96},{1... | collective-permute-start | bytes 7864328 | tf_op jit(solution)/shard_map/ppermute | solution.py:414
  41.6 70.3 %collective-permute-start.10 = (bf16[5120,256]{1,0:T(8,128)(2,1)}, bf16[5120,256]{1,0:T(8,128)(2,1)}, u32[]{:S(2)}, u32[]{:S(2)}) collective-permute-start(bf16[5120,256]{1,0:T(8,128)(2,1)} %bitcast.22), channel_id=1, source_target_pairs={{0,16},{16,0},{32,48},{48,32},{64,80},{80,64},{96,112},{112,96},{1... | collective-permute-start | bytes 7864328 | tf_op jit(solution)/shard_map/ppermute | solution.py:414
  42.1 69.9 %collective-permute-start.11 = (bf16[256,5120]{1,0:T(8,128)(2,1)}, bf16[256,5120]{1,0:T(8,128)(2,1)}, u32[]{:S(2)}, u32[]{:S(2)}) collective-permute-start(bf16[256,5120]{1,0:T(8,128)(2,1)} %bitcast.24), channel_id=1, source_target_pairs={{0,16},{16,0},{32,48},{48,32},{64,80},{80,64},{96,112},{112,96},{1... | collective-permute-start | bytes 7864328 | tf_op jit(solution)/shard_map/ppermute | solution.py:414
  43.6 36.8 %all-to-all-start.1 = ((bf16[16,416,128]{2,1,0:T(8,128)(2,1)}), bf16[16,416,128]{2,1,0:T(8,128)(2,1)S(1)}, u32[]{:S(2)}, u32[]{:S(2)}) async-start(bf16[16,416,128]{2,1,0:T(8,128)(2,1)} %pack_own.1), calls=%async_computation.1 | async-start | bytes 3407872 | tf_op jit(solution)/shard_map/all_to_all | solution.py:255
  50.9 140.8 %reduce-scatter.2.cloned.1.call-start = ((), (), s32[]{:S(2)}) async-start(), calls=%async_computation.7 | async-start | bytes 5898240 | tf_op jit(solution)/shard_map/reduce_scatter | solution.py:386
  50.9 15.6 %collective-permute-start.4 = (bf16[2,64,1024]{2,1,0:T(8,128)(2,1)S(1)}, bf16[2,64,1024]{2,1,0:T(8,128)(2,1)S(1)}, u32[]{:S(2)}, u32[]{:S(2)}) collective-permute-start(bf16[2,64,1024]{2,1,0:T(8,128)(2,1)S(1)} %collective-permute-done.1.refs_2_), channel_id=1, source_target_pairs={{0,32},{16,48},{32,64},{48,80},{64,96},{80,112},{96,128},{112,144}... | collective-permute-start | bytes 786440 | tf_op jit(solution)/shard_map/ppermute | solution.py:56
  51.0 15.6 %collective-permute-start.6 = (bf16[2,64,1024]{2,1,0:T(8,128)(2,1)S(1)}, bf16[2,64,1024]{2,1,0:T(8,128)(2,1)S(1)}, u32[]{:S(2)}, u32[]{:S(2)}) collective-permute-start(bf16[2,64,1024]{2,1,0:T(8,128)(2,1)S(1)} %collective-permute-done.3.refs_7_), channel_id=1, source_target_pairs={{0,224},{16,240},{32,0},{48,16},{64,32},{80,48},{96,64},{112,80},{... | collective-permute-start | bytes 786440 | tf_op jit(solution)/shard_map/ppermute | solution.py:60
  66.5 9.7 %collective-permute-start.5 = (bf16[1,64,1024]{2,1,0:T(8,128)(2,1)S(1)}, bf16[1,64,1024]{2,1,0:T(8,128)(2,1)S(1)}, u32[]{:S(2)}, u32[]{:S(2)}) collective-permute-start(bf16[1,64,1024]{2,1,0:T(8,128)(2,1)S(1)} %slice.25), channel_id=1, source_target_pairs={{0,32},{16,48},{32,64},{48,80},{64,96},{80,112},{96,128},{112,144}... | collective-permute-start | bytes 393224 | tf_op jit(solution)/shard_map/ppermute | solution.py:56
  66.6 9.6 %collective-permute-start.7 = (bf16[1,64,1024]{2,1,0:T(8,128)(2,1)S(1)}, bf16[1,64,1024]{2,1,0:T(8,128)(2,1)S(1)}, u32[]{:S(2)}, u32[]{:S(2)}) collective-permute-start(bf16[1,64,1024]{2,1,0:T(8,128)(2,1)S(1)} %slice.26), channel_id=1, source_target_pairs={{0,224},{16,240},{32,0},{48,16},{64,32},{80,48},{96,64},{112,80},{... | collective-permute-start | bytes 393224 | tf_op jit(solution)/shard_map/ppermute | solution.py:60
  76.9 1.8 collective-permute-start.8
  127.9 22.4 %all-to-all-start.2 = ((bf16[16,256,128]{2,1,0:T(8,128)(2,1)}), bf16[16,256,128]{2,1,0:T(8,128)(2,1)S(1)}, u32[]{:S(2)}, u32[]{:S(2)}) async-start(bf16[16,256,128]{2,1,0:T(8,128)(2,1)} %pack_listed.1), calls=%async_computation.3 | async-start | bytes 2097152 | tf_op jit(solution)/shard_map/all_to_all | solution.py:255
  174.9 37.0 %copy-start.7 = (bf16[64,32]{1,0:T(8,128)(2,1)S(1)}, bf16[64,32]{1,0:T(8,128)(2,1)}, u32[]{:S(2)}) copy-start(bf16[64,32]{1,0:T(8,128)(2,1)} %copy-done.6) | copy-start | bytes 12292
  (2 other events, 1.6 us)
Sparse Core Ops, SparseCore 0:
  41.6 70.2 all-gather.1
  128.1 63.5 reduce-scatter.1
